TPU v7x, 32 devices: a whole 2x2x4 slice. The times are simulated.
32 devices in a mesh: img: 4 (over y, x), tile: 8 (over z, core).
Axes of the slice: x: 2, y: 2, z: 4, core: 2. Of those that a mesh axis runs over, the one named last changes fastest.
Arguments:
- images: bfloat16 [8, 2, 256, 1024], P('img', None, 'tile'), may hold values from -6 to 6
- nucleus: int32 [8], P('img'), may hold values 0 or 1
- target_flow: int32 [8, 2, 256, 1024], P('img', None, 'tile'), may hold values from -4 to 4
- cell_label: int32 [8, 256, 1024], P('img', 'tile'), may hold values 0 or 1
- step_count: int32 [1], replicated, may hold values from 1 to 20
- conv1_weight: float32 [3, 3, 2, 32], replicated, may hold values from -1.5 to 1.5
- conv1_momentum: float32 [3, 3, 2, 32], replicated, may hold values from -6 to 6
- conv1_average: float32 [3, 3, 2, 32], replicated, may hold values from -1.5 to 1.5
- conv2_weight: float32 [3, 3, 32, 64], replicated, may hold values from -0.375 to 0.375
- conv2_momentum: float32 [3, 3, 32, 64], replicated, may hold values from -6 to 6
- conv2_average: float32 [3, 3, 32, 64], replicated, may hold values from -0.375 to 0.375
- conv3_weight: float32 [3, 3, 64, 32], replicated, may hold values from -0.25 to 0.25
- conv3_momentum: float32 [3, 3, 64, 32], replicated, may hold values from -6 to 6
- conv3_average: float32 [3, 3, 64, 32], replicated, may hold values from -0.25 to 0.25
- style_weight: float32 [64, 32], replicated, may hold values from -0.75 to 0.75
- style_momentum: float32 [64, 32], replicated, may hold values from -6 to 6
- style_average: float32 [64, 32], replicated, may hold values from -0.75 to 0.75
- head_weight: float32 [32, 3], replicated, may hold values from -1 to 1
- head_momentum: float32 [32, 3], replicated, may hold values from -6 to 6
- head_average: float32 [32, 3], replicated, may hold values from -1 to 1
- biases: float32 [163], replicated, may hold values from -1.8 to 1.8
- bias_momentum: float32 [163], replicated, may hold values from -6 to 6
- bias_average: float32 [163], replicated, may hold values from -1.8 to 1.8
Outputs:
- loss: float32 [1], replicated
- conv1_weight_out: float32 [3, 3, 2, 32], replicated
- conv1_momentum_out: float32 [3, 3, 2, 32], replicated
- conv1_average_out: float32 [3, 3, 2, 32], replicated
- conv2_weight_out: float32 [3, 3, 32, 64], replicated
- conv2_momentum_out: float32 [3, 3, 32, 64], replicated
- conv2_average_out: float32 [3, 3, 32, 64], replicated
- conv3_weight_out: float32 [3, 3, 64, 32], replicated
- conv3_momentum_out: float32 [3, 3, 64, 32], replicated
- conv3_average_out: float32 [3, 3, 64, 32], replicated
- style_weight_out: float32 [64, 32], replicated
- style_momentum_out: float32 [64, 32], replicated
- style_average_out: float32 [64, 32], replicated
- head_weight_out: float32 [32, 3], replicated
- head_momentum_out: float32 [32, 3], replicated
- head_average_out: float32 [32, 3], replicated
- biases_out: float32 [163], replicated
- bias_momentum_out: float32 [163], replicated
- bias_average_out: float32 [163], replicated
All inputs are finite; a program needn't handle non-finite values. No bound on the sum of `nucleus` or of `cell_label` on one device may be relied on, other than what follows from the above.
Results may differ from a plain program's by a relative error of at most 0.00075.
The roundings to bfloat16 on the way count: a program that leaves them out, or rounds other values in their place, can miss the bound.
Values may be sent and summed in bfloat16 or wider, within the bound.
A program may use at most 384 MiB of HBM per device.

v0:
```python
import math

import jax
import jax.numpy as jnp
from jax import lax
from jax.sharding import PartitionSpec as P

CH_ONE = 32
CH_TWO = 64
OUT_CH = 3


momentum_rate = 0.9
learn_rate = 0.02
decay_rate = 0.0001
norm_eps = 1e-05
highest = lax.Precision.HIGHEST


def padded_2(block, sides, width):
    for axis, dim in sides:
        count = lax.axis_size(axis)
        forward = [(i, i + 1) for i in range(count - 1)]
        backward = [(target, source) for source, target in forward]
        low = lax.ppermute(
            lax.slice_in_dim(block, block.shape[dim] - width, None, axis=dim), axis, forward
        )
        high = lax.ppermute(lax.slice_in_dim(block, 0, width, axis=dim), axis, backward)
        block = jnp.concatenate([low, block, high], axis=dim)
    return block


def as_sent(shard):

    def short(part):
        return part.astype(jnp.bfloat16) if part.dtype == jnp.float32 else part

    return jax.tree.map(short, shard)


def widen(padded):
    return jnp.pad(padded, ((0, 0), (0, 0), (0, 0), (1, 1)))


def conv_rows(padded, kernel):
    height = padded.shape[2] - 2
    breadth = padded.shape[3]
    widened = widen(padded)
    result = 0.0
    for offset_row in range(3):
        for offset_col in range(3):
            window = widened[
                :, :, offset_row : offset_row + height, offset_col : offset_col + breadth
            ]
            result = result + jnp.einsum(
                "cirw,io->corw",
                window,
                kernel[offset_row, offset_col],
                preferred_element_type=jnp.float32,
            )
    return result


def conv_weight_grad(padded, grad_out):
    height = grad_out.shape[2]
    breadth = grad_out.shape[3]
    widened = widen(padded)
    rows_list = []
    for offset_row in range(3):
        cols_list = []
        for offset_col in range(3):
            window = widened[
                :, :, offset_row : offset_row + height, offset_col : offset_col + breadth
            ]
            cols_list.append(
                jnp.einsum("cirw,corw->io", window, grad_out, preferred_element_type=jnp.float32)
            )
        rows_list.append(jnp.stack(cols_list))
    return jnp.stack(rows_list)


def input_grad_padded(grad_out, kernel):
    result = 0.0
    for offset_row in range(3):
        for offset_col in range(3):
            partial_term = jnp.einsum(
                "corw,io->cirw",
                grad_out,
                kernel[offset_row, offset_col],
                preferred_element_type=jnp.float32,
            )
            result = result + jnp.pad(
                partial_term,
                ((0, 0), (0, 0), (offset_row, 2 - offset_row), (offset_col, 2 - offset_col)),
            )
    return result[:, :, :, 1:-1]


def pool_sum(values):
    in_shape = values.shape
    return jnp.sum(
        values.reshape(in_shape[0], in_shape[1], in_shape[2] // 2, 2, in_shape[3] // 2, 2),
        axis=(3, 5),
        dtype=jnp.float32,
    )


def upsample(values):
    return jnp.repeat(jnp.repeat(values, 2, axis=2), 2, axis=3)


def row_diff_padded(padded):
    return 0.5 * (padded[:, 2:] - padded[:, :-2])


def col_diff(values):
    padded = jnp.pad(values, ((0, 0), (0, 0), (1, 1)))
    return 0.5 * (padded[:, :, 2:] - padded[:, :, :-2])


def edge_rows(padded):
    return jnp.concatenate([padded[:, :, :1], padded[:, :, -1:]], axis=2)


def fold_rims(padded, arrived):
    inner = padded[:, :, 1:-1]
    inner = inner.at[:, :, 0].add(arrived[:, :, 0])
    return inner.at[:, :, -1].add(arrived[:, :, 3])


def masked(grad_in, before):
    return jnp.where(before > 0, grad_in, jnp.zeros_like(grad_in))


def nesterov(weight, gradient, momentum, average, count):
    decayed = gradient + decay_rate * weight
    momentum_new = momentum_rate * momentum + decayed
    weight_new = weight - learn_rate * (decayed + momentum_rate * momentum_new)
    average_new = average + (weight_new - average) / (count + 1.0)
    return (weight_new, momentum_new, average_new)


def on_device(
    images,
    nucleus,
    target_flow,
    cell_label,
    step_count,
    conv1_weight,
    conv1_momentum,
    conv1_average,
    conv2_weight,
    conv2_momentum,
    conv2_average,
    conv3_weight,
    conv3_momentum,
    conv3_average,
    style_weight,
    style_momentum,
    style_average,
    head_weight,
    head_momentum,
    head_average,
    biases,
    bias_momentum,
    bias_average,
):
    kernel_one = conv1_weight.astype(jnp.bfloat16)
    kernel_two = conv2_weight.astype(jnp.bfloat16)
    kernel_three = conv3_weight.astype(jnp.bfloat16)
    kernel_head = head_weight.astype(jnp.bfloat16)
    bias_one = biases[0:CH_ONE][None, :, None, None]
    bias_two = biases[CH_ONE : CH_ONE + CH_TWO][None, :, None, None]
    bias_three = biases[CH_ONE + CH_TWO : 2 * CH_ONE + CH_TWO][None, :, None, None]
    bias_style = biases[2 * CH_ONE + CH_TWO : 3 * CH_ONE + CH_TWO]
    bias_head = biases[3 * CH_ONE + CH_TWO : 3 * CH_ONE + CH_TWO + OUT_CH][None, :, None, None]
    pixel_count = (
        lax.axis_size("img")
        * lax.axis_size("tile")
        * images.shape[0]
        * images.shape[2]
        * images.shape[3]
    )
    grad_scale = 1.0 / math.sqrt(pixel_count)
    coarse_count = lax.axis_size("tile") * (images.shape[2] // 2) * (images.shape[3] // 2)
    nucleus_gate = nucleus.astype(jnp.bfloat16)[:, None, None]
    inputs = jnp.stack([images[:, 0], images[:, 1] * nucleus_gate], axis=1)
    input_pad = padded_2(inputs, (("tile", 2),), 1)
    pre_one = conv_rows(input_pad, kernel_one) + bias_one
    hidden_one = jnp.maximum(pre_one, 0.0).astype(jnp.bfloat16)
    pooled = (0.25 * pool_sum(hidden_one)).astype(jnp.bfloat16)
    pooled_pad = padded_2(pooled, (("tile", 2),), 1)
    pre_two = conv_rows(pooled_pad, kernel_two) + bias_two
    hidden_two = jnp.maximum(pre_two, 0.0).astype(jnp.bfloat16)
    style_part = jnp.sum(hidden_two, axis=(2, 3), dtype=jnp.float32)
    style_raw = lax.psum(style_part, "tile") / coarse_count
    style_inv = lax.rsqrt(jnp.mean(style_raw * style_raw, axis=1, keepdims=True) + norm_eps)
    style_unit = style_raw * style_inv
    style_vec = jnp.dot(style_unit, style_weight, precision=highest) + bias_style
    two_pad = padded_2(hidden_two, (("tile", 2),), 1)
    upsampled = upsample(two_pad)[:, :, 1:-1]
    pre_three = conv_rows(upsampled, kernel_three) + bias_three + style_vec[:, :, None, None]
    hidden_three = (jnp.maximum(pre_three, 0.0) + hidden_one.astype(jnp.float32)).astype(
        jnp.bfloat16
    )
    output = (
        jnp.einsum("cirw,io->corw", hidden_three, kernel_head, preferred_element_type=jnp.float32)
        + bias_head
    )
    targets = 0.25 * target_flow.astype(jnp.float32)
    labels = cell_label.astype(jnp.float32)
    flow_error = output[:, 0:2] - targets
    error_pad = padded_2(flow_error[:, 0].astype(jnp.bfloat16), (("tile", 1),), 1).astype(
        jnp.float32
    )
    spread = row_diff_padded(error_pad) + col_diff(flow_error[:, 1])
    logits = output[:, 2]
    loss_part = (
        jnp.sum(flow_error * flow_error)
        + jnp.sum(spread * spread)
        + jnp.sum(jax.nn.softplus(logits) - labels * logits)
    )
    spread_grad = 2.0 * grad_scale * spread
    spread_pad = padded_2(as_sent(spread_grad), (("tile", 1),), 1).astype(spread_grad.dtype)
    grad_error = 2.0 * grad_scale * flow_error - jnp.stack(
        [row_diff_padded(spread_pad), col_diff(spread_grad)], axis=1
    )
    grad_logits = grad_scale * (jax.nn.sigmoid(logits) - labels)
    grad_output = jnp.concatenate([grad_error, grad_logits[:, None]], axis=1).astype(jnp.bfloat16)
    grad_head = jnp.einsum(
        "cirw,corw->io", hidden_three, grad_output, preferred_element_type=jnp.float32
    )
    grad_bias_head = jnp.sum(grad_output, axis=(0, 2, 3), dtype=jnp.float32)
    grad_three = jnp.einsum(
        "corw,io->cirw", grad_output, kernel_head, preferred_element_type=jnp.float32
    ).astype(jnp.bfloat16)
    grad_pre_three = masked(grad_three, pre_three)
    grad_kernel_three = conv_weight_grad(upsampled, grad_pre_three)
    style_grad_part = jnp.sum(grad_pre_three, axis=(2, 3), dtype=jnp.float32)
    grad_bias_three = jnp.sum(style_grad_part, axis=0)
    grad_style_weight = jnp.dot(style_unit.T, style_grad_part, precision=highest)
    style_grad = lax.psum(style_grad_part, "tile")
    grad_unit = jnp.dot(style_grad, style_weight.T, precision=highest)
    grad_raw = style_inv * grad_unit - style_inv**3 * style_raw * jnp.mean(
        style_raw * grad_unit, axis=1, keepdims=True
    )
    style_to_map = (grad_raw / coarse_count)[:, :, None, None]
    grad_up = input_grad_padded(grad_pre_three, kernel_three)
    coarse_pad = pool_sum(jnp.pad(grad_up, ((0, 0), (0, 0), (1, 1), (0, 0))))
    arrived = padded_2(edge_rows(coarse_pad).astype(jnp.bfloat16), (("tile", 2),), 1).astype(
        jnp.float32
    )
    grad_coarse = fold_rims(coarse_pad, arrived)
    grad_two = (grad_coarse + style_to_map).astype(jnp.bfloat16)
    grad_pre_two = masked(grad_two, pre_two)
    grad_kernel_two = conv_weight_grad(pooled_pad, grad_pre_two)
    grad_bias_two = jnp.sum(grad_pre_two, axis=(0, 2, 3), dtype=jnp.float32)
    pooled_grad_pad = input_grad_padded(grad_pre_two, kernel_two)
    arrived_two = padded_2(
        edge_rows(pooled_grad_pad).astype(jnp.bfloat16), (("tile", 2),), 1
    ).astype(jnp.float32)
    grad_pooled = fold_rims(pooled_grad_pad, arrived_two).astype(jnp.bfloat16)
    grad_one = (
        0.25 * upsample(grad_pooled).astype(jnp.float32) + grad_three.astype(jnp.float32)
    ).astype(jnp.bfloat16)
    grad_pre_one = masked(grad_one, pre_one)
    grad_kernel_one = conv_weight_grad(input_pad, grad_pre_one)
    grad_bias_one = jnp.sum(grad_pre_one, axis=(0, 2, 3), dtype=jnp.float32)
    grad_bias = jnp.concatenate(
        [grad_bias_one, grad_bias_two, grad_bias_three, grad_bias_three, grad_bias_head]
    )
    summed = lax.psum(
        (
            grad_kernel_one,
            grad_kernel_two,
            grad_kernel_three,
            grad_style_weight,
            grad_head,
            grad_bias,
            loss_part,
        ),
        ("img", "tile"),
    )
    count = step_count[0].astype(jnp.float32)
    olds = (
        (conv1_weight, conv1_momentum, conv1_average),
        (conv2_weight, conv2_momentum, conv2_average),
        (conv3_weight, conv3_momentum, conv3_average),
        (style_weight, style_momentum, style_average),
        (head_weight, head_momentum, head_average),
        (biases, bias_momentum, bias_average),
    )
    results = [(summed[6] / pixel_count).reshape(1)]
    for index_pos in range(6):
        state = olds[index_pos]
        results.extend(nesterov(state[0], summed[index_pos], state[1], state[2], count))
    return tuple(results)


def solution(mesh):
    return jax.shard_map(
        on_device,
        mesh=mesh,
        in_specs=(
            P("img", None, "tile", None),
            P("img"),
            P("img", None, "tile", None),
            P("img", "tile", None),
            P(),
            P(),
            P(),
            P(),
            P(),
            P(),
            P(),
            P(),
            P(),
            P(),
            P(),
            P(),
            P(),
            P(),
            P(),
            P(),
            P(),
            P(),
            P(),
        ),
        out_specs=(
            P(),
            P(),
            P(),
            P(),
            P(),
            P(),
            P(),
            P(),
            P(),
            P(),
            P(),
            P(),
            P(),
            P(),
            P(),
            P(),
            P(),
            P(),
            P(),
        ),
        check_vma=False,
    )
```

profile of v0, /device:TPU:0, one launch (start us, length us, event | category | flops | bytes accessed | tf_op | source)
XLA Modules:
  0.0 964.6 jit_solution(16571981800269271047)
XLA Ops:
  55.1 27.5 %add_add_fusion.1 = f32[2,32,1024,32]{2,3,1,0:T(8,128)} fusion(f32[2,32,1024,32]{2,3,1,0:T(8,128)} %fusion.154, f32[2,32,1024,32]{2,3,1,0:T(8,128)} %fusion.129, f32[2,32,1024,32]{2,3,1,0:T(8,128)} %fusion.132, f32[2,32,1024,32]{2,3,1,0:T(8,128)} %fusion.155, f32[2,32,1024,32]{2,3,1,0:T(8,128)} %fusion.135, f32[2,32,1024,32]{2,3,1,0:T(8,128)} %fusion.138, ...), kind=kOutput, calls=%fused_computation.22 | convolution fusion | flops 27262976 | bytes 75760640 | tf_op jit(solution)/shard_map/cirw,io->corw/dot_general | solution.py:55
  91.2 19.6 %copy.80 = f32[2,32,32,1024]{1,3,2,0:T(8,128)} copy(f32[2,32,32,1024]{3,1,2,0:T(8,128)} %convert_bitcast_fusion) | data formatting | bytes 16777216 | tf_op jit(solution)/shard_map/convert_element_type | solution.py:101
  110.8 33.4 %reduce_sum.117 = f32[2,32,16,512]{1,3,2,0:T(8,128)} reduce(f32[2,32,16,2,512,2]{1,5,4,3,2,0:T(2,128)} %bitcast.584, f32[]{:T(128)} %constant.142.clone.1), dimensions={3,5}, to_apply=%region_0.1 | reduce | flops 1572864 | bytes 10485764 | tf_op jit(solution)/shard_map/reduce_sum | solution.py:101
  177.8 10.6 %add_add_fusion.2 = f32[2,16,512,64]{2,3,1,0:T(8,128)S(1)} fusion(f32[2,16,512,64]{2,3,1,0:T(8,128)} %fusion.93, f32[2,16,512,64]{2,3,1,0:T(8,128)} %fusion.79, f32[2,16,512,64]{2,3,1,0:T(8,128)S(1)} %fusion.82, f32[2,16,512,64]{2,3,1,0:T(8,128)S(1)} %fusion.147, f32[2,16,512,64]{2,3,1,0:T(8,128)} %fusion.85, f32[2,16,512,64]{2,3,1,0:T(8,128)} %fusion.88, ...), kind=kOutput, calls=%fused_computation.63 | convolution fusion | flops 76546048 | bytes 38806016 | tf_op jit(solution)/shard_map/cirw,io->corw/dot_general | solution.py:55
  197.2 16.4 %psum.63 = f32[2,64]{1,0:T(2,128)S(1)} all-reduce(f32[2,64]{1,0:T(2,128)S(1)} %get-tuple-element.107), channel_id=1, replica_groups=mesh['img'=4,'tile'=8] {'tile'}, use_global_device_ids=true, to_apply=%region_2.3 | all-reduce | flops 128 | bytes 1024 | tf_op jit(solution)/shard_map/psum | solution.py:196
  231.5 12.8 %broadcast_in_dim.14 = bf16[2,64,36,512,2]{1,4,3,2,0:T(2,128)(2,1)} broadcast(bf16[2,64,36,512]{1,3,2,0:T(8,128)(2,1)} %bitcast.585), dimensions={0,1,2,3} | broadcast | bytes 14155776 | tf_op jit(solution)/shard_map/broadcast_in_dim | solution.py:109
  244.3 15.6 %slice.597 = bf16[2,64,34,1024]{1,3,2,0:T(8,128)(2,1)} slice(bf16[2,64,36,1024]{1,3,2,0:T(8,128)(2,1)} %bitcast.573), slice={[0:2], [0:64], [1:35], [0:1024]} | slice | bytes 17825792 | tf_op jit(solution)/shard_map/slice | solution.py:201
  259.9 17.0 %copy.156 = bf16[2,64,34,1024]{3,1,2,0:T(8,128)(2,1)} copy(bf16[2,64,34,1024]{1,3,2,0:T(8,128)(2,1)} %slice.597) | data formatting | bytes 17825792
  276.9 9.3 fusion.10
  304.9 14.7 %fusion = f32[2,32,1024,32]{2,3,1,0:T(8,128)} fusion(bf16[2,64,36,1024]{1,3,2,0:T(8,128)(2,1)} %bitcast.574, bf16[3,3,64,32]{2,3,1,0:T(8,128)(2,1)S(1)} %convert_element_type.166), kind=kOutput, calls=%fused_computation.7 | convolution fusion | flops 268435456 | bytes 25174016 | tf_op jit(solution)/shard_map/cirw,io->corw/dot_general | solution.py:55
  319.5 14.7 %fusion.2 = f32[2,32,1024,32]{2,3,1,0:T(8,128)} fusion(bf16[2,64,36,1024]{1,3,2,0:T(8,128)(2,1)} %bitcast.575, bf16[3,3,64,32]{2,3,1,0:T(8,128)(2,1)S(1)} %convert_element_type.166), kind=kOutput, calls=%fused_computation.9 | convolution fusion | flops 268435456 | bytes 25174016 | tf_op jit(solution)/shard_map/cirw,io->corw/dot_general | solution.py:55
  334.2 14.7 %fusion.4 = f32[2,32,1024,32]{2,3,1,0:T(8,128)} fusion(bf16[2,64,36,1024]{1,3,2,0:T(8,128)(2,1)} %bitcast.576, bf16[3,3,64,32]{2,3,1,0:T(8,128)(2,1)S(1)} %convert_element_type.166), kind=kOutput, calls=%fused_computation.11 | convolution fusion | flops 268435456 | bytes 25174016 | tf_op jit(solution)/shard_map/cirw,io->corw/dot_general | solution.py:55
  348.9 31.0 %fusion.7 = (bf16[2,32,32,1024]{3,1,2,0:T(8,128)(2,1)S(1)}, f32[2,32,1024,32]{2,3,1,0:T(8,128)}) fusion(f32[2,32,1024,32]{2,3,1,0:T(8,128)} %add_add_fusion.1, f32[2,32]{1,0:T(2,128)S(1)} %convolution_add_fusion.1, f32[32]{0:T(128)S(1)} %copy-done.65, f32[2,32,1024,32]{2,3,1,0:T(8,128)} %fusion.10, f32[2,32,1024,32]{2,3,1,0:T(8,128)} %fusion, ...), kind=kOutput, calls=%fused_computation.18 | convolution fusion | flops 299892736 | bytes 97003008 | tf_op jit(solution)/shard_map/cirw,io->corw/dot_general | solution.py:55
  525.7 22.7 %pad_add_fusion = f32[2,64,34,1026]{3,1,2,0:T(8,128)} fusion(f32[2,64,32,1024]{3,1,2,0:T(8,128)S(1)} %convolution_bitcast_fusion.6, f32[2,64,32,1024]{3,1,2,0:T(8,128)} %convolution_bitcast_fusion.7, f32[2,64,32,1024]{3,1,2,0:T(8,128)} %convolution_bitcast_fusion.8), kind=kLoop, calls=%fused_computation | loop fusion | flops 8930304 | bytes 68192256 | tf_op jit(solution)/shard_map/add | solution.py:92
  548.4 46.4 %pad_add_fusion.1 = f32[2,64,34,1024]{3,1,2,0:T(8,128)} fusion(f32[2,64,32,1024]{3,1,2,0:T(8,128)} %convolution_bitcast_fusion, f32[2,64,32,1024]{3,1,2,0:T(8,128)} %convolution_bitcast_fusion.1, f32[2,64,32,1024]{3,1,2,0:T(8,128)} %convolution_bitcast_fusion.2, f32[2,64,32,1024]{3,1,2,0:T(8,128)} %convolution_bitcast_fusion.3, ...), kind=kLoop, calls=%fused_computation.1 | loop fusion | flops 26738688 | bytes 136314880 | tf_op jit(solution)/shard_map/add | solution.py:92
  594.8 24.5 %copy.161 = f32[2,64,34,1024]{1,3,2,0:T(8,128)} copy(f32[2,64,34,1024]{3,1,2,0:T(8,128)} %pad_add_fusion.1) | data formatting | bytes 35651584
  619.3 25.7 %pad.120.clone = f32[2,64,36,1024]{1,3,2,0:T(8,128)} pad(f32[2,64,34,1024]{1,3,2,0:T(8,128)} %copy.161, f32[]{:T(128)} %constant.142.clone.1), padding=0_0x0_0x1_1x0_0 | pad | bytes 36700164 | tf_op jit(solution)/shard_map/jit(_pad)/pad | solution.py:249
  645.0 37.3 %reduce_sum.123 = f32[2,64,18,512]{1,3,2,0:T(8,128)} reduce(f32[2,64,18,2,512,2]{1,5,4,3,2,0:T(2,128)} %bitcast.582, f32[]{:T(128)} %constant.142.clone.1), dimensions={3,5}, to_apply=%region_8.9 | reduce | flops 3538944 | bytes 23592964 | tf_op jit(solution)/shard_map/reduce_sum | solution.py:101
  693.6 14.7 %psum.65 = f32[2,32]{1,0:T(2,128)S(1)} all-reduce(f32[2,32]{1,0:T(2,128)S(1)} %copy-done.66), channel_id=1, replica_groups=mesh['img'=4,'tile'=8] {'tile'}, use_global_device_ids=true, to_apply=%region_10.11 | all-reduce | flops 64 | bytes 512 | tf_op jit(solution)/shard_map/psum | solution.py:242
  749.5 14.5 %copy.94 = f32[2,32,32,512]{2,1,3,0:T(8,128)} copy(f32[2,32,32,512]{3,1,2,0:T(8,128)} %bitcast.586) | data formatting | bytes 8388608 | tf_op jit(solution)/shard_map/mul | solution.py:264
  764.0 18.9 %broadcast_in_dim.34 = f32[2,32,32,512,2]{2,1,4,3,0:T(8,128)} broadcast(f32[2,32,32,512]{2,1,3,0:T(8,128)} %copy.94), dimensions={0,1,2,3} | broadcast | bytes 12582912 | tf_op jit(solution)/shard_map/broadcast_in_dim | solution.py:109
  782.9 22.8 %copy.95 = f32[2,32,32,1024]{3,1,2,0:T(8,128)} copy(f32[2,32,32,1024]{2,1,3,0:T(8,128)} %bitcast.583) | data formatting | bytes 16777216 | tf_op jit(solution)/shard_map/mul | solution.py:264
  826.5 41.9 %all-reduce.24 = (f32[]{:T(128)}, f32[3,3,2,32]{3,2,1,0:T(2,128)S(1)}, f32[64,32]{0,1:T(8,128)S(1)}, f32[32,3]{0,1:T(4,128)S(1)}, f32[163]{0:T(256)S(1)}) all-reduce(f32[]{:T(128)S(6)} %add.453, f32[3,3,2,32]{3,2,1,0:T(2,128)S(1)} %pad_maximum_fusion.18, f32[64,32]{0,1:T(8,128)S(1)} %fusion.150, ...), channel_id=1, replica_groups=mesh['img'=4,'tile'=8] {'img','tile'}, use_global_device_ids=true, to_apply=%region_7.8 | all-reduce | flops 2884 | bytes 23072 | tf_op jit(solution)/shard_map/psum | solution.py:272
  871.4 81.3 %all-reduce.28.cloned.1.call-done = (f32[3,3,32,64]{3,2,1,0:T(8,128)}, f32[3,3,64,32]{2,3,1,0:T(8,128)}) async-done(((f32[3,3,32,64]{3,2,1,0:T(8,128)}, f32[3,3,64,32]{2,3,1,0:T(8,128)}), (f32[3,3,32,64]{3,2,1,0:T(8,128)}, f32[3,3,64,32]{2,3,1,0:T(8,128)})) %all-reduce.28.cloned.1.call-update) | async-done | bytes 147472 | tf_op jit(solution)/shard_map/psum | solution.py:272
  (339 shorter events, 356.3 us)
Async XLA Ops:
  7.2 945.6 %all-reduce.28.cloned.1.call-start = ((), (), s32[]{:S(2)}) async-start(), calls=%async_computation | async-start | bytes 589824 | tf_op jit(solution)/shard_map/psum | solution.py:272
  9.5 11.2 %collective-permute-start = (bf16[2,2,1,1024]{3,1,2,0:T(2,128)(2,1)S(1)}, bf16[2,2,1,1024]{3,1,2,0:T(2,128)(2,1)S(1)}, u32[]{:S(2)}, u32[]{:S(2)}) collective-permute-start(bf16[2,2,1,1024]{3,1,2,0:T(2,128)(2,1)S(1)} %get-tuple-element.119), channel_id=1, source_target_pairs={{0,1},{1,2},{2,3},{3,4},{4,5},{5,6},{6,7},{8,9},{9,10},{10,11},{11... | collective-permute-start | bytes 24584 | tf_op jit(solution)/shard_map/ppermute | solution.py:25
  11.8 8.8 collective-permute-start.1
  19.9 157.9 %copy-start.22 = (bf16[3,3,32,64]{3,2,1,0:T(8,128)(2,1)}, bf16[3,3,32,64]{3,2,1,0:T(8,128)(2,1)S(1)}, u32[]{:S(2)}) copy-start(bf16[3,3,32,64]{3,2,1,0:T(8,128)(2,1)S(1)} %convert_element_type.164) | copy-start | bytes 110596
  149.7 7.7 collective-permute-start.2
  154.9 4.4 collective-permute-start.3
  191.1 23.9 %collective-permute-start.4 = (bf16[2,64,1,512]{3,1,2,0:T(8,128)(2,1)S(1)}, bf16[2,64,1,512]{3,1,2,0:T(8,128)(2,1)S(1)}, u32[]{:S(2)}, u32[]{:S(2)}) collective-permute-start(bf16[2,64,1,512]{3,1,2,0:T(8,128)(2,1)S(1)} %get-tuple-element.111), channel_id=1, source_target_pairs={{0,1},{1,2},{2,3},{3,4},{4,5},{5,6},{6,7},{8,9},{9,10},{10,11},{11... | collective-permute-start | bytes 393224 | tf_op jit(solution)/shard_map/ppermute | solution.py:25
  195.9 19.1 %collective-permute-start.5 = (bf16[2,64,1,512]{3,1,2,0:T(8,128)(2,1)S(1)}, bf16[2,64,1,512]{3,1,2,0:T(8,128)(2,1)S(1)}, u32[]{:S(2)}, u32[]{:S(2)}) collective-permute-start(bf16[2,64,1,512]{3,1,2,0:T(8,128)(2,1)S(1)} %get-tuple-element.112), channel_id=1, source_target_pairs={{1,0},{2,1},{3,2},{4,3},{5,4},{6,5},{7,6},{9,8},{10,9},{11,10},{12... | collective-permute-start | bytes 393224 | tf_op jit(solution)/shard_map/ppermute | solution.py:28
  382.4 3.5 collective-permute-start.6
  383.7 3.1 collective-permute-start.7
  387.1 6.8 collective-permute-start.8
  389.7 4.1 collective-permute-start.9
  712.4 3.9 collective-permute-start.10
  713.7 3.2 collective-permute-start.11
  735.0 7.7 collective-permute-start.12
  739.3 3.4 collective-permute-start.13
  823.5 46.7 %copy-start.63 = (f32[163]{0:T(256)S(1)}, f32[163]{0:T(256)}, u32[]{:S(2)}) copy-start(f32[163]{0:T(256)} %param.51) | copy-start | bytes 1960
  823.5 46.7 %copy-start.70 = (f32[163]{0:T(256)S(1)}, f32[163]{0:T(256)}, u32[]{:S(2)}) copy-start(f32[163]{0:T(256)} %param.53) | copy-start | bytes 1960
  823.5 129.2 %copy-start.25 = (f32[3,3,64,32]{2,3,1,0:T(8,128)S(1)}, f32[3,3,64,32]{2,3,1,0:T(8,128)}, u32[]{:S(2)}) copy-start(f32[3,3,64,32]{2,3,1,0:T(8,128)} %param.42) | copy-start | bytes 221188
  823.6 129.2 %copy-start.34 = (f32[3,3,64,32]{2,3,1,0:T(8,128)S(1)}, f32[3,3,64,32]{2,3,1,0:T(8,128)}, u32[]{:S(2)}) copy-start(f32[3,3,64,32]{2,3,1,0:T(8,128)} %param.44) | copy-start | bytes 221188
  823.6 129.2 %copy-start.35 = (f32[3,3,64,32]{2,3,1,0:T(8,128)S(1)}, f32[3,3,64,32]{2,3,1,0:T(8,128)}, u32[]{:S(2)}) copy-start(f32[3,3,64,32]{2,3,1,0:T(8,128)} %param.43) | copy-start | bytes 221188
  824.9 129.6 %copy-start.27 = (f32[3,3,32,64]{3,2,1,0:T(8,128)S(1)}, f32[3,3,32,64]{3,2,1,0:T(8,128)}, u32[]{:S(2)}) copy-start(f32[3,3,32,64]{3,2,1,0:T(8,128)} %param.39) | copy-start | bytes 221188
  824.9 129.6 %copy-start.36 = (f32[3,3,32,64]{3,2,1,0:T(8,128)S(1)}, f32[3,3,32,64]{3,2,1,0:T(8,128)}, u32[]{:S(2)}) copy-start(f32[3,3,32,64]{3,2,1,0:T(8,128)} %param.41) | copy-start | bytes 221188
  824.9 129.6 %copy-start.37 = (f32[3,3,32,64]{3,2,1,0:T(8,128)S(1)}, f32[3,3,32,64]{3,2,1,0:T(8,128)}, u32[]{:S(2)}) copy-start(f32[3,3,32,64]{3,2,1,0:T(8,128)} %param.40) | copy-start | bytes 221188
  (72 other events, 1265.7 us)
Sparse Core Ops, SparseCore 0:
  826.6 126.1 all-reduce.27
where the time goes:
time: 977 us; the launch traced here: 965 us
  matrix products  348 us (36%)
  local copies, waits for them, and re-layouts  213 us (22%)
  other arithmetic  194 us (20%)
  waiting for transfers between devices  84.8 us (9%)
  blocking collectives  73 us (7%)
  starting transfers between devices  31.7 us (3%)
  between operations  20.1 us (2%)
    dot_general x27, matrix products, conv_rows(): jnp.einsum('cirw,io->corw', window, kernel[offset_row, offset_col], prefe...  197 us
    psum x1, waiting for transfers between devices, on_device(): lax.psum((grad_kernel_one, grad_kernel_two, grad_kernel_three, grad_style...  81.3 us
    dot_general x18, matrix products, input_grad_padded(): jnp.einsum('corw,io->cirw', grad_out, kernel[offset_row, offset_col], pre...  73.5 us
    reduce_sum x2, other arithmetic, pool_sum(): jnp.sum(values.reshape(in_shape[0], in_shape[1], in_shape[2] // 2, 2, in_...  70.7 us
    dot_general x27, matrix products, conv_weight_grad(): jnp.einsum('cirw,corw->io', window, grad_out, preferred_element_type=jnp....  70.7 us
    add x2, other arithmetic, input_grad_padded(): result + jnp.pad(partial_term, ((0, 0), (0, 0), (offset_row, 2 - offset_r...  69.2 us
    unnamed x163, local copies, waits for them, and re-layouts  47.8 us
    broadcast_in_dim x4, local copies, waits for them, and re-layouts, upsample(): return jnp.repeat(jnp.repeat(values, 2, axis=2), 2, axis=3)  43.5 us
  transfers between devices with their start and end apart: 15, of which 4 were waited for; matrix products, arithmetic and copies ran while one was open for 2% of the time, Pallas kernels for 0%

commit v1 on v0

v1 whole, which is shorter than its diff:
```python
import math

import numpy as np
import jax
import jax.numpy as jnp
from jax import lax
from jax.experimental import pallas as pl
from jax.experimental.pallas import tpu as pltpu
from jax.sharding import PartitionSpec as P

CH_ONE = 32
CH_TWO = 64
OUT_CH = 3

momentum_rate = 0.9
learn_rate = 0.02
decay_rate = 0.0001
norm_eps = 1e-05
highest = lax.Precision.HIGHEST
f32 = jnp.float32
bf16 = jnp.bfloat16

IN_HALO = 7
LABEL_HALO = 2
VMEM = pl.BlockSpec(memory_space=pltpu.VMEM)
SMEM = pl.BlockSpec(memory_space=pltpu.SMEM)


def tap_select(kind):
    table = np.zeros(kind[0], np.float32)
    for spot in kind[1]:
        table[spot] = 1.0
    return table


SEL_ONE = tap_select(((2, 4, 3), [(p, p + a, a) for p in range(2) for a in range(3)]))
SEL_UP = tap_select(((2, 3, 3), [(p, (p + a + 1) // 2, a) for p in range(2) for a in range(3)]))
SEL_DOWN = tap_select(((4, 3), [(x - a + 2, a) for x in range(2) for a in range(3)]))


def dot(a, b):
    return jnp.dot(a, b, preferred_element_type=f32)


def dot_nt(a, b):
    return lax.dot_general(a, b, (((1,), (1,)), ((), ())), preferred_element_type=f32)


def from_left(x):
    lane = lax.broadcasted_iota(jnp.int32, x.shape, 1)
    return jnp.where(lane == 0, 0.0, pltpu.roll(x, 1, 1))


def from_right(x):
    width = x.shape[1]
    lane = lax.broadcasted_iota(jnp.int32, x.shape, 1)
    return jnp.where(lane == width - 1, 0.0, pltpu.roll(x, width - 1, 1))


def fold_lanes(x):
    total = x[:, 0:128]
    for k in range(1, x.shape[1] // 128):
        total = total + x[:, 128 * k : 128 * (k + 1)]
    return total


def wide(tile, width):
    return jnp.concatenate([tile] * (width // 128), axis=1)


def rows_of(ref, crop, start, size, align=16):
    return ref[crop, pl.ds(pl.multiple_of(start, align), size), :]


def put_lanes(ref, crop, start, size, value):
    for k in range(value.shape[1] // 128):
        ref[crop, k, pl.ds(pl.multiple_of(start, 8), size), :] = value[:, 128 * k : 128 * (k + 1)]


def get_lanes(ref, crop, start, size, stride=None):
    parts = []
    for k in range(ref.shape[1]):
        spot = pl.ds(start, size, stride=stride) if stride else pl.ds(pl.multiple_of(start, 8), size)
        parts.append(ref[crop, k, spot, :])
    return jnp.concatenate(parts, axis=1)


def valid(row, edge_ref):
    return jnp.where((row >= edge_ref[0]) & (row < edge_ref[1]), 1.0, 0.0).astype(f32)


def split_columns(x, select):
    even, odd = [], []
    for k in range(x.shape[1] // 256):
        piece = dot(x[:, 256 * k : 256 * (k + 1)], select)
        even.append(piece[:, 0:128])
        odd.append(piece[:, 128:256])
    return jnp.concatenate(even, axis=1), jnp.concatenate(odd, axis=1)


def first_kernel(
    edge_ref, nucleus_ref, x_ref, t_ref, w1_ref, b1_ref, w2_ref, b2_ref,
    y_ref, t_out, h1_ref, pool_ref, h2_ref, style_ref, x2_ref,
):
    crops = x_ref.shape[0]
    width = x_ref.shape[2] // 2
    rows = h2_ref.shape[1] // CH_TWO - 4
    top = IN_HALO // 2
    r_id = lax.broadcasted_iota(jnp.int32, (256, 256), 0)
    c_id = lax.broadcasted_iota(jnp.int32, (256, 256), 1)
    select = jnp.where(r_id == 2 * (c_id % 128) + c_id // 128, 1.0, 0.0).astype(bf16)
    x_rows = x_ref.shape[1]
    per_ch = x_rows // 2
    y_rows = y_ref.shape[1]
    ri = lax.broadcasted_iota(jnp.int32, (y_rows, 4 * x_rows), 0)
    ci = lax.broadcasted_iota(jnp.int32, (y_rows, 4 * x_rows), 1)
    source = (ri % 4) * x_rows + ((ri // 4) % 2) * per_ch + 2 * (ri // 16) + (ri // 8) % 2
    perm_x = jnp.where(ci == source, 1.0, 0.0).astype(bf16)
    t_rows = t_ref.shape[1]
    per_t = t_rows // 3
    ri = lax.broadcasted_iota(jnp.int32, (t_out.shape[2], 2 * t_rows), 0)
    ci = lax.broadcasted_iota(jnp.int32, (t_out.shape[2], 2 * t_rows), 1)
    part = (ri // 4) % 4
    source = (ri % 2) * t_rows + part * per_t + 2 * (ri // 16) + (ri // 2) % 2
    perm_t = jnp.where((ci == source) & (part < 3), 1.0, 0.0).astype(bf16)
    for c in range(crops):
        even, odd = split_columns(x_ref[c], select)
        row = lax.broadcasted_iota(jnp.int32, (x_rows, width), 0)
        gate = jnp.where(row >= per_ch, nucleus_ref[c].astype(f32), 1.0)
        even, odd = even * gate, odd * gate
        stack = jnp.concatenate([from_left(odd), even, odd, from_right(even)], axis=0)
        y_ref[c] = dot(perm_x, stack.astype(bf16)).astype(bf16)
        even, odd = split_columns(t_ref[c], select)
        put_lanes(t_out, c, 0, t_out.shape[2], dot(perm_t, jnp.concatenate([even, odd], axis=0).astype(bf16)))
    style_ref[...] = jnp.zeros_like(style_ref)
    bias1 = jnp.broadcast_to(b1_ref[...], (4 * CH_ONE, 128))
    bias2 = jnp.broadcast_to(b2_ref[...], (CH_TWO, 128))

    def conv_one(k):
        row = k - top
        keep = valid(row, edge_ref)
        spot = jnp.clip(row + 1, 0, rows + 2)
        pre = [dot(w1_ref[...], rows_of(y_ref, c, k * 16, 32)) for c in range(crops)]
        for c in range(crops):
            hidden = (jnp.maximum(pre[c] + wide(bias1, width), 0.0) * keep).astype(bf16)
            h1_ref[c, pl.ds(pl.multiple_of(spot * 128, 128), 128), :] = hidden
            h = hidden.astype(f32)
            pooled = (0.25 * ((h[0:32] + h[32:64]) + (h[64:96] + h[96:128]))).astype(bf16)
            pool_ref[c, pl.ds(pl.multiple_of(spot * 32, 32), 32), :] = pooled
            p = pooled.astype(f32)
            both = jnp.concatenate([from_left(p).astype(bf16), pooled, from_right(p).astype(bf16)], axis=0)
            x2_ref[c, pl.ds(pl.multiple_of(k * 96, 96), 96), :] = both

    def conv_two(q):
        row = q - 2
        keep = valid(row, edge_ref)
        own = jnp.where((row >= 0) & (row < rows), 1.0, 0.0).astype(f32)
        pre = [dot(w2_ref[...], rows_of(x2_ref, c, q * 96, 288)) for c in range(crops)]
        for c in range(crops):
            hidden = (jnp.maximum(pre[c] + wide(bias2, width), 0.0) * keep).astype(bf16)
            h2_ref[c, pl.ds(pl.multiple_of(q * 64, 64), 64), :] = hidden
            style_ref[c] += fold_lanes(hidden.astype(f32)) * own

    def loop_one(k, carry):
        conv_one(k)
        return carry

    def loop_both(k, carry):
        conv_two(k - 3)
        conv_one(k)
        return carry

    lax.fori_loop(0, 3, loop_one, 0)
    lax.fori_loop(3, rows + 6, loop_both, 0)
    conv_two(rows + 3)


def second_kernel(
    scale, edge_ref, h1_ref, h2_ref, t_ref, bs_ref, w3_ref, wh_ref, wht_ref, wd3_ref, bh_ref,
    gc_ref, go_out, d3_ref, head_ref, small_ref, sg_ref, loss_ref,
    x3_ref, h3_ref, m_ref, fe_ref, go_ref, g3_ref,
):
    crops = h1_ref.shape[0]
    width = h1_ref.shape[2]
    rows = go_out.shape[1] // 16

    def shift(k, carry):
        for c in range(crops):
            mid = rows_of(h2_ref, c, k * 64, 64)
            x = mid.astype(f32)
            x3_ref[c, pl.ds(pl.multiple_of(k * 192, 192), 192), :] = jnp.concatenate(
                [from_left(x).astype(bf16), mid, from_right(x).astype(bf16)], axis=0
            )
        return carry

    lax.fori_loop(0, rows + 4, shift, 0)
    bias3 = [jnp.broadcast_to(bs_ref[c], (4 * CH_ONE, 128)) for c in range(crops)]
    bias_h = jnp.broadcast_to(bh_ref[...], (16, 128))

    def forward(k, carry):
        row = k - 1
        keep = valid(row, edge_ref)
        pre = [dot(w3_ref[...], rows_of(x3_ref, c, k * 192, 576)) for c in range(crops)]
        hs = []
        for c in range(crops):
            p = pre[c][0:128] + pre[c][128:256] + wide(bias3[c], width)
            h1 = rows_of(h1_ref, c, k * 128, 128).astype(f32)
            h3 = (jnp.maximum(p, 0.0) + h1).astype(bf16)
            h3_ref[c, pl.ds(pl.multiple_of(k * 128, 128), 128), :] = h3
            m_ref[c, pl.ds(pl.multiple_of(k * 128, 128), 128), :] = jnp.where(p > 0, 1.0, 0.0).astype(bf16)
            hs.append(h3)
        outs = [dot(wh_ref[...], h) for h in hs]
        for c in range(crops):
            o = outs[c] + wide(bias_h, width)
            t = get_lanes(t_ref, c, k * 16, 16)
            fe = (o[0:8] - 0.25 * t[0:8]) * keep
            put_lanes(fe_ref, c, k * 16, 16, jnp.concatenate([fe, o[8:16]], axis=0))
        return carry

    lax.fori_loop(0, rows + 2, forward, 0)

    r_id = lax.broadcasted_iota(jnp.int32, (rows, width), 0)
    above = jnp.where(r_id - 1 >= edge_ref[0], 1.0, 0.0)
    below = jnp.where(r_id + 1 < edge_ref[1], 1.0, 0.0)
    loss = jnp.zeros((rows, 128), f32)
    go_ref[...] = jnp.zeros_like(go_ref)
    for c in range(crops):

        def at(part, off):
            return get_lanes(fe_ref, c, 16 * (1 + off) + part, rows, 16)

        def column_part(pr, off):
            odd, even = at(4 + 2 * pr + 1, off), at(4 + 2 * pr, off)
            return 0.5 * (odd - from_left(odd)), 0.5 * (from_right(even) - even)

        e0 = [at(k, 0) for k in range(4)]
        e1 = [at(4 + k, 0) for k in range(4)]
        cols0, cols1 = column_part(0, 0), column_part(1, 0)
        cols_up, cols_dn = column_part(1, -1), column_part(0, 1)
        spread = [None] * 4
        g_up, g_dn = [None] * 2, [None] * 2
        for pc in range(2):
            f_up, f_dn = at(2 + pc, -1), at(pc, 1)
            spread[pc] = 0.5 * (e0[2 + pc] - f_up) + cols0[pc]
            spread[2 + pc] = 0.5 * (f_dn - e0[pc]) + cols1[pc]
            g_up[pc] = 2.0 * scale * above * (0.5 * (e0[pc] - at(pc, -1)) + cols_up[pc])
            g_dn[pc] = 2.0 * scale * below * (0.5 * (at(2 + pc, 1) - e0[2 + pc]) + cols_dn[pc])
        g = [2.0 * scale * v for v in spread]
        for pr in range(2):
            even, odd = g[2 * pr], g[2 * pr + 1]
            col = [0.5 * (odd - from_left(odd)), 0.5 * (from_right(even) - even)]
            for pc in range(2):
                k = 2 * pr + pc
                if pr == 0:
                    row_part = 0.5 * (g[2 + pc] - g_up[pc])
                else:
                    row_part = 0.5 * (g_dn[pc] - g[pc])
                logit = at(8 + k, 0)
                label = get_lanes(t_ref, c, 16 + 8 + k, rows, 16)
                ex = jnp.exp(-jnp.abs(logit))
                sig = jnp.where(logit >= 0, 1.0, ex) / (1.0 + ex)
                grads = (2.0 * scale * e0[k] - row_part, 2.0 * scale * e1[k] - col[pc], scale * (sig - label))
                for part in range(OUT_CH):
                    for j in range(width // 128):
                        go_ref[c, j, pl.ds(4 * part + k, rows, stride=16), :] = grads[part][:, 128 * j : 128 * (j + 1)]
                term = jnp.maximum(logit, 0.0) + jnp.log1p(ex) - label * logit
                loss = loss + fold_lanes(e0[k] * e0[k] + e1[k] * e1[k] + spread[k] * spread[k] + term)
    loss_ref[...] = loss

    head_ref[...] = jnp.zeros_like(head_ref)
    small_ref[...] = jnp.zeros_like(small_ref)
    sg_ref[...] = jnp.zeros_like(sg_ref)
    d3_ref[...] = jnp.zeros_like(d3_ref)
    edge = jnp.zeros((256, width), bf16)
    for c in range(crops):
        for k in (0, 1, rows + 2, rows + 3):
            g3_ref[c, 256 * k : 256 * (k + 1), :] = edge

    def backward(r, carry):
        gos, gts = [], []
        for c in range(crops):
            go = get_lanes(go_ref, c, r * 16, 16).astype(bf16)
            go_out[c, pl.ds(pl.multiple_of(r * 16, 16), 16), :] = go
            gos.append(go)
            gts.append(dot(wht_ref[...], go))
        for c in range(crops):
            spot = (r + 1) * 128
            head_ref[...] += dot_nt(gos[c], rows_of(h3_ref, c, spot, 128))
            small_ref[...] += fold_lanes(gos[c].astype(f32))
            g = gts[c].astype(bf16).astype(f32) * rows_of(m_ref, c, spot, 128).astype(f32)
            sg_ref[c] += fold_lanes(g)
            parts = []
            gb = g.astype(bf16)
            for pr in range(2):
                even, odd = g[64 * pr : 64 * pr + 32], g[64 * pr + 32 : 64 * pr + 64]
                parts += [from_left(odd).astype(bf16), gb[64 * pr : 64 * pr + 64], from_right(even).astype(bf16)]
            g3_ref[c, pl.ds(pl.multiple_of((r + 2) * 256, 256), 256), :] = jnp.concatenate(parts, axis=0)
            d3_ref[...] += dot_nt(gb, rows_of(x3_ref, c, (r + 1) * 192, 576))
        return carry

    lax.fori_loop(0, rows, backward, 0)

    def down(k, carry):
        both = [dot(wd3_ref[...], rows_of(g3_ref, c, k * 256 + 128, 512)) for c in range(crops)]
        for c in range(crops):
            gc_ref[c, pl.ds(pl.multiple_of(k * 64, 64), 64), :] = both[c][0:64] + both[c][64:128]
        return carry

    lax.fori_loop(0, rows + 2, down, 0)


def third_kernel(
    gc_ref, up_ref, dn_ref, raw_ref, h2_ref, pool_ref, h1_ref, y_ref, go_ref, wd2_ref, wht_ref,
    d2_ref, d1_ref, b2_ref, b1_ref,
    g2_ref, x2_ref,
):
    crops = h1_ref.shape[0]
    width = h1_ref.shape[2]
    rows = go_ref.shape[1] // 16
    raw = [jnp.broadcast_to(raw_ref[c], (CH_TWO, 128)) for c in range(crops)]
    b2_ref[...] = jnp.zeros_like(b2_ref)
    b1_ref[...] = jnp.zeros_like(b1_ref)
    d2_ref[...] = jnp.zeros_like(d2_ref)
    d1_ref[...] = jnp.zeros_like(d1_ref)

    def masked(k, c, extra, own):
        coarse = rows_of(gc_ref, c, k * 64, 64)
        if extra is not None:
            coarse = coarse + extra.astype(f32)
        grad = (coarse + wide(raw[c], width)).astype(bf16)
        h2 = rows_of(h2_ref, c, (k + 1) * 64, 64).astype(f32)
        g = jnp.where(h2 > 0, grad.astype(f32), 0.0)
        if own:
            b2_ref[...] += fold_lanes(g)
        g2_ref[c, pl.ds(pl.multiple_of(k * 192, 192), 192), :] = jnp.concatenate(
            [from_left(g).astype(bf16), g.astype(bf16), from_right(g).astype(bf16)], axis=0
        )

    def widen(k, carry):
        for c in range(crops):
            mid = rows_of(pool_ref, c, k * 32, 32)
            x = mid.astype(f32)
            x2_ref[c, pl.ds(pl.multiple_of(k * 96, 96), 96), :] = jnp.concatenate(
                [from_left(x).astype(bf16), mid, from_right(x).astype(bf16)], axis=0
            )
        return carry

    lax.fori_loop(0, rows + 2, widen, 0)
    for c in range(crops):
        masked(0, c, up_ref[c, 0:64], False)
        masked(1, c, up_ref[c, 64:128], True)
        masked(rows, c, dn_ref[c, 0:64], True)
        masked(rows + 1, c, dn_ref[c, 64:128], False)

    def inner(k, carry):
        for c in range(crops):
            masked(k, c, None, True)
        return carry

    lax.fori_loop(2, rows, inner, 0)

    def backward(r, carry):
        gps = [dot(wd2_ref[...], rows_of(g2_ref, c, r * 192, 576)) for c in range(crops)]
        gts = [dot(wht_ref[...], rows_of(go_ref, c, r * 16, 16)) for c in range(crops)]
        for c in range(crops):
            d2_ref[...] += dot_nt(rows_of(g2_ref, c, (r + 1) * 192 + 64, 64), rows_of(x2_ref, c, r * 96, 288))
            gp = 0.25 * gps[c].astype(bf16).astype(f32)
            g1 = (jnp.concatenate([gp] * 4, axis=0) + gts[c].astype(bf16).astype(f32)).astype(bf16).astype(f32)
            h1 = rows_of(h1_ref, c, (r + 1) * 128, 128).astype(f32)
            g1 = jnp.where(h1 > 0, g1, 0.0)
            b1_ref[...] += fold_lanes(g1)
            d1_ref[...] += dot_nt(g1.astype(bf16), rows_of(y_ref, c, (r + 3) * 16, 32))
        return carry

    lax.fori_loop(0, rows, backward, 0)


def neighbours(block_low, block_high, axis):
    count = lax.axis_size(axis)
    forward = [(i, i + 1) for i in range(count - 1)]
    backward = [(i + 1, i) for i in range(count - 1)]
    return lax.ppermute(block_high, axis, forward), lax.ppermute(block_low, axis, backward)


def nesterov(weight, gradient, momentum, average, count):
    decayed = gradient + decay_rate * weight
    momentum_new = momentum_rate * momentum + decayed
    weight_new = weight - learn_rate * (decayed + momentum_rate * momentum_new)
    average_new = average + (weight_new - average) / (count + 1.0)
    return (weight_new, momentum_new, average_new)


def on_device(
    images, nucleus, target_flow, cell_label, step_count,
    conv1_weight, conv1_momentum, conv1_average,
    conv2_weight, conv2_momentum, conv2_average,
    conv3_weight, conv3_momentum, conv3_average,
    style_weight, style_momentum, style_average,
    head_weight, head_momentum, head_average,
    biases, bias_momentum, bias_average,
):
    tiles = lax.axis_size("tile")
    me = lax.axis_index("tile")
    crops, _, height, cols = images.shape
    rows, width = height // 2, cols // 2
    pixel_count = lax.axis_size("img") * tiles * crops * height * cols
    grad_scale = 1.0 / math.sqrt(pixel_count)
    coarse_count = tiles * rows * width

    def sds(shape, dtype=f32):
        return jax.ShapeDtypeStruct(shape, dtype)

    k1, k2, k3, kh = (w.astype(bf16) for w in (conv1_weight, conv2_weight, conv3_weight, head_weight))
    bias_one = biases[0:CH_ONE]
    bias_two = biases[CH_ONE : CH_ONE + CH_TWO]
    bias_three = biases[CH_ONE + CH_TWO : 2 * CH_ONE + CH_TWO]
    bias_style = biases[2 * CH_ONE + CH_TWO : 3 * CH_ONE + CH_TWO]
    bias_head = biases[3 * CH_ONE + CH_TWO :]

    w1 = jnp.einsum("pja,qlb,abio->pqojil", SEL_ONE, SEL_ONE, k1.astype(f32), precision=highest)
    w1 = w1.reshape(4 * CH_ONE, 32).astype(bf16)
    w2 = jnp.transpose(k2, (3, 0, 1, 2)).reshape(CH_TWO, 9 * CH_ONE)
    w3 = jnp.einsum("pra,qcb,abio->pqorci", SEL_UP, SEL_UP, k3.astype(f32), precision=highest)
    w3 = w3.reshape(4 * CH_ONE, 9 * CH_TWO)
    w3_hi = lax.reduce_precision(w3, 8, 7)
    w3 = jnp.concatenate([w3_hi.astype(bf16), (w3 - w3_hi).astype(bf16)], axis=0)
    wd3 = jnp.einsum("ra,cb,abio->irco", SEL_DOWN, SEL_DOWN, k3.astype(f32), precision=highest)
    wd3 = wd3.reshape(CH_TWO, 16 * CH_ONE)
    wd3_hi = lax.reduce_precision(wd3, 8, 7)
    wd3 = jnp.concatenate([wd3_hi.astype(bf16), (wd3 - wd3_hi).astype(bf16)], axis=0)
    wd2 = jnp.transpose(k2[::-1, ::-1], (2, 0, 1, 3)).reshape(CH_ONE, 9 * CH_TWO)
    wht = jnp.einsum("pq,io->piqo", jnp.eye(4, dtype=f32), kh.astype(f32)).transpose(0, 1, 3, 2)
    wht = jnp.pad(wht.reshape(4 * CH_ONE, 4 * OUT_CH), ((0, 0), (0, 4))).astype(bf16)
    wh = wht.T
    bh = jnp.pad(jnp.repeat(bias_head, 4), (0, 4)).reshape(16, 1)
    b1 = jnp.tile(bias_one, 4).reshape(4 * CH_ONE, 1)
    b2 = bias_two.reshape(CH_TWO, 1)

    edges = jnp.stack([-me * rows, (tiles - me) * rows]).astype(jnp.int32)
    low, high = neighbours(images[:, :, :IN_HALO], images[:, :, -IN_HALO:], "tile")
    pad = jnp.zeros((crops, 2, 2, cols), bf16)
    x = jnp.concatenate([low, images, high, pad], axis=2).reshape(crops, 2 * (height + 16), cols)
    flow = target_flow.astype(bf16)
    low, high = neighbours(flow[:, :, :LABEL_HALO], flow[:, :, -LABEL_HALO:], "tile")
    flow = jnp.concatenate([low, flow, high], axis=2)
    label = jnp.pad(cell_label.astype(bf16), ((0, 0), (2, 2), (0, 0)))[:, None]
    t = jnp.pad(jnp.concatenate([flow, label], axis=1), ((0, 0), (0, 0), (0, 4), (0, 0)))
    t = t.reshape(crops, 3 * (height + 8), cols)

    limit = pltpu.CompilerParams(vmem_limit_bytes=60 * 2**20)
    y, targets, h1, pool, h2, style_part = pl.pallas_call(
        first_kernel,
        out_shape=(
            sds((crops, 16 * (rows + 7), width), bf16),
            sds((crops, width // 128, 16 * (rows + 2), 128)),
            sds((crops, 128 * (rows + 3), width), bf16),
            sds((crops, 32 * (rows + 3), width), bf16),
            sds((crops, 64 * (rows + 4), width), bf16),
            sds((crops, CH_TWO, 128)),
        ),
        in_specs=[SMEM, SMEM] + [VMEM] * 6,
        out_specs=[VMEM] * 6,
        scratch_shapes=[pltpu.VMEM((crops, 96 * (rows + 6), width), bf16)],
        compiler_params=limit,
        name="forward_one_two",
    )(edges, nucleus, x, t, w1, b1, w2, b2)

    style_raw = lax.psum(jnp.sum(style_part, axis=2), "tile") / coarse_count
    style_inv = lax.rsqrt(jnp.mean(style_raw * style_raw, axis=1, keepdims=True) + norm_eps)
    style_unit = style_raw * style_inv
    style_vec = jnp.dot(style_unit, style_weight, precision=highest) + bias_style
    bs = jnp.tile(style_vec + bias_three, (1, 4))[:, :, None]

    def second(*refs):
        second_kernel(grad_scale, *refs)

    gc, go, d3, head, small, sg, loss = pl.pallas_call(
        second,
        out_shape=(
            sds((crops, 64 * (rows + 2), width)),
            sds((crops, 16 * rows, width), bf16),
            sds((4 * CH_ONE, 9 * CH_TWO)),
            sds((16, 128)),
            sds((16, 128)),
            sds((crops, 4 * CH_ONE, 128)),
            sds((rows, 128)),
        ),
        in_specs=[SMEM] + [VMEM] * 9,
        out_specs=[VMEM] * 7,
        scratch_shapes=[
            pltpu.VMEM((crops, 192 * (rows + 4), width), bf16),
            pltpu.VMEM((crops, 128 * (rows + 2), width), bf16),
            pltpu.VMEM((crops, 128 * (rows + 2), width), bf16),
            pltpu.VMEM((crops, width // 128, 16 * (rows + 2), 128), f32),
            pltpu.VMEM((crops, width // 128, 16 * rows, 128), f32),
            pltpu.VMEM((crops, 256 * (rows + 4), width), bf16),
        ],
        compiler_params=limit,
        name="forward_three_back",
    )(edges, h1, h2, targets, bs, w3, wh, wht, wd3, bh)

    style_grad_part = jnp.sum(sg.reshape(crops, 4, CH_ONE, 128), axis=(1, 3))
    grad_bias_three = jnp.sum(style_grad_part, axis=0)
    grad_style_weight = jnp.dot(style_unit.T, style_grad_part, precision=highest)
    style_grad = lax.psum(style_grad_part, "tile")
    grad_unit = jnp.dot(style_grad, style_weight.T, precision=highest)
    grad_raw = style_inv * grad_unit - style_inv**3 * style_raw * jnp.mean(
        style_raw * grad_unit, axis=1, keepdims=True
    )
    raw = (grad_raw / coarse_count)[:, :, None]
    rim = gc.reshape(crops, rows + 2, CH_TWO, width)
    rim_low = rim[:, 0:2].reshape(crops, 128, width).astype(bf16)
    rim_high = rim[:, rows : rows + 2].reshape(crops, 128, width).astype(bf16)
    from_up, from_dn = neighbours(rim_low, rim_high, "tile")

    d2, d1, gb2, gb1 = pl.pallas_call(
        third_kernel,
        out_shape=(
            sds((CH_TWO, 9 * CH_ONE)),
            sds((4 * CH_ONE, 32)),
            sds((CH_TWO, 128)),
            sds((4 * CH_ONE, 128)),
        ),
        in_specs=[VMEM] * 11,
        out_specs=[VMEM] * 4,
        scratch_shapes=[
            pltpu.VMEM((crops, 192 * (rows + 2), width), bf16),
            pltpu.VMEM((crops, 96 * (rows + 2), width), bf16),
        ],
        compiler_params=limit,
        name="back_two_one",
    )(gc, from_up, from_dn, raw, h2, pool, h1, y, go, wd2, wht)

    d1 = d1.reshape(2, 2, CH_ONE, 4, 2, 4)
    grad_kernel_one = jnp.einsum("pqojil,pja,qlb->abio", d1, SEL_ONE, SEL_ONE, precision=highest)
    grad_kernel_two = jnp.transpose(d2.reshape(CH_TWO, 3, 3, CH_ONE), (1, 2, 3, 0))
    d3 = d3.reshape(2, 2, CH_ONE, 3, 3, CH_TWO)
    grad_kernel_three = jnp.einsum("pqorci,pra,qcb->abio", d3, SEL_UP, SEL_UP, precision=highest)
    head = head.reshape(4, 4, 4, CH_ONE)[:OUT_CH]
    grad_head = jnp.einsum("oppi->io", head)
    grad_bias_head = jnp.sum(small.reshape(4, 4, 128), axis=(1, 2))[:OUT_CH]
    grad_bias_two = jnp.sum(gb2, axis=1)
    grad_bias_one = jnp.sum(gb1.reshape(4, CH_ONE, 128), axis=(0, 2))
    grad_bias = jnp.concatenate([grad_bias_one, grad_bias_two, grad_bias_three, grad_bias_three, grad_bias_head])
    summed = lax.psum(
        (grad_kernel_one, grad_kernel_two, grad_kernel_three, grad_style_weight, grad_head, grad_bias, jnp.sum(loss)),
        ("img", "tile"),
    )
    count = step_count[0].astype(f32)
    olds = (
        (conv1_weight, conv1_momentum, conv1_average),
        (conv2_weight, conv2_momentum, conv2_average),
        (conv3_weight, conv3_momentum, conv3_average),
        (style_weight, style_momentum, style_average),
        (head_weight, head_momentum, head_average),
        (biases, bias_momentum, bias_average),
    )
    results = [(summed[6] / pixel_count).reshape(1)]
    for k, state in enumerate(olds):
        results.extend(nesterov(state[0], summed[k], state[1], state[2], count))
    return tuple(results)


def solution(mesh):
    return jax.shard_map(
        on_device,
        mesh=mesh,
        in_specs=(
            P("img", None, "tile", None),
            P("img"),
            P("img", None, "tile", None),
            P("img", "tile", None),
        )
        + (P(),) * 19,
        out_specs=(P(),) * 19,
        check_vma=False,
    )
```

time: 977 us -> 312 us (0.32); the launches traced: 965 us -> 311 us
  matrix products: 348 us -> 6.05 us
  local copies, waits for them, and re-layouts: 213 us -> 20.5 us
  other arithmetic: 194 us -> 22.2 us
  Pallas kernels: 0 us -> 77.4 us
  starting transfers between devices: 31.7 us -> 13.3 us
    dot_general x75 -> x10, matrix products: 347 us -> 5.39 us  [the longest x2 1.8 us: on_device(): jnp.einsum('pra,qcb,abio->pqorci', SEL_UP, SEL_UP, k3.astype(f32), precis...]
    reduce_sum x7 -> x9, other arithmetic: 82.4 us -> 3.73 us  [the longest x2 0.98 us: on_device(): grad_bias_one = jnp.sum(gb1.reshape(4, CH_ONE, 128), axis=(0, 2))]
    pallas_call x0 -> x3, Pallas kernels: none -> 77.4 us  [the longest x1 39.4 us: on_device(): pl.pallas_call(second, out_shape=(sds((crops, 64 * (rows + 2), width)), s...]
    add x2 -> x0, other arithmetic: 69.2 us -> none  [input_grad_padded(): result + jnp.pad(partial_term, ((0, 0), (0, 0), (offset_row, 2 - offset_r...]
    unnamed x163 -> x63, local copies, waits for them, and re-layouts: 47.8 us -> 2.72 us
    broadcast_in_dim x4, local copies, waits for them, and re-layouts: 43.5 us -> 0.86 us  [the longest x1 0.75 us: on_device(): raw = (grad_raw / coarse_count)[:, :, None]]
    mul x2 -> x0, local copies, waits for them, and re-layouts: 37.3 us -> none  [on_device(): 0.25 * upsample(grad_pooled).astype(jnp.float32)]
    pad x1, local copies, waits for them, and re-layouts: 25.7 us -> 0.62 us  [on_device(): jnp.pad(wht.reshape(4 * CH_ONE, 4 * OUT_CH), ((0, 0), (0, 4))).astype(bf16)]
  transfers between devices with their start and end apart: 15 -> 7, of which waited for: 4 -> 1; matrix products, arithmetic and copies ran while one was open for 2% -> 9% of each run, Pallas kernels for 0% -> 0%
where the time goes in v1:
time: 312 us; the launch traced here: 311 us
  waiting for transfers between devices  80.2 us (26%)
  Pallas kernels  77.4 us (25%)
  blocking collectives  74.2 us (24%)
  other arithmetic  22.2 us (7%)
  local copies, waits for them, and re-layouts  20.5 us (7%)
  between operations  17.1 us (5%)
  starting transfers between devices  13.3 us (4%)
  matrix products  6.05 us (2%)
    psum x1, waiting for transfers between devices, on_device(): lax.psum((grad_kernel_one, grad_kernel_two, grad_kernel_three, grad_style...  80.2 us
    psum x1, blocking collectives, on_device(): lax.psum((grad_kernel_one, grad_kernel_two, grad_kernel_three, grad_style...  42.4 us
    pallas_call x1, Pallas kernels, on_device(): pl.pallas_call(second, out_shape=(sds((crops, 64 * (rows + 2), width)), s...  39.4 us
    pallas_call x1, Pallas kernels, on_device(): pl.pallas_call(third_kernel, out_shape=(sds((CH_TWO, 9 * CH_ONE)), sds((4...  21.3 us
    psum x1, blocking collectives, on_device(): style_raw = lax.psum(jnp.sum(style_part, axis=2), 'tile') / coarse_count  18 us
    pallas_call x1, Pallas kernels, on_device(): pl.pallas_call(first_kernel, out_shape=(sds((crops, 16 * (rows + 7), widt...  16.7 us
    psum x1, blocking collectives, on_device(): style_grad = lax.psum(style_grad_part, 'tile')  13.8 us
    ppermute x3, starting transfers between devices, neighbours(): lax.ppermute(block_high, axis, forward)  9.39 us
  transfers between devices with their start and end apart: 7, of which 1 were waited for; matrix products, arithmetic and copies ran while one was open for 9% of the time, Pallas kernels for 0%

profile of v1, /device:TPU:0, one launch (start us, length us, event | category | flops | bytes accessed | tf_op | source)
XLA Modules:
  0.0 310.9 jit_solution(15676635375351182518)
XLA Ops:
  8.2 2.4 collective-permute-start
  10.5 1.3 collective-permute-start.1
  11.8 1.1 convert_element_type.63
  13.0 5.2 %collective-permute-start.2 = (bf16[2,2,2,1024]{3,2,1,0:T(2,128)(2,1)S(1)}, bf16[2,2,2,1024]{3,2,1,0:T(2,128)(2,1)S(1)}, u32[]{:S(2)}, u32[]{:S(2)}) collective-permute-start(bf16[2,2,2,1024]{3,2,1,0:T(2,128)(2,1)S(1)} %get-tuple-element.161), channel_id=1, source_target_pairs={{0,1},{1,2},{2,3},{3,4},{4,5},{5,6},{6,7},{8,9},{9,10},{10,11},{11... | collective-permute-start | bytes 49160 | tf_op jit(solution)/shard_map/ppermute | solution.py:382
  18.2 1.3 collective-permute-start.3
  26.2 1.0 convert_element_type.64
  28.9 1.4 convolution_bitcast_fusion
  41.1 16.7 %forward_one_two.1 = (bf16[2,368,512]{2,1,0:T(8,128)(2,1)}, f32[2,4,288,128]{3,2,1,0:T(8,128)}, bf16[2,2432,512]{2,1,0:T(8,128)(2,1)}, bf16[2,608,512]{2,1,0:T(8...) custom-call(s32[2]{0:T(128)} %pad_add_fusion.edge_ref.refs_0_, s32[2]{0:T(128)} %nucleus_ref.1, ...), custom_call_target="tpu_custom_call" | custom-call | tf_op jit(solution)/shard_map/forward_one_two/pallas_call | solution.py:451
  58.8 18.0 %psum.63 = f32[2,64]{1,0:T(2,128)S(1)} all-reduce(f32[2,64]{1,0:T(2,128)S(1)} %reduce_sum.97), channel_id=1, replica_groups=mesh['img'=4,'tile'=8] {'tile'}, use_global_device_ids=true, to_apply=%region_1.2 | all-reduce | flops 128 | bytes 1024 | tf_op jit(solution)/shard_map/psum | solution.py:468
  77.9 39.4 %forward_three_back.1 = (f32[2,1152,512]{2,1,0:T(8,128)}, bf16[2,256,512]{2,1,0:T(8,128)(2,1)}, f32[128,576]{1,0:T(8,128)}, f32[16,128]{1,0:T(8,128)}, f32[16,12...) custom-call(s32[2]{0:T(128)} %pad_add_fusion.edge_ref.refs_0_, ...), custom_call_target="tpu_custom_call" | custom-call | tf_op jit(solution)/shard_map/forward_three_back/pallas_call | solution.py:477
  117.3 1.0 fusion.33
  118.4 13.8 %psum.65 = f32[2,32]{1,0:T(2,128)S(1)} all-reduce(f32[2,32]{1,0:T(2,128)S(1)} %reduce_sum.123), channel_id=1, replica_groups=mesh['img'=4,'tile'=8] {'tile'}, use_global_device_ids=true, to_apply=%region_7.8 | all-reduce | flops 64 | bytes 512 | tf_op jit(solution)/shard_map/psum | solution.py:505
  133.2 1.3 reshape.143
  134.5 1.2 convolution_bitcast_fusion.2
  135.8 2.7 convert.20
  138.5 1.8 collective-permute-start.4
  140.3 1.3 collective-permute-start.5
  146.0 21.3 %back_two_one.1 = (f32[64,288]{1,0:T(8,128)}, f32[128,32]{1,0:T(8,128)}, f32[64,128]{1,0:T(8,128)}, f32[128,128]{1,0:T(8,128)}) custom-call(f32[2,1152,512]{2,1,0:T(8,128)} %get-tuple-element.41.gc_ref, bf16[2,128,512]{2,1,0:T(8,128)(2,1)} %copy-done.3, bf16[2,128,512]{2,1,0:T(8,128)(2,1)} %copy-done.4, f32[2,64,1]{2,1,0:T(8,128)} %copy.188.raw_ref, ...), custom_call_target="tpu_custom_call" | custom-call | tf_op jit(solution)/shard_map/back_two_one/pallas_call | solution.py:516
  168.2 1.0 reduce_sum.126
  170.6 1.7 copy.199
  172.6 42.4 %all-reduce.4 = (f32[]{:T(128)}, f32[3,3,2,32]{3,1,2,0:T(4,128)S(1)}, f32[64,32]{0,1:T(8,128)S(1)}, f32[32,3]{0,1:T(4,128)S(1)}, f32[163]{0:T(256)S(1)}) all-reduce(f32[]{:T(128)} %reduce_sum.120, f32[3,3,2,32]{3,1,2,0:T(4,128)S(1)} %convolution_bitcast_fusion.8, ...), channel_id=1, replica_groups=mesh['img'=4,'tile'=8] {'img','tile'}, use_global_device_ids=true, to_apply=%region_4.5 | all-reduce | flops 2884 | bytes 23072 | tf_op jit(solution)/shard_map/psum | solution.py:545
  219.3 80.2 %all-reduce.8.cloned.1.call-done = (f32[3,3,32,64]{3,2,1,0:T(8,128)}, f32[3,3,64,32]{2,3,1,0:T(8,128)}) async-done(((f32[3,3,32,64]{3,2,1,0:T(8,128)}, f32[3,3,64,32]{2,3,1,0:T(8,128)}), (f32[3,3,32,64]{3,2,1,0:T(8,128)}, f32[3,3,64,32]{2,3,1,0:T(8,128)})) %all-reduce.8.cloned.1.call-update) | async-done | bytes 147472 | tf_op jit(solution)/shard_map/psum | solution.py:545
  299.5 1.7 divide_add_fusion.1
  301.3 1.7 divide_add_fusion
  (157 shorter events, 33.1 us)
Async XLA Ops:
  7.2 292.3 %all-reduce.8.cloned.1.call-start = ((), (), s32[]{:S(2)}) async-start(), calls=%async_computation | async-start | bytes 589824 | tf_op jit(solution)/shard_map/psum | solution.py:545
  8.2 32.0 %collective-permute-start = (bf16[2,2,7,1024]{3,2,1,0:T(8,128)(2,1)S(1)}, bf16[2,2,7,1024]{3,2,1,0:T(8,128)(2,1)S(1)}, u32[]{:S(2)}, u32[]{:S(2)}) collective-permute-start(bf16[2,2,7,1024]{3,2,1,0:T(8,128)(2,1)S(1)} %get-tuple-element.163), channel_id=1, source_target_pairs={{0,1},{1,2},{2,3},{3,4},{4,5},{5,6},{6,7},{8,9},{9,10},{10,11},{11... | collective-permute-start | bytes 172040 | tf_op jit(solution)/shard_map/ppermute | solution.py:382
  10.5 29.6 %collective-permute-start.1 = (bf16[2,2,7,1024]{3,2,1,0:T(8,128)(2,1)S(1)}, bf16[2,2,7,1024]{3,2,1,0:T(8,128)(2,1)S(1)}, u32[]{:S(2)}, u32[]{:S(2)}) collective-permute-start(bf16[2,2,7,1024]{3,2,1,0:T(8,128)(2,1)S(1)} %get-tuple-element.164), channel_id=1, source_target_pairs={{1,0},{2,1},{3,2},{4,3},{5,4},{6,5},{7,6},{9,8},{10,9},{11,10},{12... | collective-permute-start | bytes 172040 | tf_op jit(solution)/shard_map/ppermute | solution.py:382
  13.0 26.3 %collective-permute-start.2 = (bf16[2,2,2,1024]{3,2,1,0:T(2,128)(2,1)S(1)}, bf16[2,2,2,1024]{3,2,1,0:T(2,128)(2,1)S(1)}, u32[]{:S(2)}, u32[]{:S(2)}) collective-permute-start(bf16[2,2,2,1024]{3,2,1,0:T(2,128)(2,1)S(1)} %get-tuple-element.161), channel_id=1, source_target_pairs={{0,1},{1,2},{2,3},{3,4},{4,5},{5,6},{6,7},{8,9},{9,10},{10,11},{11... | collective-permute-start | bytes 49160 | tf_op jit(solution)/shard_map/ppermute | solution.py:382
  18.2 21.1 %collective-permute-start.3 = (bf16[2,2,2,1024]{3,2,1,0:T(2,128)(2,1)S(1)}, bf16[2,2,2,1024]{3,2,1,0:T(2,128)(2,1)S(1)}, u32[]{:S(2)}, u32[]{:S(2)}) collective-permute-start(bf16[2,2,2,1024]{3,2,1,0:T(2,128)(2,1)S(1)} %get-tuple-element.162), channel_id=1, source_target_pairs={{1,0},{2,1},{3,2},{4,3},{5,4},{6,5},{7,6},{9,8},{10,9},{11,10},{12... | collective-permute-start | bytes 49160 | tf_op jit(solution)/shard_map/ppermute | solution.py:382
  138.5 6.6 %collective-permute-start.4 = (bf16[2,128,512]{2,1,0:T(8,128)(2,1)S(1)}, bf16[2,128,512]{2,1,0:T(8,128)(2,1)S(1)}, u32[]{:S(2)}, u32[]{:S(2)}) collective-permute-start(bf16[2,128,512]{2,1,0:T(8,128)(2,1)S(1)} %bitcast.121), channel_id=1, source_target_pairs={{0,1},{1,2},{2,3},{3,4},{4,5},{5,6},{6,7},{8,9},{9,10},{10,11},{11... | collective-permute-start | bytes 786440 | tf_op jit(solution)/shard_map/ppermute | solution.py:382
  140.3 4.8 %collective-permute-start.5 = (bf16[2,128,512]{2,1,0:T(8,128)(2,1)S(1)}, bf16[2,128,512]{2,1,0:T(8,128)(2,1)S(1)}, u32[]{:S(2)}, u32[]{:S(2)}) collective-permute-start(bf16[2,128,512]{2,1,0:T(8,128)(2,1)S(1)} %bitcast.120), channel_id=1, source_target_pairs={{1,0},{2,1},{3,2},{4,3},{5,4},{6,5},{7,6},{9,8},{10,9},{11,10},{12... | collective-permute-start | bytes 786440 | tf_op jit(solution)/shard_map/ppermute | solution.py:382
  145.8 69.2 %copy-start.20 = (f32[32,3]{0,1:T(4,128)S(1)}, f32[32,3]{0,1:T(4,128)}, u32[]{:S(2)}) copy-start(f32[32,3]{0,1:T(4,128)} %param.50) | copy-start | bytes 1156
  145.8 69.2 %copy-start.25 = (f32[32,3]{0,1:T(4,128)S(1)}, f32[32,3]{0,1:T(4,128)}, u32[]{:S(2)}) copy-start(f32[32,3]{0,1:T(4,128)} %param.52) | copy-start | bytes 1156
  145.8 69.2 %copy-start.26 = (f32[32,3]{0,1:T(4,128)S(1)}, f32[32,3]{0,1:T(4,128)}, u32[]{:S(2)}) copy-start(f32[32,3]{0,1:T(4,128)} %param.51) | copy-start | bytes 1156
  145.8 69.7 %copy-start.10 = (f32[3,3,2,32]{3,2,1,0:T(2,128)S(1)}, f32[3,3,2,32]{3,2,1,0:T(2,128)}, u32[]{:S(2)}) copy-start(f32[3,3,2,32]{3,2,1,0:T(2,128)} %param.38) | copy-start | bytes 6916
  145.8 69.7 %copy-start.15 = (f32[3,3,2,32]{3,2,1,0:T(2,128)S(1)}, f32[3,3,2,32]{3,2,1,0:T(2,128)}, u32[]{:S(2)}) copy-start(f32[3,3,2,32]{3,2,1,0:T(2,128)} %param.40) | copy-start | bytes 6916
  145.8 69.7 %copy-start.16 = (f32[3,3,2,32]{3,2,1,0:T(2,128)S(1)}, f32[3,3,2,32]{3,2,1,0:T(2,128)}, u32[]{:S(2)}) copy-start(f32[3,3,2,32]{3,2,1,0:T(2,128)} %param.39) | copy-start | bytes 6916
  145.9 69.7 %copy-start.12 = (f32[64,32]{0,1:T(8,128)S(1)}, f32[64,32]{0,1:T(8,128)}, u32[]{:S(2)}) copy-start(f32[64,32]{0,1:T(8,128)} %param.49) | copy-start | bytes 24580
  145.9 69.7 %copy-start.13 = (f32[64,32]{0,1:T(8,128)S(1)}, f32[64,32]{0,1:T(8,128)}, u32[]{:S(2)}) copy-start(f32[64,32]{0,1:T(8,128)} %param.48) | copy-start | bytes 24580
  145.9 70.4 %copy-start.21 = (f32[163]{0:T(256)S(1)}, f32[163]{0:T(256)}, u32[]{:S(2)}) copy-start(f32[163]{0:T(256)} %param.53) | copy-start | bytes 1960
  145.9 70.4 %copy-start.27 = (f32[163]{0:T(256)S(1)}, f32[163]{0:T(256)}, u32[]{:S(2)}) copy-start(f32[163]{0:T(256)} %param.55) | copy-start | bytes 1960
  145.9 70.4 %copy-start.28 = (f32[163]{0:T(256)S(1)}, f32[163]{0:T(256)}, u32[]{:S(2)}) copy-start(f32[163]{0:T(256)} %param.54) | copy-start | bytes 1960
  145.9 153.6 %copy-start = (f32[3,3,32,64]{3,2,1,0:T(8,128)S(1)}, f32[3,3,32,64]{3,2,1,0:T(8,128)}, u32[]{:S(2)}) copy-start(f32[3,3,32,64]{3,2,1,0:T(8,128)} %param.41) | copy-start | bytes 221188
  145.9 153.6 %copy-start.5 = (f32[3,3,32,64]{3,2,1,0:T(8,128)S(1)}, f32[3,3,32,64]{3,2,1,0:T(8,128)}, u32[]{:S(2)}) copy-start(f32[3,3,32,64]{3,2,1,0:T(8,128)} %param.43) | copy-start | bytes 221188
  145.9 153.6 %copy-start.6 = (f32[3,3,32,64]{3,2,1,0:T(8,128)S(1)}, f32[3,3,32,64]{3,2,1,0:T(8,128)}, u32[]{:S(2)}) copy-start(f32[3,3,32,64]{3,2,1,0:T(8,128)} %param.42) | copy-start | bytes 221188
  167.2 134.0 %copy-start.1 = (f32[3,3,64,32]{2,3,1,0:T(8,128)S(1)}, f32[3,3,64,32]{2,3,1,0:T(8,128)}, u32[]{:S(2)}) copy-start(f32[3,3,64,32]{2,3,1,0:T(8,128)} %param.44) | copy-start | bytes 221188
  167.2 134.0 %copy-start.7 = (f32[3,3,64,32]{2,3,1,0:T(8,128)S(1)}, f32[3,3,64,32]{2,3,1,0:T(8,128)}, u32[]{:S(2)}) copy-start(f32[3,3,64,32]{2,3,1,0:T(8,128)} %param.46) | copy-start | bytes 221188
  167.3 134.0 %copy-start.8 = (f32[3,3,64,32]{2,3,1,0:T(8,128)S(1)}, f32[3,3,64,32]{2,3,1,0:T(8,128)}, u32[]{:S(2)}) copy-start(f32[3,3,64,32]{2,3,1,0:T(8,128)} %param.45) | copy-start | bytes 221188
  (13 other events, 167.1 us)
Sparse Core Ops, SparseCore 0:
  172.6 126.8 all-reduce.7

commit v2 on v1

v2 whole, which is shorter than its diff:
```python
import math

import jax
import jax.numpy as jnp
from jax import lax
from jax.experimental import pallas as pl
from jax.experimental.pallas import tpu as pltpu
from jax.sharding import PartitionSpec as P

CH_ONE = 32
CH_TWO = 64
OUT_CH = 3

momentum_rate = 0.9
learn_rate = 0.02
decay_rate = 0.0001
norm_eps = 1e-05
highest = lax.Precision.HIGHEST
f32 = jnp.float32
bf16 = jnp.bfloat16

HALO = 8
VMEM = pl.BlockSpec(memory_space=pltpu.VMEM)
SMEM = pl.BlockSpec(memory_space=pltpu.SMEM)
ANY = pl.BlockSpec(memory_space=pl.ANY)
MESH = pl.DeviceIdType.MESH
DMA = pltpu.SemaphoreType.DMA

PART_ROWS = (144, 160, 32, 16, 16, 8)


def dot(a, b):
    return jnp.dot(a, b, preferred_element_type=f32)


def dot_nt(a, b, precision=None):
    return lax.dot_general(a, b, (((1,), (1,)), ((), ())), preferred_element_type=f32, precision=precision)


def from_left(x):
    lane = lax.broadcasted_iota(jnp.int32, x.shape, 1)
    return jnp.where(lane == 0, 0.0, pltpu.roll(x, 1, 1))


def from_right(x):
    width = x.shape[1]
    lane = lax.broadcasted_iota(jnp.int32, x.shape, 1)
    return jnp.where(lane == width - 1, 0.0, pltpu.roll(x, width - 1, 1))


def turn(x, by, axis):
    by = by % x.shape[axis]
    return pltpu.roll(x, by, axis) if by else x


def lane_group(x, group, size=32):
    lane = lax.broadcasted_iota(jnp.int32, x.shape, 1)
    return jnp.where(lane // size == group, x, 0.0)


def over_phases(x):
    return (x + turn(x, 32, 1)) + (turn(x, 64, 1) + turn(x, 96, 1))


def as_column(row):
    return jnp.transpose(jnp.broadcast_to(row, (128, 128)))


def fold_lanes(x):
    total = x[:, 0:128]
    for k in range(1, x.shape[1] // 128):
        total = total + x[:, 128 * k : 128 * (k + 1)]
    return total


def wide(tile, width):
    return jnp.concatenate([tile] * (width // 128), axis=1)


def rows_of(ref, crop, start, size, align=16):
    return ref[crop, pl.ds(pl.multiple_of(start, align), size), :]


def put_lanes(ref, crop, start, size, value):
    for k in range(value.shape[1] // 128):
        ref[crop, k, pl.ds(pl.multiple_of(start, 8), size), :] = value[:, 128 * k : 128 * (k + 1)]


def get_lanes(ref, crop, start, size, stride=None):
    parts = []
    for k in range(ref.shape[1]):
        spot = pl.ds(start, size, stride=stride) if stride else pl.ds(pl.multiple_of(start, 8), size)
        parts.append(ref[crop, k, spot, :])
    return jnp.concatenate(parts, axis=1)


def valid(row, edge_ref):
    return jnp.where((row >= edge_ref[0]) & (row < edge_ref[1]), 1.0, 0.0).astype(f32)


def meet(sizes):
    gate = pltpu.get_barrier_semaphore()
    for axis, count in sizes:
        me = lax.axis_index(axis)
        for j in range(1, count):
            pl.semaphore_signal(gate, inc=1, device_id={axis: lax.rem(me + j, count)}, device_id_type=MESH)
    pl.semaphore_wait(gate, sum(count - 1 for _, count in sizes))


def send_all(count, axis, source, target, send_sem, recv_sem):
    me = lax.axis_index(axis)
    copies = []
    for j in range(1, count):
        to = lax.rem(me + j, count)
        copy = pltpu.make_async_remote_copy(
            src_ref=source(to), dst_ref=target, send_sem=send_sem.at[j - 1], recv_sem=recv_sem.at[j - 1],
            device_id={axis: to}, device_id_type=MESH,
        )
        copy.start()
        copies.append(copy)
    return copies


def in_order(ref, count):
    total = ref[0]
    for k in range(1, count):
        total = total + ref[k]
    return total


def meet_next(tiles):
    gate = pltpu.get_barrier_semaphore()
    me = lax.axis_index("tile")

    @pl.when(me > 0)
    def _():
        pl.semaphore_signal(gate, inc=1, device_id={"tile": me - 1}, device_id_type=MESH)

    @pl.when(me < tiles - 1)
    def _():
        pl.semaphore_signal(gate, inc=1, device_id={"tile": me + 1}, device_id_type=MESH)

    pl.semaphore_wait(gate, jnp.minimum(me, 1) + jnp.minimum(tiles - 1 - me, 1))


def swap_edges(tiles, pairs, send_sem, recv_sem):
    me = lax.axis_index("tile")
    copies = []
    for k, (low, high, from_before, from_after) in enumerate(pairs):
        down = pltpu.make_async_remote_copy(
            src_ref=high, dst_ref=from_before, send_sem=send_sem.at[2 * k], recv_sem=recv_sem.at[2 * k],
            device_id={"tile": jnp.minimum(me + 1, tiles - 1)}, device_id_type=MESH,
        )
        up = pltpu.make_async_remote_copy(
            src_ref=low, dst_ref=from_after, send_sem=send_sem.at[2 * k + 1], recv_sem=recv_sem.at[2 * k + 1],
            device_id={"tile": jnp.maximum(me - 1, 0)}, device_id_type=MESH,
        )
        copies.append((down, up))

    @pl.when(me < tiles - 1)
    def _():
        for down, _up in copies:
            down.start()

    @pl.when(me > 0)
    def _():
        for _down, up in copies:
            up.start()

    def finish():
        @pl.when(me < tiles - 1)
        def _():
            for down, up in copies:
                down.wait_send()
                up.wait_recv()

        @pl.when(me > 0)
        def _():
            for down, up in copies:
                up.wait_send()
                down.wait_recv()

    return finish


def halo_kernel(tiles, x_ref, t_ref, x_lo, x_hi, t_lo, t_hi, send_sem, recv_sem):
    meet_next(tiles)
    last = x_ref.shape[2] - HALO
    finish = swap_edges(
        tiles,
        [
            (ref.at[:, :, pl.ds(0, HALO), :], ref.at[:, :, pl.ds(last, HALO), :], lo, hi)
            for ref, lo, hi in ((x_ref, x_lo, x_hi), (t_ref, t_lo, t_hi))
        ],
        send_sem, recv_sem,
    )
    finish()


def sum_kernel(tiles, x_ref, o_ref, got, send_sem, recv_sem):
    me = lax.axis_index("tile")
    got[me] = x_ref[...]
    meet((("tile", tiles),))
    copies = send_all(tiles, "tile", lambda to: x_ref, got.at[me], send_sem, recv_sem)
    for copy in copies:
        copy.wait()
    o_ref[...] = in_order(got, tiles)


def sum_rim_kernel(tiles, x_ref, lo_ref, hi_ref, o_ref, up_ref, dn_ref, got, send_sem, recv_sem, rim_send, rim_recv):
    me = lax.axis_index("tile")
    got[me] = x_ref[...]
    meet((("tile", tiles),))
    finish = swap_edges(tiles, [(lo_ref, hi_ref, up_ref, dn_ref)], rim_send, rim_recv)
    copies = send_all(tiles, "tile", lambda to: x_ref, got.at[me], send_sem, recv_sem)
    for copy in copies:
        copy.wait()
    o_ref[...] = in_order(got, tiles)
    finish()


def reduce_kernel(
    tiles, images, part, k3_ref, k2_ref, k1_ref, head_ref, style_ref, sums_a, sums_b, o_ref,
    pay, got, own, met, full, send_one, recv_one, send_two, recv_two, send_three, recv_three,
):
    me, mine = lax.axis_index("tile"), lax.axis_index("img")
    start = 0
    for ref, rows in zip((k3_ref, k2_ref, k1_ref, head_ref, style_ref), PART_ROWS):
        pay[start : start + rows, :] = ref[...]
        start += rows
    pay[start : start + 8, :] = sums_a[...] + sums_b[...]
    start += 8
    if start < part * tiles:
        pay[start : part * tiles, :] = jnp.zeros((part * tiles - start, 128), f32)
    meet((("tile", tiles), ("img", images)))

    def block(ref, k):
        return ref.at[pl.ds(pl.multiple_of(k * part, 8), part), :]

    got[me] = pay[pl.ds(pl.multiple_of(me * part, 8), part), :]
    for copy in send_all(tiles, "tile", lambda to: block(pay, to), got.at[me], send_one, recv_one):
        copy.wait()
    own[...] = in_order(got, tiles)
    met[mine] = own[...]
    for copy in send_all(images, "img", lambda to: own, met.at[mine], send_two, recv_two):
        copy.wait()
    total = in_order(met, images)
    full[pl.ds(pl.multiple_of(me * part, 8), part), :] = total
    copies = send_all(tiles, "tile", lambda to: block(full, me), block(full, me), send_three, recv_three)
    for copy in copies:
        copy.wait()
    o_ref[...] = full[...]


def weight_kernel(
    k1_ref, k2_ref, k3_ref, kh_ref, bias_ref,
    w1_ref, w2_ref, w3_ref, wd3_ref, wd2_ref, wh_ref, wht_ref, b1_ref, b2_ref, bh_ref,
    base_ref,
):
    base_ref[...] = jnp.zeros_like(base_ref)
    for a in range(3):
        for b in range(3):
            for i in range(2):
                base_ref[8 * a + 4 * i + b : 8 * a + 4 * i + b + 1, 0:32] = k1_ref[a, b, i : i + 1, :]
    base = base_ref[...]
    w1t = jnp.zeros((32, 128), f32)
    for p in range(4):
        w1t = w1t + turn(turn(base, 8 * (p // 2) + p % 2, 0), 32 * p, 1)
    w1_ref[...] = jnp.transpose(w1t).astype(bf16)

    k2 = [[k2_ref[a, b].astype(bf16).astype(f32) for b in range(3)] for a in range(3)]
    w2t = jnp.concatenate([k2[a][b] for a in range(3) for b in range(3)], axis=0)
    w2_ref[...] = jnp.transpose(w2t).astype(bf16)
    wd2_ref[...] = jnp.concatenate([k2[2 - s][2 - t] for s in range(3) for t in range(3)], axis=1).astype(bf16)

    def tap_sum(first, second):
        total = None
        for a in first:
            for b in second:
                total = k3[a][b] if total is None else total + k3[a][b]
        return jnp.zeros((CH_TWO, CH_ONE), f32) if total is None else total

    k3 = [[k3_ref[a, b].astype(bf16).astype(f32) for b in range(3)] for a in range(3)]
    up = [[[a for a in range(3) if (p + a + 1) // 2 == r] for r in range(3)] for p in range(2)]
    w3t = jnp.concatenate(
        [
            jnp.concatenate([tap_sum(up[p // 2][r], up[p % 2][c]) for p in range(4)], axis=1)
            for r in range(3)
            for c in range(3)
        ],
        axis=0,
    )
    w3 = jnp.transpose(w3t)
    w3_hi = w3.astype(bf16)
    w3_ref[0:128, :] = w3_hi
    w3_ref[128:256, :] = (w3 - w3_hi.astype(f32)).astype(bf16)
    down = ((2,), (1, 2), (0, 1), (0,))
    wd3 = jnp.concatenate([tap_sum(down[r], down[c]) for r in range(4) for c in range(4)], axis=1)
    wd3_hi = wd3.astype(bf16)
    wd3_ref[0:64, :] = wd3_hi
    wd3_ref[64:128, :] = (wd3 - wd3_hi.astype(f32)).astype(bf16)

    kht = jnp.transpose(jnp.concatenate([kh_ref[...], jnp.zeros((CH_ONE, 5), f32)], axis=1))
    row = lax.broadcasted_iota(jnp.int32, (16, 128), 0)
    lane = lax.broadcasted_iota(jnp.int32, (16, 128), 1)
    wh = jnp.zeros((16, 128), f32)
    for o in range(OUT_CH):
        one = jnp.concatenate([kht[o : o + 1, :]] * 4, axis=1)
        wh = jnp.where(row // 4 == o, jnp.broadcast_to(one, (16, 128)), wh)
    wh = jnp.where(row % 4 == lane // 32, wh, 0.0)
    wh_ref[...] = wh.astype(bf16)
    wht_ref[...] = jnp.transpose(wh).astype(bf16)

    b1 = bias_ref[0:1, 0:32]
    b1_ref[...] = as_column(jnp.concatenate([b1] * 4, axis=1))
    b2 = bias_ref[0:1, 32:96]
    b2_ref[...] = as_column(jnp.concatenate([b2] * 2, axis=1))[0:64]
    bh = jnp.zeros((16, 128), f32)
    for o in range(OUT_CH):
        bh = jnp.where(row // 4 == o, jnp.broadcast_to(bias_ref[0:1, 160 + o : 161 + o], (16, 128)), bh)
    bh_ref[...] = bh


def split_columns(x, select):
    even, odd = [], []
    for k in range(x.shape[1] // 256):
        piece = dot(x[:, 256 * k : 256 * (k + 1)], select)
        even.append(piece[:, 0:128])
        odd.append(piece[:, 128:256])
    return jnp.concatenate(even, axis=1), jnp.concatenate(odd, axis=1)


def first_kernel(
    edge_ref, nucleus_ref, x_ref, x_lo, x_hi, t_ref, t_lo, t_hi, label_ref, w1_ref, b1_ref, w2_ref, b2_ref,
    y_ref, t_out, h1_ref, pool_ref, h2_ref, style_ref, x2_ref,
):
    crops = x_ref.shape[0]
    width = x_ref.shape[3] // 2
    rows = h2_ref.shape[1] // CH_TWO - 4
    height = 2 * rows
    top = 3
    r_id = lax.broadcasted_iota(jnp.int32, (256, 256), 0)
    c_id = lax.broadcasted_iota(jnp.int32, (256, 256), 1)
    select = jnp.where(r_id == 2 * (c_id % 128) + c_id // 128, 1.0, 0.0).astype(bf16)
    x_rows = 2 * (height + 2 * HALO)
    y_rows = y_ref.shape[1]
    ri = lax.broadcasted_iota(jnp.int32, (y_rows, 4 * x_rows), 0)
    ci = lax.broadcasted_iota(jnp.int32, (y_rows, 4 * x_rows), 1)
    fine = 2 * (ri // 16) + (ri // 8) % 2 - 7
    channel = (ri // 4) % 2
    source = jnp.where(
        fine < 0,
        channel * HALO + fine + HALO,
        jnp.where(
            fine < height,
            2 * HALO + channel * height + fine,
            2 * HALO + 2 * height + channel * HALO + fine - height,
        ),
    )
    perm_x = jnp.where(ci == (ri % 4) * x_rows + source, 1.0, 0.0).astype(bf16)
    t_rows = 3 * height + 4 * HALO
    ri = lax.broadcasted_iota(jnp.int32, (t_out.shape[2], 2 * t_rows), 0)
    ci = lax.broadcasted_iota(jnp.int32, (t_out.shape[2], 2 * t_rows), 1)
    part = (ri // 4) % 4
    fine = 2 * (ri // 16) + (ri // 2) % 2 - 2
    source = jnp.where(
        fine < 0,
        3 * height + part * HALO + fine + HALO,
        jnp.where(fine < height, part * height + fine, 3 * height + 2 * HALO + part * HALO + fine - height),
    )
    outside = (fine < 0) | (fine >= height)
    known = (part < 2) | ((part == 2) & jnp.logical_not(outside))
    perm_t = jnp.where((ci == (ri % 2) * t_rows + source) & known, 1.0, 0.0).astype(bf16)
    has_up, has_dn = edge_ref[0] < 0, edge_ref[1] > rows
    for c in range(crops):
        pieces = [jnp.where(has_up, x_lo[c, k].astype(f32), 0.0) for k in range(2)]
        pieces += [x_ref[c, k].astype(f32) for k in range(2)]
        pieces += [jnp.where(has_dn, x_hi[c, k].astype(f32), 0.0) for k in range(2)]
        even, odd = split_columns(jnp.concatenate(pieces, axis=0).astype(bf16), select)
        row = lax.broadcasted_iota(jnp.int32, (x_rows, width), 0)
        second = ((row >= HALO) & (row < 2 * HALO)) | (row >= x_rows - HALO)
        second = second | ((row >= 2 * HALO + height) & (row < 2 * HALO + 2 * height))
        gate = jnp.where(second, nucleus_ref[c].astype(f32), 1.0)
        even, odd = even * gate, odd * gate
        stack = jnp.concatenate([from_left(odd), even, odd, from_right(even)], axis=0)
        y_ref[c] = dot(perm_x, stack.astype(bf16)).astype(bf16)
        pieces = [t_ref[c, 0].astype(f32), t_ref[c, 1].astype(f32), label_ref[c].astype(f32)]
        pieces += [jnp.where(has_up, t_lo[c, k], 0).astype(f32) for k in range(2)]
        pieces += [jnp.where(has_dn, t_hi[c, k], 0).astype(f32) for k in range(2)]
        even, odd = split_columns(jnp.concatenate(pieces, axis=0).astype(bf16), select)
        put_lanes(t_out, c, 0, t_out.shape[2], dot(perm_t, jnp.concatenate([even, odd], axis=0).astype(bf16)))
    style_ref[...] = jnp.zeros_like(style_ref)
    ones = jnp.ones((8, width), bf16)

    def conv_one(k):
        row = k - top
        keep = valid(row, edge_ref)
        spot = jnp.clip(row + 1, 0, rows + 2)
        pre = [dot(w1_ref[...], rows_of(y_ref, c, k * 16, 32)) for c in range(crops)]
        for c in range(crops):
            hidden = (jnp.maximum(pre[c] + wide(b1_ref[...], width), 0.0) * keep).astype(bf16)
            h1_ref[c, pl.ds(pl.multiple_of(spot * 128, 128), 128), :] = hidden
            h = hidden.astype(f32)
            pooled = (0.25 * ((h[0:32] + h[32:64]) + (h[64:96] + h[96:128]))).astype(bf16)
            pool_ref[c, pl.ds(pl.multiple_of(spot * 32, 32), 32), :] = pooled
            p = pooled.astype(f32)
            both = jnp.concatenate([from_left(p).astype(bf16), pooled, from_right(p).astype(bf16)], axis=0)
            x2_ref[c, pl.ds(pl.multiple_of(k * 96, 96), 96), :] = both

    def conv_two(q):
        row = q - 2
        keep = valid(row, edge_ref)
        own = jnp.where((row >= 0) & (row < rows), 1.0, 0.0).astype(f32)
        pre = [dot(w2_ref[...], rows_of(x2_ref, c, q * 96, 288)) for c in range(crops)]
        for c in range(crops):
            hidden = (jnp.maximum(pre[c] + wide(b2_ref[...], width), 0.0) * keep).astype(bf16)
            h2_ref[c, pl.ds(pl.multiple_of(q * 64, 64), 64), :] = hidden
            style_ref[c : c + 1, 0:64] += dot_nt(ones, hidden)[0:1] * own

    def loop_one(k, carry):
        conv_one(k)
        return carry

    def loop_both(k, carry):
        conv_two(k - 3)
        conv_one(k)
        return carry

    lax.fori_loop(0, 3, loop_one, 0)
    lax.fori_loop(3, rows + 6, loop_both, 0)
    conv_two(rows + 3)


def second_kernel(
    scale, coarse_count,
    edge_ref, h1_ref, h2_ref, t_ref, total_ref, bias_ref, ws_ref, w3_ref, wh_ref, wht_ref, wd3_ref, bh_ref,
    gc_ref, rim_lo, rim_hi, go_out, k3_ref, head_ref, style_ref, sums_ref, sg_ref,
    x3_ref, h3_ref, m_ref, fe_ref, go_ref, g3_ref, d3_ref,
):
    crops = h1_ref.shape[0]
    width = h1_ref.shape[2]
    rows = go_out.shape[1] // 16

    def shift(k, carry):
        for c in range(crops):
            mid = rows_of(h2_ref, c, k * 64, 64)
            x = mid.astype(f32)
            x3_ref[c, pl.ds(pl.multiple_of(k * 192, 192), 192), :] = jnp.concatenate(
                [from_left(x).astype(bf16), mid, from_right(x).astype(bf16)], axis=0
            )
        return carry

    lax.fori_loop(0, rows + 4, shift, 0)
    raw = total_ref[:, 0:64] / coarse_count
    unit = raw * lax.rsqrt(jnp.mean(raw * raw, axis=1, keepdims=True) + norm_eps)
    vec = jnp.dot(unit, ws_ref[...], precision=highest, preferred_element_type=f32) + bias_ref[0:1, 128:160]
    vec = jnp.concatenate([vec + bias_ref[0:1, 96:128]] * 4, axis=1)
    bias3 = [as_column(vec[c : c + 1]) for c in range(crops)]
    ones = jnp.ones((8, width), bf16)

    def forward(k, carry):
        row = k - 1
        keep = valid(row, edge_ref)
        pre = [dot(w3_ref[...], rows_of(x3_ref, c, k * 192, 576)) for c in range(crops)]
        hs = []
        for c in range(crops):
            p = pre[c][0:128] + pre[c][128:256] + wide(bias3[c], width)
            h1 = rows_of(h1_ref, c, k * 128, 128).astype(f32)
            h3 = (jnp.maximum(p, 0.0) + h1).astype(bf16)
            h3_ref[c, pl.ds(pl.multiple_of(k * 128, 128), 128), :] = h3
            m_ref[c, pl.ds(pl.multiple_of(k * 128, 128), 128), :] = jnp.where(p > 0, 1.0, 0.0).astype(bf16)
            hs.append(h3)
        outs = [dot(wh_ref[...], h) for h in hs]
        for c in range(crops):
            o = outs[c] + wide(bh_ref[...], width)
            t = get_lanes(t_ref, c, k * 16, 16)
            fe = (o[0:8] - 0.25 * t[0:8]) * keep
            put_lanes(fe_ref, c, k * 16, 16, jnp.concatenate([fe, o[8:16]], axis=0))
        return carry

    lax.fori_loop(0, rows + 2, forward, 0)

    r_id = lax.broadcasted_iota(jnp.int32, (rows, width), 0)
    above = jnp.where(r_id - 1 >= edge_ref[0], 1.0, 0.0)
    below = jnp.where(r_id + 1 < edge_ref[1], 1.0, 0.0)
    loss = jnp.zeros((rows, 128), f32)
    go_ref[...] = jnp.zeros_like(go_ref)
    for c in range(crops):

        def at(part, off):
            return get_lanes(fe_ref, c, 16 * (1 + off) + part, rows, 16)

        def column_part(pr, off):
            odd, even = at(4 + 2 * pr + 1, off), at(4 + 2 * pr, off)
            return 0.5 * (odd - from_left(odd)), 0.5 * (from_right(even) - even)

        e0 = [at(k, 0) for k in range(4)]
        e1 = [at(4 + k, 0) for k in range(4)]
        cols0, cols1 = column_part(0, 0), column_part(1, 0)
        cols_up, cols_dn = column_part(1, -1), column_part(0, 1)
        spread = [None] * 4
        g_up, g_dn = [None] * 2, [None] * 2
        for pc in range(2):
            f_up, f_dn = at(2 + pc, -1), at(pc, 1)
            spread[pc] = 0.5 * (e0[2 + pc] - f_up) + cols0[pc]
            spread[2 + pc] = 0.5 * (f_dn - e0[pc]) + cols1[pc]
            g_up[pc] = 2.0 * scale * above * (0.5 * (e0[pc] - at(pc, -1)) + cols_up[pc])
            g_dn[pc] = 2.0 * scale * below * (0.5 * (at(2 + pc, 1) - e0[2 + pc]) + cols_dn[pc])
        g = [2.0 * scale * v for v in spread]
        for pr in range(2):
            even, odd = g[2 * pr], g[2 * pr + 1]
            col = [0.5 * (odd - from_left(odd)), 0.5 * (from_right(even) - even)]
            for pc in range(2):
                k = 2 * pr + pc
                if pr == 0:
                    row_part = 0.5 * (g[2 + pc] - g_up[pc])
                else:
                    row_part = 0.5 * (g_dn[pc] - g[pc])
                logit = at(8 + k, 0)
                label = get_lanes(t_ref, c, 16 + 8 + k, rows, 16)
                ex = jnp.exp(-jnp.abs(logit))
                sig = jnp.where(logit >= 0, 1.0, ex) / (1.0 + ex)
                grads = (2.0 * scale * e0[k] - row_part, 2.0 * scale * e1[k] - col[pc], scale * (sig - label))
                for part in range(OUT_CH):
                    for j in range(width // 128):
                        go_ref[c, j, pl.ds(4 * part + k, rows, stride=16), :] = grads[part][:, 128 * j : 128 * (j + 1)]
                term = jnp.maximum(logit, 0.0) + jnp.log1p(ex) - label * logit
                loss = loss + fold_lanes(e0[k] * e0[k] + e1[k] * e1[k] + spread[k] * spread[k] + term)
    sums_ref[...] = jnp.zeros_like(sums_ref)
    sums_ref[4:5, :] = jnp.sum(loss, axis=0, keepdims=True)
    head_ref[...] = jnp.zeros_like(head_ref)
    sg_ref[...] = jnp.zeros_like(sg_ref)
    d3_ref[...] = jnp.zeros_like(d3_ref)
    edge = jnp.zeros((256, width), bf16)
    for c in range(crops):
        for k in (0, 1, rows + 2, rows + 3):
            g3_ref[c, 256 * k : 256 * (k + 1), :] = edge

    def backward(r, carry):
        gos, gts = [], []
        for c in range(crops):
            go = get_lanes(go_ref, c, r * 16, 16).astype(bf16)
            go_out[c, pl.ds(pl.multiple_of(r * 16, 16), 16), :] = go
            gos.append(go)
            gts.append(dot(wht_ref[...], go))
        for c in range(crops):
            spot = (r + 1) * 128
            head_ref[...] += dot_nt(gos[c], rows_of(h3_ref, c, spot, 128))
            sums_ref[3:4, 0:16] += dot_nt(ones, gos[c])[0:1]
            g = gts[c].astype(bf16).astype(f32) * rows_of(m_ref, c, spot, 128).astype(f32)
            parts = []
            gb = g.astype(bf16)
            sg_ref[c : c + 1, :] += dot_nt(ones, gb)[0:1]
            for pr in range(2):
                even, odd = g[64 * pr : 64 * pr + 32], g[64 * pr + 32 : 64 * pr + 64]
                parts += [from_left(odd).astype(bf16), gb[64 * pr : 64 * pr + 64], from_right(even).astype(bf16)]
            g3_ref[c, pl.ds(pl.multiple_of((r + 2) * 256, 256), 256), :] = jnp.concatenate(parts, axis=0)
            d3_ref[...] += dot_nt(rows_of(x3_ref, c, (r + 1) * 192, 576), gb)
        return carry

    lax.fori_loop(0, rows, backward, 0)

    def down(k, carry):
        both = [dot(wd3_ref[...], rows_of(g3_ref, c, k * 256 + 128, 512)) for c in range(crops)]
        for c in range(crops):
            gc_ref[c, pl.ds(pl.multiple_of(k * 64, 64), 64), :] = both[c][0:64] + both[c][64:128]
        return carry

    lax.fori_loop(0, rows + 2, down, 0)
    for c in range(crops):
        rim_lo[c] = gc_ref[c, 0:128, :].astype(bf16)
        rim_hi[c] = gc_ref[c, 64 * rows : 64 * rows + 128, :].astype(bf16)

    for block in range(3):
        packed = jnp.zeros((CH_TWO, 128), f32)
        for tap in range(4 * block, min(4 * block + 4, 9)):
            a, b = tap // 3, tap % 3
            total = jnp.zeros((CH_TWO, 128), f32)
            for p in range(4):
                n = 3 * ((p // 2 + a + 1) // 2) + (p % 2 + b + 1) // 2
                total = total + turn(d3_ref[64 * n : 64 * (n + 1), :], 32 * (tap % 4 - p), 1)
            packed = packed + lane_group(total, tap % 4)
        if block < 2:
            k3_ref[64 * block : 64 * (block + 1), :] = packed
        else:
            last = packed[0:16]
            for k in range(1, 4):
                last = last + turn(packed[16 * k : 16 * (k + 1)], 32 * k, 1)
            k3_ref[128:144, :] = last
    outer = jnp.zeros((CH_TWO, 128), f32)
    for c in range(crops):
        column = as_column(jnp.concatenate([unit[c : c + 1]] * 2, axis=1))[0:64]
        outer = outer + column * over_phases(sg_ref[c : c + 1, :])
        sums_ref[2:3, :] += sg_ref[c : c + 1, :]
    packed = lane_group(outer[0:16], 0)
    for k in range(1, 4):
        packed = packed + lane_group(outer[16 * k : 16 * (k + 1)], k)
    style_ref[...] = packed


def third_kernel(
    coarse_count,
    edge_ref, gc_ref, up_ref, dn_ref, total_ref, sg_ref, ws_ref, h2_ref, pool_ref, h1_ref, y_ref, go_ref, wd2_ref, wht_ref,
    k2_ref, d1_ref, sums_ref,
    g2_ref, x2_ref, d2_ref,
):
    crops = h1_ref.shape[0]
    width = h1_ref.shape[2]
    rows = go_ref.shape[1] // 16
    style_raw = total_ref[:, 0:64] / coarse_count
    inv = lax.rsqrt(jnp.mean(style_raw * style_raw, axis=1, keepdims=True) + norm_eps)
    style_grad = over_phases(sg_ref[...])[:, 0:32]
    grad_unit = dot_nt(style_grad, ws_ref[...], highest)
    grad_raw = inv * grad_unit - inv * inv * inv * style_raw * jnp.mean(style_raw * grad_unit, axis=1, keepdims=True)
    grad_raw = jnp.concatenate([grad_raw / coarse_count] * 2, axis=1)
    raw = [as_column(grad_raw[c : c + 1])[0:64] for c in range(crops)]
    ones = jnp.ones((8, width), bf16)
    sums_ref[...] = jnp.zeros_like(sums_ref)
    d2_ref[...] = jnp.zeros_like(d2_ref)
    d1_ref[...] = jnp.zeros_like(d1_ref)

    def masked(k, c, extra, own):
        coarse = rows_of(gc_ref, c, k * 64, 64)
        if extra is not None:
            coarse = coarse + extra
        grad = (coarse + wide(raw[c], width)).astype(bf16)
        h2 = rows_of(h2_ref, c, (k + 1) * 64, 64).astype(f32)
        g = jnp.where(h2 > 0, grad.astype(f32), 0.0)
        gb = g.astype(bf16)
        if own:
            sums_ref[1:2, 0:64] += dot_nt(ones, gb)[0:1]
        g2_ref[c, pl.ds(pl.multiple_of(k * 192, 192), 192), :] = jnp.concatenate(
            [from_left(g).astype(bf16), gb, from_right(g).astype(bf16)], axis=0
        )

    def widen(k, carry):
        for c in range(crops):
            mid = rows_of(pool_ref, c, k * 32, 32)
            x = mid.astype(f32)
            x2_ref[c, pl.ds(pl.multiple_of(k * 96, 96), 96), :] = jnp.concatenate(
                [from_left(x).astype(bf16), mid, from_right(x).astype(bf16)], axis=0
            )
        return carry

    lax.fori_loop(0, rows + 2, widen, 0)
    for c in range(crops):
        up = jnp.where(edge_ref[0] < 0, up_ref[c].astype(f32), 0.0)
        dn = jnp.where(edge_ref[1] > rows, dn_ref[c].astype(f32), 0.0)
        masked(0, c, up[0:64], False)
        masked(1, c, up[64:128], True)
        masked(rows, c, dn[0:64], True)
        masked(rows + 1, c, dn[64:128], False)

    def inner(k, carry):
        for c in range(crops):
            masked(k, c, None, True)
        return carry

    lax.fori_loop(2, rows, inner, 0)

    def backward(r, carry):
        gps = [dot(wd2_ref[...], rows_of(g2_ref, c, r * 192, 576)) for c in range(crops)]
        gts = [dot(wht_ref[...], rows_of(go_ref, c, r * 16, 16)) for c in range(crops)]
        for c in range(crops):
            d2_ref[...] += dot_nt(rows_of(x2_ref, c, r * 96, 288), rows_of(g2_ref, c, (r + 1) * 192 + 64, 64))
            gp = 0.25 * gps[c].astype(bf16).astype(f32)
            g1 = (jnp.concatenate([gp] * 4, axis=0) + gts[c].astype(bf16).astype(f32)).astype(bf16).astype(f32)
            h1 = rows_of(h1_ref, c, (r + 1) * 128, 128).astype(f32)
            g1 = jnp.where(h1 > 0, g1, 0.0)
            gb = g1.astype(bf16)
            sums_ref[0:1, :] += dot_nt(ones, gb)[0:1]
            d1_ref[...] += dot_nt(rows_of(y_ref, c, (r + 3) * 16, 32), gb)
        return carry

    lax.fori_loop(0, rows, backward, 0)
    rest = jnp.concatenate([d2_ref[160:288, :], jnp.zeros((32, 64), f32)], axis=0)
    k2_ref[...] = jnp.concatenate([d2_ref[0:160, :], rest], axis=1)


def update_kernel(pixel_count, count_ref, sum_ref, *refs):
    olds, tail_ref, outs = refs[:15], refs[15], refs[16:]
    starts = [sum(PART_ROWS[:k]) for k in range(len(PART_ROWS))]
    rate = 1.0 / (jnp.zeros((8, 128), f32) + (count_ref[0].astype(f32) + 1.0))

    def step(index, spot, grad):
        weight, momentum, average = (olds[3 * index + k][spot] for k in range(3))
        decayed = grad + decay_rate * weight
        momentum = momentum_rate * momentum + decayed
        new = weight - learn_rate * (decayed + momentum_rate * momentum)
        outs[3 * index][spot] = new
        outs[3 * index + 1][spot] = momentum
        outs[3 * index + 2][spot] = average + (new - average) * rate[0:1, 0:1]

    d1 = sum_ref[starts[2] : starts[2] + 32, :]
    total = jnp.zeros((32, 128), f32)
    for p in range(4):
        total = total + turn(turn(d1, -32 * p, 1), -(8 * (p // 2) + p % 2), 0)
    for a in range(3):
        for b in range(3):
            for i in range(2):
                k = 8 * a + 4 * i + b
                step(0, (a, b, slice(i, i + 1), slice(None)), total[k : k + 1, 0:32])
    for tap in range(9):
        a, b = tap // 3, tap % 3
        first = starts[1] + 32 * (tap % 5)
        half = 64 * (tap // 5)
        step(1, (a, b), sum_ref[first : first + 32, half : half + 64])
        if tap < 8:
            first = starts[0] + 64 * (tap // 4)
            lane = 32 * (tap % 4)
            grad = sum_ref[first : first + 64, lane : lane + 32]
        else:
            first = starts[0] + 128
            grad = jnp.concatenate([sum_ref[first : first + 16, 32 * k : 32 * (k + 1)] for k in range(4)], axis=0)
        step(2, (a, b), grad)
    first = starts[4]
    grad = jnp.concatenate([sum_ref[first : first + 16, 32 * k : 32 * (k + 1)] for k in range(4)], axis=0)
    step(3, (slice(None), slice(None)), grad)
    head = sum_ref[starts[3] : starts[3] + 16, :]
    total = jnp.zeros((16, 128), f32)
    for p in range(4):
        total = total + turn(turn(head, -32 * p, 1), -p, 0)
    total = jnp.concatenate([total[4 * o : 4 * o + 1] for o in range(OUT_CH)] + [jnp.zeros((5, 128), f32)], axis=0)
    step(4, (slice(None), slice(None)), jnp.transpose(total)[0:32, 0:OUT_CH])
    sums = sum_ref[starts[5] : starts[5] + 8, :]
    one, three = over_phases(sums[0:1]), over_phases(sums[2:3])
    lane = lax.broadcasted_iota(jnp.int32, (1, 128), 1)
    low = jnp.where(lane < 32, one, jnp.where(lane < 96, turn(sums[1:2], 32, 1), three))
    ends = sums[3:4]
    ends = (ends + turn(ends, -1, 1)) + (turn(ends, -2, 1) + turn(ends, -3, 1))
    high = jnp.where(lane < 32, three, 0.0)
    for o in range(OUT_CH):
        high = jnp.where(lane == 32 + o, turn(ends, 32 + o - 4 * o, 1), high)
    tail_ref[...] = jnp.zeros_like(tail_ref)
    tail_ref[0:1, :] = jnp.concatenate([low, high], axis=1)
    tail_ref[1:2, 0:1] = jnp.sum(sums[4:5], axis=1, keepdims=True) / pixel_count


def nesterov(weight, gradient, momentum, average, count):
    decayed = gradient + decay_rate * weight
    momentum_new = momentum_rate * momentum + decayed
    weight_new = weight - learn_rate * (decayed + momentum_rate * momentum_new)
    average_new = average + (weight_new - average) / (count + 1.0)
    return (weight_new, momentum_new, average_new)


def on_device(
    images, nucleus, target_flow, cell_label, step_count,
    conv1_weight, conv1_momentum, conv1_average,
    conv2_weight, conv2_momentum, conv2_average,
    conv3_weight, conv3_momentum, conv3_average,
    style_weight, style_momentum, style_average,
    head_weight, head_momentum, head_average,
    biases, bias_momentum, bias_average,
):
    tiles = lax.axis_size("tile")
    me = lax.axis_index("tile")
    crops, _, height, cols = images.shape
    rows, width = height // 2, cols // 2
    pixel_count = lax.axis_size("img") * tiles * crops * height * cols
    grad_scale = 1.0 / math.sqrt(pixel_count)
    coarse_count = tiles * rows * width

    def sds(shape, dtype=f32):
        return jax.ShapeDtypeStruct(shape, dtype)

    def params(**more):
        return pltpu.CompilerParams(vmem_limit_bytes=60 * 2**20, **more)

    def remote(collective_id):
        return pltpu.CompilerParams(collective_id=collective_id, has_side_effects=True)

    images_count = lax.axis_size("img")
    edges = jnp.stack([-me * rows, (tiles - me) * rows]).astype(jnp.int32)
    bias_row = jnp.pad(biases.reshape(1, -1), ((0, 7), (0, 256 - biases.shape[0])))
    edge = (crops, 2, HALO, cols)
    x_lo, x_hi, t_lo, t_hi = pl.pallas_call(
        lambda *refs: halo_kernel(tiles, *refs),
        out_shape=(sds(edge, bf16), sds(edge, bf16), sds(edge, jnp.int32), sds(edge, jnp.int32)),
        in_specs=[ANY] * 2,
        out_specs=[ANY] * 4,
        scratch_shapes=[DMA((4,)), DMA((4,))],
        compiler_params=remote(1),
        name="halo",
    )(images, target_flow)
    w1, w2, w3, wd3, wd2, wh, wht, b1, b2, bh = pl.pallas_call(
        weight_kernel,
        out_shape=(
            sds((128, 32), bf16),
            sds((CH_TWO, 9 * CH_ONE), bf16),
            sds((256, 9 * CH_TWO), bf16),
            sds((128, 16 * CH_ONE), bf16),
            sds((CH_ONE, 9 * CH_TWO), bf16),
            sds((16, 128), bf16),
            sds((128, 16), bf16),
            sds((128, 128)),
            sds((64, 128)),
            sds((16, 128)),
        ),
        in_specs=[VMEM] * 5,
        out_specs=[VMEM] * 10,
        scratch_shapes=[pltpu.VMEM((32, 128), f32)],
        compiler_params=params(),
        name="weights",
    )(conv1_weight, conv2_weight, conv3_weight, head_weight, bias_row)

    y, targets, h1, pool, h2, style_part = pl.pallas_call(
        first_kernel,
        out_shape=(
            sds((crops, 16 * (rows + 7), width), bf16),
            sds((crops, width // 128, 16 * (rows + 2), 128)),
            sds((crops, 128 * (rows + 3), width), bf16),
            sds((crops, 32 * (rows + 3), width), bf16),
            sds((crops, 64 * (rows + 4), width), bf16),
            sds((8, 128)),
        ),
        in_specs=[SMEM, SMEM] + [VMEM] * 11,
        out_specs=[VMEM] * 6,
        scratch_shapes=[pltpu.VMEM((crops, 96 * (rows + 6), width), bf16)],
        compiler_params=params(),
        name="forward_one_two",
    )(edges, nucleus, images, x_lo, x_hi, target_flow, t_lo, t_hi, cell_label, w1, b1, w2, b2)

    style_total = pl.pallas_call(
        lambda *refs: sum_kernel(tiles, *refs),
        out_shape=sds((8, 128)),
        in_specs=[VMEM],
        out_specs=VMEM,
        scratch_shapes=[pltpu.VMEM((tiles, 8, 128), f32), DMA((tiles,)), DMA((tiles,))],
        compiler_params=remote(2),
        name="style_sum",
    )(style_part)

    rim = (crops, 128, width)
    gc, rim_lo, rim_hi, go, k3, head, style, sums_a, sg = pl.pallas_call(
        lambda *refs: second_kernel(grad_scale, float(coarse_count), *refs),
        out_shape=(
            sds((crops, 64 * (rows + 2), width)),
            sds(rim, bf16),
            sds(rim, bf16),
            sds((crops, 16 * rows, width), bf16),
            sds((144, 128)),
            sds((16, 128)),
            sds((16, 128)),
            sds((8, 128)),
            sds((8, 128)),
        ),
        in_specs=[SMEM] + [VMEM] * 11,
        out_specs=[VMEM] * 9,
        scratch_shapes=[
            pltpu.VMEM((crops, 192 * (rows + 4), width), bf16),
            pltpu.VMEM((crops, 128 * (rows + 2), width), bf16),
            pltpu.VMEM((crops, 128 * (rows + 2), width), bf16),
            pltpu.VMEM((crops, width // 128, 16 * (rows + 2), 128), f32),
            pltpu.VMEM((crops, width // 128, 16 * rows, 128), f32),
            pltpu.VMEM((crops, 256 * (rows + 4), width), bf16),
            pltpu.VMEM((9 * CH_TWO, 128), f32),
        ],
        compiler_params=params(),
        name="forward_three_back",
    )(edges, h1, h2, targets, style_total, bias_row, style_weight, w3, wh, wht, wd3, bh)

    sg_total, rim_up, rim_dn = pl.pallas_call(
        lambda *refs: sum_rim_kernel(tiles, *refs),
        out_shape=(sds((8, 128)), sds(rim, bf16), sds(rim, bf16)),
        in_specs=[VMEM, ANY, ANY],
        out_specs=[VMEM, ANY, ANY],
        scratch_shapes=[
            pltpu.VMEM((tiles, 8, 128), f32), DMA((tiles,)), DMA((tiles,)), DMA((2,)), DMA((2,)),
        ],
        compiler_params=remote(3),
        name="style_grad_sum",
    )(sg, rim_lo, rim_hi)

    k2, d1, sums_b = pl.pallas_call(
        lambda *refs: third_kernel(float(coarse_count), *refs),
        out_shape=(sds((160, 128)), sds((32, 128)), sds((8, 128))),
        in_specs=[SMEM] + [VMEM] * 13,
        out_specs=[VMEM] * 3,
        scratch_shapes=[
            pltpu.VMEM((crops, 192 * (rows + 2), width), bf16),
            pltpu.VMEM((crops, 96 * (rows + 2), width), bf16),
            pltpu.VMEM((9 * CH_ONE, CH_TWO), f32),
        ],
        compiler_params=params(),
        name="back_two_one",
    )(edges, gc, rim_up, rim_dn, style_total, sg_total, style_weight, h2, pool, h1, y, go, wd2, wht)

    part = 8 * pl.cdiv(sum(PART_ROWS), 8 * tiles)
    summed = pl.pallas_call(
        lambda *refs: reduce_kernel(tiles, images_count, part, *refs),
        out_shape=sds((part * tiles, 128)),
        in_specs=[VMEM] * 7,
        out_specs=VMEM,
        scratch_shapes=[
            pltpu.VMEM((part * tiles, 128), f32),
            pltpu.VMEM((tiles, part, 128), f32),
            pltpu.VMEM((part, 128), f32),
            pltpu.VMEM((images_count, part, 128), f32),
            pltpu.VMEM((part * tiles, 128), f32),
            DMA((tiles,)), DMA((tiles,)), DMA((images_count,)), DMA((images_count,)), DMA((tiles,)), DMA((tiles,)),
        ],
        compiler_params=remote(4),
        name="gradient_sum",
    )(k3, k2, d1, head, style, sums_a, sums_b)

    olds = (
        conv1_weight, conv1_momentum, conv1_average,
        conv2_weight, conv2_momentum, conv2_average,
        conv3_weight, conv3_momentum, conv3_average,
        style_weight, style_momentum, style_average,
        head_weight, head_momentum, head_average,
    )
    tail, *news = pl.pallas_call(
        lambda *refs: update_kernel(float(pixel_count), *refs),
        out_shape=(sds((8, 256)),) + tuple(sds(v.shape) for v in olds),
        in_specs=[SMEM] + [VMEM] * 16,
        out_specs=[VMEM] * 16,
        compiler_params=params(),
        name="update",
    )(step_count, summed, *olds)
    grad_bias = tail[0, 0 : biases.shape[0]]
    last = nesterov(biases, grad_bias, bias_momentum, bias_average, step_count[0].astype(f32))
    return (tail[1, 0:1], *news, *last)


def solution(mesh):
    return jax.shard_map(
        on_device,
        mesh=mesh,
        in_specs=(
            P("img", None, "tile", None),
            P("img"),
            P("img", None, "tile", None),
            P("img", "tile", None),
        )
        + (P(),) * 19,
        out_specs=(P(),) * 19,
        check_vma=False,
    )
```

time: 312 us -> 162 us (0.52)
  waiting for transfers between devices: 80.2 us -> 0 us
  blocking collectives: 74.2 us -> 0 us
  Pallas kernels: 77.4 us -> 133 us
  other arithmetic: 22.2 us -> 1.16 us
  between operations: 17.1 us -> 1.45 us
  starting transfers between devices: 13.3 us -> 0 us
  matrix products: 6.05 us -> 0 us
  local copies, waits for them, and re-layouts: 20.5 us -> 25.3 us
    psum x1 -> x0, waiting for transfers between devices: 80.2 us -> none  [on_device(): lax.psum((grad_kernel_one, grad_kernel_two, grad_kernel_three, grad_style...]
    psum x3 -> x0, blocking collectives: 74.2 us -> none  [the longest x1 42.4 us: on_device(): lax.psum((grad_kernel_one, grad_kernel_two, grad_kernel_three, grad_style...]
    pallas_call x2 -> x8, Pallas kernels: 60.6 us -> 112 us  [the longest x1 41.2 us: on_device(): pl.pallas_call(lambda *refs: second_kernel(grad_scale, float(coarse_count...]
    unnamed x63 -> x38, local copies, waits for them, and re-layouts: 2.72 us -> 22.1 us
    ppermute x6 -> x0, starting transfers between devices: 13.3 us -> none  [the longest x3 9.39 us: neighbours(): lax.ppermute(block_high, axis, forward)]
    dot_general x13 -> x0, matrix products: 6.05 us -> none  [the longest x2 1.8 us: on_device(): jnp.einsum('pra,qcb,abio->pqorci', SEL_UP, SEL_UP, k3.astype(f32), precis...]
    reshape x13 -> x0, local copies, waits for them, and re-layouts: 5.82 us -> none  [the longest x2 1.45 us: on_device(): b2 = bias_two.reshape(CH_TWO, 1)]
    reduce_sum x12 -> x0, other arithmetic: 4.92 us -> none  [the longest x2 1.07 us: on_device(): grad_bias_three = jnp.sum(style_grad_part, axis=0)]
  transfers between devices with their start and end apart: 7 -> 0, of which waited for: 1 -> 0; matrix products, arithmetic and copies ran while one was open for 9% -> 0% of each run, Pallas kernels for 0% -> 0%
where the time goes in v2:
time: 162 us; the launch traced here: 161 us
  Pallas kernels  133 us (82%)
  local copies, waits for them, and re-layouts  25.3 us (16%)
    pallas_call x1, Pallas kernels, on_device(): pl.pallas_call(lambda *refs: second_kernel(grad_scale, float(coarse_count...  41.2 us
    unnamed x38, local copies, waits for them, and re-layouts  22.1 us
    pallas_call x1, Pallas kernels, on_device(): pl.pallas_call(lambda *refs: third_kernel(float(coarse_count), *refs), ou...  21.7 us
    pallas_call x1, Pallas kernels, on_device(): pl.pallas_call(first_kernel, out_shape=(sds((crops, 16 * (rows + 7), widt...  20.7 us
    pallas_call x1, Pallas kernels, on_device(): pl.pallas_call(lambda *refs: reduce_kernel(tiles, images_count, part, *re...  19.2 us
    pallas_call x1, Pallas kernels, on_device(): pl.pallas_call(lambda *refs: sum_rim_kernel(tiles, *refs), out_shape=(sds...  10.2 us
    pallas_call x1, Pallas kernels, on_device(): pl.pallas_call(lambda *refs: sum_kernel(tiles, *refs), out_shape=sds((8,...  9.69 us
    pallas_call x1, Pallas kernels, on_device(): pl.pallas_call(lambda *refs: halo_kernel(tiles, *refs), out_shape=(sds(ed...  4.48 us

profile of v2, /device:TPU:0, one launch (start us, length us, event | category | flops | bytes accessed | tf_op | source)
XLA Modules:
  0.0 160.9 jit_solution(8436663570414384307)
XLA Ops:
  0.7 1.8 %copy.42.k3_ref.refs_8_ = f32[3,3,64,32]{3,2,1,0:T(8,128)} copy(f32[3,3,64,32]{2,3,1,0:T(8,128)} %param.34) | data formatting | bytes 147456 | tf_op args[11]
  2.5 1.4 copy.43.kh_ref.refs_14_
  3.8 1.3 pad.4.bias_ref.refs_5_
  5.1 2.4 %weights.1 = (bf16[128,32]{1,0:T(8,128)(2,1)}, bf16[64,288]{1,0:T(8,128)(2,1)}, bf16[256,576]{1,0:T(8,128)(2,1)}, bf16[128,512]{1,0:T(8,128)(2,1)}, bf16[32,576]...) custom-call(f32[3,3,2,32]{3,2,1,0:T(2,128)} %refs_2_.1, ...), custom_call_target="tpu_custom_call" | custom-call | tf_op jit(solution)/shard_map/weights/pallas_call | solution.py:786
  8.1 4.5 %halo.1 = (bf16[2,2,8,1024]{3,2,1,0:T(8,128)(2,1)}, bf16[2,2,8,1024]{3,2,1,0:T(8,128)(2,1)}, s32[2,2,8,1024]{3,2,1,0:T(8,128)}, s32[2,2,8,1024]{3,2,1,0:T(8,128)}) custom-call(bf16[2,2,32,1024]{3,2,1,0:T(8,128)(2,1)} %x_ref.1, s32[2,2,32,1024]{3,2,1,0:T(8,128)} %t_ref.1), custom_call_target="tpu_custom_call" | custom-call | tf_op jit(solution)/shard_map/halo/pallas_call | solution.py:777
  12.6 20.7 %forward_one_two.1 = (bf16[2,368,512]{2,1,0:T(8,128)(2,1)}, f32[2,4,288,128]{3,2,1,0:T(8,128)}, bf16[2,2432,512]{2,1,0:T(8,128)(2,1)}, bf16[2,608,512]{2,1,0:T(8...) custom-call(s32[2]{0:T(128)} %pad_add_fusion.edge_ref.refs_0_, s32[2]{0:T(128)} %nucleus_ref.1, ...), custom_call_target="tpu_custom_call" | custom-call | tf_op jit(solution)/shard_map/forward_one_two/pallas_call | solution.py:807
  33.3 9.7 %style_sum.1.refs_4_ = f32[8,128]{1,0:T(8,128)} custom-call(f32[8,128]{1,0:T(8,128)} %get-tuple-element.81.refs_0_), custom_call_target="tpu_custom_call" | custom-call | tf_op jit(solution)/shard_map/style_sum/pallas_call | solution.py:824
  43.7 41.2 %forward_three_back.1 = (f32[2,1152,512]{2,1,0:T(8,128)}, bf16[2,128,512]{2,1,0:T(8,128)(2,1)}, bf16[2,128,512]{2,1,0:T(8,128)(2,1)}, bf16[2,256,512]{2,1,0:T(8,...) custom-call(s32[2]{0:T(128)} %pad_add_fusion.edge_ref.refs_0_, ...), custom_call_target="tpu_custom_call" | custom-call | tf_op jit(solution)/shard_map/forward_three_back/pallas_call | solution.py:835
  84.9 10.2 %style_grad_sum.1 = (f32[8,128]{1,0:T(8,128)}, bf16[2,128,512]{2,1,0:T(8,128)(2,1)}, bf16[2,128,512]{2,1,0:T(8,128)(2,1)}) custom-call(f32[8,128]{1,0:T(8,128)} %get-tuple-element.89.refs_0_, bf16[2,128,512]{2,1,0:T(8,128)(2,1)} %get-tuple-element.90.refs_1_, bf16[2,128,512]{2,1,0:T(8,128)(2,1)} %get-tuple-element.91.refs_2_), custom_call_target="tpu_custom_call" | custom-call | tf_op jit(solution)/shard_map/style_grad_sum/pallas_call | solution.py:863
  95.2 21.7 %back_two_one.1 = (f32[160,128]{1,0:T(8,128)}, f32[32,128]{1,0:T(8,128)}, f32[8,128]{1,0:T(8,128)}) custom-call(s32[2]{0:T(128)} %pad_add_fusion.edge_ref.refs_0_, f32[2,1152,512]{2,1,0:T(8,128)} %get-tuple-element.88.refs_1_, bf16[2,128,512]{2,1,0:T(8,128)(2,1)} %get-tuple-element.92.refs_2_, bf16[2,128,512]{2,1,0:T(8,128)(2,1)} %get-tuple-element.93.refs_3_, ...), custom_call_target="tpu_custom_call" | custom-call | tf_op jit(solution)/shard_map/back_two_one/pallas_call | solution.py:875
  116.9 19.2 %gradient_sum.1.refs_1_ = f32[384,128]{1,0:T(8,128)} custom-call(f32[144,128]{1,0:T(8,128)} %get-tuple-element.87.refs_0_, f32[160,128]{1,0:T(8,128)} %get-tuple-element.99.refs_1_, f32[32,128]{1,0:T(8,128)} %get-tuple-element.100.refs_2_, f32[16,128]{1,0:T(8,128)} %get-tuple-element.101.refs_3_, f32[16,128]{1,0:T(8,128)} %get-tuple-element.102.refs_4_, ...), custom_call_target="tpu_custom_call" | custom-call | tf_op jit(solution)/shard_map/gradient_sum/pallas_call | solution.py:890
  136.7 0.9 copy.47.refs_9_
  137.6 0.9 copy.48.refs_10_
  141.2 3.4 %update.1 = (f32[8,256]{1,0:T(8,128)}, f32[3,3,2,32]{3,2,1,0:T(2,128)}, f32[3,3,2,32]{3,2,1,0:T(2,128)}, f32[3,3,2,32]{3,2,1,0:T(2,128)}, f32[3,3,32,64]{3,2,1,0...) custom-call(s32[1]{0:T(128)S(6)} %copy.64.refs_0_, ...), custom_call_target="tpu_custom_call" | custom-call | tf_op jit(solution)/shard_map/update/pallas_call | solution.py:914
  144.7 1.8 %copy.55 = f32[3,3,64,32]{2,3,1,0:T(8,128)} copy(f32[3,3,64,32]{3,2,1,0:T(8,128)} %get-tuple-element.128) | data formatting | bytes 147456
  146.5 1.8 %copy.56 = f32[3,3,64,32]{2,3,1,0:T(8,128)} copy(f32[3,3,64,32]{3,2,1,0:T(8,128)} %get-tuple-element.129) | data formatting | bytes 147456
  148.2 1.8 %copy.57 = f32[3,3,64,32]{2,3,1,0:T(8,128)} copy(f32[3,3,64,32]{3,2,1,0:T(8,128)} %get-tuple-element.130) | data formatting | bytes 147456
  150.0 1.4 copy.58
  151.4 1.4 copy.59
  152.9 1.4 copy.60
  155.6 1.4 copy.61
  157.0 1.4 copy.62
  158.3 1.4 copy.63
  159.7 1.2 slice.6
  (28 shorter events, 5.4 us)
Async XLA Ops:
  0.7 42.3 %copy-start.2 = (f32[64,32]{0,1:T(8,128)S(1)}, f32[64,32]{0,1:T(8,128)}, u32[]{:S(2)}) copy-start(f32[64,32]{0,1:T(8,128)} %param.37) | copy-start | bytes 24580
  95.1 41.6 %copy-start = (f32[3,3,64,32]{2,3,1,0:T(8,128)S(1)}, f32[3,3,64,32]{2,3,1,0:T(8,128)}, u32[]{:S(2)}) copy-start(f32[3,3,64,32]{2,3,1,0:T(8,128)} %param.35) | copy-start | bytes 221188
  95.1 42.4 %copy-start.1 = (f32[3,3,64,32]{2,3,1,0:T(8,128)S(1)}, f32[3,3,64,32]{2,3,1,0:T(8,128)}, u32[]{:S(2)}) copy-start(f32[3,3,64,32]{2,3,1,0:T(8,128)} %param.36) | copy-start | bytes 221188
  95.2 43.3 %copy-start.3 = (f32[64,32]{0,1:T(8,128)S(1)}, f32[64,32]{0,1:T(8,128)}, u32[]{:S(2)}) copy-start(f32[64,32]{0,1:T(8,128)} %param.38) | copy-start | bytes 24580
  95.2 44.0 %copy-start.4 = (f32[64,32]{0,1:T(8,128)S(1)}, f32[64,32]{0,1:T(8,128)}, u32[]{:S(2)}) copy-start(f32[64,32]{0,1:T(8,128)} %param.39) | copy-start | bytes 24580
  95.2 44.7 %copy-start.6 = (f32[32,3]{0,1:T(4,128)S(1)}, f32[32,3]{0,1:T(4,128)}, u32[]{:S(2)}) copy-start(f32[32,3]{0,1:T(4,128)} %param.41) | copy-start | bytes 1156
  95.2 45.4 %copy-start.7 = (f32[32,3]{0,1:T(4,128)S(1)}, f32[32,3]{0,1:T(4,128)}, u32[]{:S(2)}) copy-start(f32[32,3]{0,1:T(4,128)} %param.42) | copy-start | bytes 1156
  116.9 38.1 %copy-start.5 = (f32[163]{0:T(256)S(1)}, f32[163]{0:T(256)}, u32[]{:S(2)}) copy-start(f32[163]{0:T(256)} %param.43) | copy-start | bytes 1960
  116.9 38.1 %copy-start.8 = (f32[163]{0:T(256)S(1)}, f32[163]{0:T(256)}, u32[]{:S(2)}) copy-start(f32[163]{0:T(256)} %param.45) | copy-start | bytes 1960
  116.9 38.1 %copy-start.9 = (f32[163]{0:T(256)S(1)}, f32[163]{0:T(256)}, u32[]{:S(2)}) copy-start(f32[163]{0:T(256)} %param.44) | copy-start | bytes 1960

commit v3 on v2

v3 whole, which is shorter than its diff:
```python
import math

import jax
import jax.numpy as jnp
from jax import lax
from jax.experimental import pallas as pl
from jax.experimental.pallas import tpu as pltpu
from jax.sharding import PartitionSpec as P

CH_ONE = 32
CH_TWO = 64
OUT_CH = 3

momentum_rate = 0.9
learn_rate = 0.02
decay_rate = 0.0001
norm_eps = 1e-05
highest = lax.Precision.HIGHEST
f32 = jnp.float32
bf16 = jnp.bfloat16

HALO = 8
VMEM = pl.BlockSpec(memory_space=pltpu.VMEM)
SMEM = pl.BlockSpec(memory_space=pltpu.SMEM)
ANY = pl.BlockSpec(memory_space=pl.ANY)
MESH = pl.DeviceIdType.MESH
DMA = pltpu.SemaphoreType.DMA

PART_ROWS = (144, 160, 32, 16, 16, 8)


def dot(a, b):
    return jnp.dot(a, b, preferred_element_type=f32)


def dot_nt(a, b, precision=None):
    return lax.dot_general(a, b, (((1,), (1,)), ((), ())), preferred_element_type=f32, precision=precision)


def from_left(x, crops=1):
    lane = lax.broadcasted_iota(jnp.int32, x.shape, 1)
    return jnp.where(lane % (x.shape[1] // crops) == 0, 0.0, pltpu.roll(x, 1, 1))


def from_right(x, crops=1):
    width = x.shape[1] // crops
    lane = lax.broadcasted_iota(jnp.int32, x.shape, 1)
    return jnp.where(lane % width == width - 1, 0.0, pltpu.roll(x, x.shape[1] - 1, 1))


def three_columns(mid, crops):
    x = mid.astype(f32)
    return jnp.concatenate([from_left(x, crops).astype(bf16), mid, from_right(x, crops).astype(bf16)], axis=0)


def crop_rows(crops, lanes):
    row = lax.broadcasted_iota(jnp.int32, (8, lanes), 0)
    lane = lax.broadcasted_iota(jnp.int32, (8, lanes), 1)
    return jnp.where(lane // (lanes // crops) == row, 1.0, 0.0).astype(bf16)


def repeat_rows(count, step, body):
    def run(k, carry):
        body([k * step + j for j in range(step)])
        return carry

    lax.fori_loop(0, count // step, run, 0)


def turn(x, by, axis):
    by = by % x.shape[axis]
    return pltpu.roll(x, by, axis) if by else x


def lane_group(x, group, size=32):
    lane = lax.broadcasted_iota(jnp.int32, x.shape, 1)
    return jnp.where(lane // size == group, x, 0.0)


def over_phases(x):
    return (x + turn(x, 32, 1)) + (turn(x, 64, 1) + turn(x, 96, 1))


def as_column(row):
    return jnp.transpose(jnp.broadcast_to(row, (128, 128)))


def fold_lanes(x):
    total = x[:, 0:128]
    for k in range(1, x.shape[1] // 128):
        total = total + x[:, 128 * k : 128 * (k + 1)]
    return total


def wide(tile, width):
    return jnp.concatenate([tile] * (width // 128), axis=1)


def rows_of(ref, start, size):
    return ref[pl.ds(pl.multiple_of(start, 16), size), :]


def put_rows(ref, start, value):
    ref[pl.ds(pl.multiple_of(start, 16), value.shape[0]), :] = value


def put_lanes(ref, start, value):
    for k in range(value.shape[1] // 128):
        ref[k, pl.ds(pl.multiple_of(start, 16), value.shape[0]), :] = value[:, 128 * k : 128 * (k + 1)]


def get_lanes(ref, start, size, stride=None):
    spot = pl.ds(start, size, stride=stride) if stride else pl.ds(pl.multiple_of(start, 16), size)
    return jnp.concatenate([ref[k, spot, :] for k in range(ref.shape[0])], axis=1)


def strip_edges(tiles, rows):
    me = lax.axis_index("tile")
    return -me * rows, (tiles - me) * rows


def valid(row, edge):
    return jnp.where((row >= edge[0]) & (row < edge[1]), 1.0, 0.0).astype(f32)


def meet(sizes):
    gate = pltpu.get_barrier_semaphore()
    for axis, count in sizes:
        me = lax.axis_index(axis)
        for j in range(1, count):
            pl.semaphore_signal(gate, inc=1, device_id={axis: lax.rem(me + j, count)}, device_id_type=MESH)
    pl.semaphore_wait(gate, sum(count - 1 for _, count in sizes))


def send_all(count, axis, source, target, send_sem, recv_sem):
    me = lax.axis_index(axis)
    copies = []
    for j in range(1, count):
        to = lax.rem(me + j, count)
        copy = pltpu.make_async_remote_copy(
            src_ref=source(to), dst_ref=target, send_sem=send_sem.at[j - 1], recv_sem=recv_sem.at[j - 1],
            device_id={axis: to}, device_id_type=MESH,
        )
        copy.start()
        copies.append(copy)
    return copies


def in_order(ref, count):
    total = ref[0]
    for k in range(1, count):
        total = total + ref[k]
    return total


def meet_next(tiles):
    gate = pltpu.get_barrier_semaphore()
    me = lax.axis_index("tile")

    @pl.when(me > 0)
    def _():
        pl.semaphore_signal(gate, inc=1, device_id={"tile": me - 1}, device_id_type=MESH)

    @pl.when(me < tiles - 1)
    def _():
        pl.semaphore_signal(gate, inc=1, device_id={"tile": me + 1}, device_id_type=MESH)

    pl.semaphore_wait(gate, jnp.minimum(me, 1) + jnp.minimum(tiles - 1 - me, 1))


def swap_edges(tiles, pairs, send_sem, recv_sem):
    me = lax.axis_index("tile")
    copies = []
    for k, (low, high, from_before, from_after) in enumerate(pairs):
        down = pltpu.make_async_remote_copy(
            src_ref=high, dst_ref=from_before, send_sem=send_sem.at[2 * k], recv_sem=recv_sem.at[2 * k],
            device_id={"tile": jnp.minimum(me + 1, tiles - 1)}, device_id_type=MESH,
        )
        up = pltpu.make_async_remote_copy(
            src_ref=low, dst_ref=from_after, send_sem=send_sem.at[2 * k + 1], recv_sem=recv_sem.at[2 * k + 1],
            device_id={"tile": jnp.maximum(me - 1, 0)}, device_id_type=MESH,
        )
        copies.append((down, up))

    @pl.when(me < tiles - 1)
    def _():
        for down, _up in copies:
            down.start()

    @pl.when(me > 0)
    def _():
        for _down, up in copies:
            up.start()

    def finish():
        @pl.when(me < tiles - 1)
        def _():
            for down, up in copies:
                down.wait_send()
                up.wait_recv()

        @pl.when(me > 0)
        def _():
            for down, up in copies:
                up.wait_send()
                down.wait_recv()

    return finish


def halo_kernel(tiles, x_ref, t_ref, x_lo, x_hi, t_lo, t_hi, send_sem, recv_sem):
    meet_next(tiles)
    last = x_ref.shape[2] - HALO
    finish = swap_edges(
        tiles,
        [
            (ref.at[:, :, pl.ds(0, HALO), :], ref.at[:, :, pl.ds(last, HALO), :], lo, hi)
            for ref, lo, hi in ((x_ref, x_lo, x_hi), (t_ref, t_lo, t_hi))
        ],
        send_sem, recv_sem,
    )
    finish()


def sum_kernel(tiles, x_ref, o_ref, got, send_sem, recv_sem):
    me = lax.axis_index("tile")
    got[me] = x_ref[...]
    meet((("tile", tiles),))
    copies = send_all(tiles, "tile", lambda to: x_ref, got.at[me], send_sem, recv_sem)
    for copy in copies:
        copy.wait()
    o_ref[...] = in_order(got, tiles)


def sum_rim_kernel(tiles, x_ref, lo_ref, hi_ref, o_ref, up_ref, dn_ref, got, send_sem, recv_sem, rim_send, rim_recv):
    me = lax.axis_index("tile")
    got[me] = x_ref[...]
    meet((("tile", tiles),))
    finish = swap_edges(tiles, [(lo_ref, hi_ref, up_ref, dn_ref)], rim_send, rim_recv)
    copies = send_all(tiles, "tile", lambda to: x_ref, got.at[me], send_sem, recv_sem)
    for copy in copies:
        copy.wait()
    o_ref[...] = in_order(got, tiles)
    finish()


def reduce_kernel(
    tiles, images, part, k3_ref, k2_ref, k1_ref, head_ref, style_ref, sums_a, sums_b, o_ref,
    pay, got, own, met, full, send_one, recv_one, send_two, recv_two, send_three, recv_three,
):
    me, mine = lax.axis_index("tile"), lax.axis_index("img")
    start = 0
    for ref, rows in zip((k3_ref, k2_ref, k1_ref, head_ref, style_ref), PART_ROWS):
        pay[start : start + rows, :] = ref[...]
        start += rows
    pay[start : start + 8, :] = sums_a[...] + sums_b[...]
    start += 8
    if start < part * tiles:
        pay[start : part * tiles, :] = jnp.zeros((part * tiles - start, 128), f32)
    meet((("tile", tiles), ("img", images)))

    def block(ref, k):
        return ref.at[pl.ds(pl.multiple_of(k * part, 8), part), :]

    got[me] = pay[pl.ds(pl.multiple_of(me * part, 8), part), :]
    for copy in send_all(tiles, "tile", lambda to: block(pay, to), got.at[me], send_one, recv_one):
        copy.wait()
    own[...] = in_order(got, tiles)
    met[mine] = own[...]
    for copy in send_all(images, "img", lambda to: own, met.at[mine], send_two, recv_two):
        copy.wait()
    total = in_order(met, images)
    full[pl.ds(pl.multiple_of(me * part, 8), part), :] = total
    copies = send_all(tiles, "tile", lambda to: block(full, me), block(full, me), send_three, recv_three)
    for copy in copies:
        copy.wait()
    o_ref[...] = full[...]


def weight_kernel(
    k1_ref, k2_ref, k3_ref, kh_ref, bias_ref,
    w1_ref, w2_ref, w3_ref, wd3_ref, wd2_ref, wh_ref, wht_ref, b1_ref, b2_ref, b3_ref, bh_ref,
    base_ref,
):
    base_ref[...] = jnp.zeros_like(base_ref)
    for a in range(3):
        for b in range(3):
            for i in range(2):
                base_ref[8 * a + 4 * i + b : 8 * a + 4 * i + b + 1, 0:32] = k1_ref[a, b, i : i + 1, :]
    base = base_ref[...]
    w1t = jnp.zeros((32, 128), f32)
    for p in range(4):
        w1t = w1t + turn(turn(base, 8 * (p // 2) + p % 2, 0), 32 * p, 1)
    w1_ref[...] = jnp.transpose(w1t).astype(bf16)

    k2 = [[k2_ref[a, b].astype(bf16).astype(f32) for b in range(3)] for a in range(3)]
    w2t = jnp.concatenate([k2[a][b] for a in range(3) for b in range(3)], axis=0)
    w2_ref[...] = jnp.transpose(w2t).astype(bf16)
    wd2_ref[...] = jnp.concatenate([k2[2 - s][2 - t] for s in range(3) for t in range(3)], axis=1).astype(bf16)

    def tap_sum(first, second):
        total = None
        for a in first:
            for b in second:
                total = k3[a][b] if total is None else total + k3[a][b]
        return jnp.zeros((CH_ONE, CH_TWO), f32) if total is None else total

    k3 = [[k3_ref[a, b].astype(bf16).astype(f32) for b in range(3)] for a in range(3)]
    up = [[[a for a in range(3) if (p + a + 1) // 2 == r] for r in range(3)] for p in range(2)]
    for p in range(4):
        w3 = jnp.concatenate([tap_sum(up[p // 2][r], up[p % 2][c]) for r in range(3) for c in range(3)], axis=1)
        w3_hi = w3.astype(bf16)
        w3_ref[32 * p : 32 * (p + 1), :] = w3_hi
        w3_ref[128 + 32 * p : 160 + 32 * p, :] = (w3 - w3_hi.astype(f32)).astype(bf16)
    down = ((2,), (1, 2), (0, 1), (0,))
    wd3 = jnp.transpose(jnp.concatenate([tap_sum(down[r], down[c]) for r in range(4) for c in range(4)], axis=0))
    wd3_hi = wd3.astype(bf16)
    wd3_ref[0:64, :] = wd3_hi
    wd3_ref[64:128, :] = (wd3 - wd3_hi.astype(f32)).astype(bf16)

    row = lax.broadcasted_iota(jnp.int32, (16, 128), 0)
    lane = lax.broadcasted_iota(jnp.int32, (16, 128), 1)
    wh = jnp.zeros((16, 128), f32)
    for o in range(OUT_CH):
        one = jnp.concatenate([kh_ref[o : o + 1, :]] * 4, axis=1)
        wh = jnp.where(row // 4 == o, jnp.broadcast_to(one, (16, 128)), wh)
    wh = jnp.where(row % 4 == lane // 32, wh, 0.0)
    wh_ref[...] = wh.astype(bf16)
    wht_ref[...] = jnp.transpose(wh).astype(bf16)

    bias = bias_ref[...].reshape(1, -1)
    b1 = bias[:, 0:32]
    b1_ref[...] = as_column(jnp.concatenate([b1] * 4, axis=1))
    b2 = bias[:, 32:96]
    b2_ref[...] = as_column(jnp.concatenate([b2] * 2, axis=1))[0:64]
    b3_ref[...] = jnp.zeros_like(b3_ref)
    b3_ref[0:1, :] = jnp.concatenate([bias[:, 96:128] + bias[:, 128:160]] * 4, axis=1)
    bh = jnp.zeros((16, 128), f32)
    for o in range(OUT_CH):
        bh = jnp.where(row // 4 == o, jnp.broadcast_to(bias[:, 160 + o : 161 + o], (16, 128)), bh)
    bh_ref[...] = bh


def split_columns(x, select):
    even, odd = [], []
    for k in range(x.shape[1] // 256):
        piece = dot(x[:, 256 * k : 256 * (k + 1)], select)
        even.append(piece[:, 0:128])
        odd.append(piece[:, 128:256])
    return jnp.concatenate(even, axis=1), jnp.concatenate(odd, axis=1)


def first_kernel(
    tiles,
    nucleus_ref, x_ref, x_lo, x_hi, t_ref, t_lo, t_hi, label_ref, w1_ref, b1_ref, w2_ref, b2_ref,
    y_ref, t_out, h1_ref, x2_ref, x3_ref, style_ref,
):
    crops = x_ref.shape[0]
    width = x_ref.shape[3] // 2
    lanes = crops * width
    height = x_ref.shape[2]
    rows = height // 2
    edge = strip_edges(tiles, rows)
    r_id = lax.broadcasted_iota(jnp.int32, (256, 256), 0)
    c_id = lax.broadcasted_iota(jnp.int32, (256, 256), 1)
    select = jnp.where(r_id == 2 * (c_id % 128) + c_id // 128, 1.0, 0.0).astype(bf16)
    x_rows = 2 * (height + 2 * HALO)
    y_rows = y_ref.shape[0]
    ri = lax.broadcasted_iota(jnp.int32, (y_rows, 4 * x_rows), 0)
    ci = lax.broadcasted_iota(jnp.int32, (y_rows, 4 * x_rows), 1)
    fine = 2 * (ri // 16) + (ri // 8) % 2 - 7
    channel = (ri // 4) % 2
    source = jnp.where(
        fine < 0,
        channel * HALO + fine + HALO,
        jnp.where(
            fine < height,
            2 * HALO + channel * height + fine,
            2 * HALO + 2 * height + channel * HALO + fine - height,
        ),
    )
    perm_x = jnp.where(ci == (ri % 4) * x_rows + source, 1.0, 0.0).astype(bf16)
    t_rows = 3 * height + 4 * HALO
    ri = lax.broadcasted_iota(jnp.int32, (t_out.shape[1], 2 * t_rows), 0)
    ci = lax.broadcasted_iota(jnp.int32, (t_out.shape[1], 2 * t_rows), 1)
    part = (ri // 4) % 4
    fine = 2 * (ri // 16) + (ri // 2) % 2 - 2
    source = jnp.where(
        fine < 0,
        3 * height + part * HALO + fine + HALO,
        jnp.where(fine < height, part * height + fine, 3 * height + 2 * HALO + part * HALO + fine - height),
    )
    outside = (fine < 0) | (fine >= height)
    known = (part < 2) | ((part == 2) & jnp.logical_not(outside))
    perm_t = jnp.where((ci == (ri % 2) * t_rows + source) & known, 1.0, 0.0).astype(bf16)
    has_up, has_dn = edge[0] < 0, edge[1] > rows

    def both_columns(of_crop):
        even, odd = [], []
        for c in range(crops):
            first, second = split_columns(of_crop(c), select)
            even.append(first)
            odd.append(second)
        return jnp.concatenate(even, axis=1), jnp.concatenate(odd, axis=1)

    def image_rows(c):
        pieces = [jnp.where(has_up, x_lo[c, k].astype(f32), 0.0) for k in range(2)]
        pieces += [x_ref[c, k].astype(f32) for k in range(2)]
        pieces += [jnp.where(has_dn, x_hi[c, k].astype(f32), 0.0) for k in range(2)]
        return jnp.concatenate(pieces, axis=0).astype(bf16)

    def target_rows(c):
        pieces = [t_ref[c, 0].astype(f32), t_ref[c, 1].astype(f32), label_ref[c].astype(f32)]
        pieces += [jnp.where(has_up, t_lo[c, k], 0).astype(f32) for k in range(2)]
        pieces += [jnp.where(has_dn, t_hi[c, k], 0).astype(f32) for k in range(2)]
        return jnp.concatenate(pieces, axis=0).astype(bf16)

    even, odd = both_columns(image_rows)
    row = lax.broadcasted_iota(jnp.int32, (x_rows, lanes), 0)
    crop = lax.broadcasted_iota(jnp.int32, (x_rows, lanes), 1) // width
    second = ((row >= HALO) & (row < 2 * HALO)) | (row >= x_rows - HALO)
    second = second | ((row >= 2 * HALO + height) & (row < 2 * HALO + 2 * height))
    gate = jnp.ones((x_rows, lanes), f32)
    for c in range(crops):
        gate = jnp.where(second & (crop == c), nucleus_ref[c].astype(f32), gate)
    even, odd = even * gate, odd * gate
    stack = jnp.concatenate([from_left(odd, crops), even, odd, from_right(even, crops)], axis=0)
    y_ref[...] = dot(perm_x, stack.astype(bf16)).astype(bf16)
    even, odd = both_columns(target_rows)
    put_lanes(t_out, 0, dot(perm_t, jnp.concatenate([even, odd], axis=0).astype(bf16)))
    ones = crop_rows(crops, lanes)
    style_ref[...] = jnp.zeros_like(style_ref)

    def conv_one(ks):
        pre = [dot(w1_ref[...], rows_of(y_ref, k * 16, 32)) for k in ks]
        for k, p in zip(ks, pre):
            keep = valid(k - 3, edge)
            hidden = (jnp.maximum(p + wide(b1_ref[...], lanes), 0.0) * keep).astype(bf16)
            put_rows(h1_ref, k * 128, hidden)
            h = hidden.astype(f32)
            pooled = (0.25 * ((h[0:32] + h[32:64]) + (h[64:96] + h[96:128]))).astype(bf16)
            put_rows(x2_ref, k * 96, three_columns(pooled, crops))

    def conv_two(qs):
        pre = [dot(w2_ref[...], rows_of(x2_ref, q * 96, 288)) for q in qs]
        sums = 0.0
        for q, p in zip(qs, pre):
            row = q - 2
            keep = valid(row, edge)
            own = jnp.where((row >= 0) & (row < rows), 1.0, 0.0).astype(f32)
            hidden = (jnp.maximum(p + wide(b2_ref[...], lanes), 0.0) * keep).astype(bf16)
            put_rows(x3_ref, q * 192, three_columns(hidden, crops))
            sums = sums + dot_nt(ones, hidden) * own
        style_ref[:, 0:64] += sums

    repeat_rows(rows + 6, 2, conv_one)
    repeat_rows(rows + 4, 2, conv_two)


def second_kernel(
    tiles, crops, scale, coarse_count,
    h1_ref, x3_ref, t_ref, total_ref, b3_ref, ws_ref, w3_ref, wh_ref, wht_ref, wd3_ref, bh_ref,
    gc_ref, rim_lo, rim_hi, go_out, k3_ref, head_ref, style_ref, sums_ref, sg_ref,
    h3_ref, m_ref, fe_ref, go_ref, g3_ref, d3_ref,
):
    lanes = h1_ref.shape[1]
    width = lanes // crops
    rows = go_out.shape[0] // 16
    edge = strip_edges(tiles, rows)
    raw = total_ref[:, 0:64] / coarse_count
    unit = raw * lax.rsqrt(jnp.mean(raw * raw, axis=1, keepdims=True) + norm_eps)
    vec = dot_nt(unit, ws_ref[...], highest)
    vec = jnp.concatenate([vec] * 4, axis=1) + b3_ref[0:1, :]
    bias3 = [as_column(vec[c : c + 1]) for c in range(crops)]
    bias3 = jnp.concatenate([wide(b, width) for b in bias3], axis=1)
    ones = crop_rows(crops, lanes)

    def forward(ks):
        pre = [dot(w3_ref[...], rows_of(x3_ref, k * 192, 576)) for k in ks]
        hs = []
        for k, both in zip(ks, pre):
            p = both[0:128] + both[128:256] + bias3
            h1 = rows_of(h1_ref, (k + 2) * 128, 128).astype(f32)
            h3 = (jnp.maximum(p, 0.0) + h1).astype(bf16)
            put_rows(h3_ref, k * 128, h3)
            put_rows(m_ref, k * 128, jnp.where(p > 0, 1.0, 0.0).astype(bf16))
            hs.append(h3)
        outs = [dot(wh_ref[...], h) for h in hs]
        for k, o in zip(ks, outs):
            o = o + wide(bh_ref[...], lanes)
            t = get_lanes(t_ref, k * 16, 16)
            fe = (o[0:8] - 0.25 * t[0:8]) * valid(k - 1, edge)
            put_lanes(fe_ref, k * 16, jnp.concatenate([fe, o[8:16]], axis=0))

    repeat_rows(rows + 2, 2, forward)

    r_id = lax.broadcasted_iota(jnp.int32, (rows, lanes), 0)
    above = jnp.where(r_id - 1 >= edge[0], 1.0, 0.0)
    below = jnp.where(r_id + 1 < edge[1], 1.0, 0.0)
    go_ref[...] = jnp.zeros_like(go_ref)

    def at(part, off):
        return get_lanes(fe_ref, 16 * (1 + off) + part, rows, 16)

    def column_part(pr, off):
        odd, even = at(4 + 2 * pr + 1, off), at(4 + 2 * pr, off)
        return 0.5 * (odd - from_left(odd, crops)), 0.5 * (from_right(even, crops) - even)

    loss = jnp.zeros((rows, 128), f32)
    e0 = [at(k, 0) for k in range(4)]
    e1 = [at(4 + k, 0) for k in range(4)]
    cols0, cols1 = column_part(0, 0), column_part(1, 0)
    cols_up, cols_dn = column_part(1, -1), column_part(0, 1)
    spread = [None] * 4
    g_up, g_dn = [None] * 2, [None] * 2
    for pc in range(2):
        f_up, f_dn = at(2 + pc, -1), at(pc, 1)
        spread[pc] = 0.5 * (e0[2 + pc] - f_up) + cols0[pc]
        spread[2 + pc] = 0.5 * (f_dn - e0[pc]) + cols1[pc]
        g_up[pc] = 2.0 * scale * above * (0.5 * (e0[pc] - at(pc, -1)) + cols_up[pc])
        g_dn[pc] = 2.0 * scale * below * (0.5 * (at(2 + pc, 1) - e0[2 + pc]) + cols_dn[pc])
    g = [2.0 * scale * v for v in spread]
    for pr in range(2):
        even, odd = g[2 * pr], g[2 * pr + 1]
        col = [0.5 * (odd - from_left(odd, crops)), 0.5 * (from_right(even, crops) - even)]
        for pc in range(2):
            k = 2 * pr + pc
            if pr == 0:
                row_part = 0.5 * (g[2 + pc] - g_up[pc])
            else:
                row_part = 0.5 * (g_dn[pc] - g[pc])
            logit = at(8 + k, 0)
            label = get_lanes(t_ref, 16 + 8 + k, rows, 16)
            ex = jnp.exp(-jnp.abs(logit))
            sig = jnp.where(logit >= 0, 1.0, ex) / (1.0 + ex)
            grads = (2.0 * scale * e0[k] - row_part, 2.0 * scale * e1[k] - col[pc], scale * (sig - label))
            for part in range(OUT_CH):
                for j in range(lanes // 128):
                    go_ref[j, pl.ds(4 * part + k, rows, stride=16), :] = grads[part][:, 128 * j : 128 * (j + 1)]
            term = jnp.maximum(logit, 0.0) + jnp.log1p(ex) - label * logit
            loss = loss + fold_lanes(e0[k] * e0[k] + e1[k] * e1[k] + spread[k] * spread[k] + term)

    sums_ref[...] = jnp.zeros_like(sums_ref)
    sums_ref[4:5, :] = jnp.sum(loss, axis=0, keepdims=True)
    head_ref[...] = jnp.zeros_like(head_ref)
    sg_ref[...] = jnp.zeros_like(sg_ref)
    d3_ref[...] = jnp.zeros_like(d3_ref)
    for k in (0, 1, rows + 2, rows + 3):
        g3_ref[256 * k : 256 * (k + 1), :] = jnp.zeros((256, lanes), bf16)

    def backward(rs):
        gos = [get_lanes(go_ref, r * 16, 16).astype(bf16) for r in rs]
        gts = [dot(wht_ref[...], go) for go in gos]
        head, gsum, sg, d3 = 0.0, 0.0, 0.0, 0.0
        for r, go, gt in zip(rs, gos, gts):
            put_rows(go_out, r * 16, go)
            spot = (r + 1) * 128
            head = head + dot_nt(go, rows_of(h3_ref, spot, 128))
            gsum = gsum + dot_nt(ones, go)
            g = gt.astype(bf16).astype(f32) * rows_of(m_ref, spot, 128).astype(f32)
            gb = g.astype(bf16)
            sg = sg + dot_nt(ones, gb)
            parts = []
            for pr in range(2):
                even, odd = g[64 * pr : 64 * pr + 32], g[64 * pr + 32 : 64 * pr + 64]
                parts += [
                    from_left(odd, crops).astype(bf16),
                    gb[64 * pr : 64 * pr + 64],
                    from_right(even, crops).astype(bf16),
                ]
            put_rows(g3_ref, (r + 2) * 256, jnp.concatenate(parts, axis=0))
            d3 = d3 + dot_nt(rows_of(x3_ref, (r + 1) * 192, 576), gb)
        head_ref[...] += head
        sums_ref[3:4, 0:16] += jnp.sum(gsum, axis=0, keepdims=True)
        sg_ref[...] += sg
        d3_ref[...] += d3

    repeat_rows(rows, 2, backward)

    def down(ks):
        both = [dot(wd3_ref[...], rows_of(g3_ref, k * 256 + 128, 512)) for k in ks]
        for k, b in zip(ks, both):
            put_rows(gc_ref, k * 64, b[0:64] + b[64:128])

    repeat_rows(rows + 2, 2, down)
    rim_lo[...] = gc_ref[0:128, :].astype(bf16)
    rim_hi[...] = gc_ref[64 * rows : 64 * rows + 128, :].astype(bf16)

    d3 = jnp.transpose(d3_ref[...])
    for block in range(5):
        packed = jnp.zeros((CH_ONE, 128), f32)
        for tap in range(2 * block, min(2 * block + 2, 9)):
            a, b = tap // 3, tap % 3
            total = jnp.zeros((CH_ONE, CH_TWO), f32)
            for p in range(4):
                n = 3 * ((p // 2 + a + 1) // 2) + (p % 2 + b + 1) // 2
                total = total + d3[32 * p : 32 * (p + 1), 64 * n : 64 * (n + 1)]
            if tap % 2 == 0:
                packed = jnp.concatenate([total, packed[:, 64:128]], axis=1)
            else:
                packed = jnp.concatenate([packed[:, 0:64], total], axis=1)
        if block < 4:
            k3_ref[32 * block : 32 * (block + 1), :] = packed
        else:
            k3_ref[128:144, :] = jnp.concatenate([packed[0:16, 0:64], packed[16:32, 0:64]], axis=1)
    outer = jnp.zeros((CH_ONE, 128), f32)
    for c in range(crops):
        outer = outer + as_column(over_phases(sg_ref[c : c + 1, :]))[0:32] * jnp.concatenate([unit[c : c + 1]] * 2, axis=1)
        sums_ref[2:3, :] += sg_ref[c : c + 1, :]
    style_ref[...] = jnp.concatenate([outer[0:16, 0:64], outer[16:32, 0:64]], axis=1)


def third_kernel(
    tiles, crops, coarse_count,
    gc_ref, up_ref, dn_ref, total_ref, sg_ref, ws_ref, x3_ref, x2_ref, h1_ref, y_ref, go_ref, wd2_ref, wht_ref,
    k2_ref, d1_ref, sums_ref,
    g2_ref, d2_ref,
):
    lanes = h1_ref.shape[1]
    width = lanes // crops
    rows = go_ref.shape[0] // 16
    edge = strip_edges(tiles, rows)
    style_raw = total_ref[:, 0:64] / coarse_count
    inv = lax.rsqrt(jnp.mean(style_raw * style_raw, axis=1, keepdims=True) + norm_eps)
    style_grad = over_phases(sg_ref[...])[:, 0:32]
    grad_unit = jnp.dot(style_grad, ws_ref[...], precision=highest, preferred_element_type=f32)
    grad_raw = inv * grad_unit - inv * inv * inv * style_raw * jnp.mean(style_raw * grad_unit, axis=1, keepdims=True)
    grad_raw = jnp.concatenate([grad_raw / coarse_count] * 2, axis=1)
    raw = jnp.concatenate([wide(as_column(grad_raw[c : c + 1])[0:64], width) for c in range(crops)], axis=1)
    ones = jnp.ones((8, lanes), bf16)
    sums_ref[...] = jnp.zeros_like(sums_ref)
    d2_ref[...] = jnp.zeros_like(d2_ref)
    d1_ref[...] = jnp.zeros_like(d1_ref)

    def masked(k, extra=None):
        coarse = rows_of(gc_ref, k * 64, 64)
        if extra is not None:
            coarse = coarse + extra
        grad = (coarse + raw).astype(bf16).astype(f32)
        h2 = rows_of(x3_ref, (k + 1) * 192 + 64, 64).astype(f32)
        put_rows(g2_ref, k * 192, three_columns(jnp.where(h2 > 0, grad, 0.0).astype(bf16), crops))

    up = jnp.where(edge[0] < 0, up_ref[...].astype(f32), 0.0)
    dn = jnp.where(edge[1] > rows, dn_ref[...].astype(f32), 0.0)
    masked(0, up[0:64])
    masked(1, up[64:128])
    masked(rows, dn[0:64])
    masked(rows + 1, dn[64:128])

    def inner(ks):
        for k in ks:
            masked(k + 2)

    repeat_rows(rows - 2, 2, inner)

    def backward(rs):
        gps = [dot(wd2_ref[...], rows_of(g2_ref, r * 192, 576)) for r in rs]
        gts = [dot(wht_ref[...], rows_of(go_ref, r * 16, 16)) for r in rs]
        d2, d1, sum_two, sum_one = 0.0, 0.0, 0.0, 0.0
        for r, gp, gt in zip(rs, gps, gts):
            g2 = rows_of(g2_ref, (r + 1) * 192 + 64, 64)
            d2 = d2 + dot_nt(rows_of(x2_ref, (r + 2) * 96, 288), g2)
            sum_two = sum_two + dot_nt(ones, g2)
            gp = 0.25 * gp.astype(bf16).astype(f32)
            g1 = (jnp.concatenate([gp] * 4, axis=0) + gt.astype(bf16).astype(f32)).astype(bf16).astype(f32)
            h1 = rows_of(h1_ref, (r + 3) * 128, 128).astype(f32)
            gb = jnp.where(h1 > 0, g1, 0.0).astype(bf16)
            sum_one = sum_one + dot_nt(ones, gb)
            d1 = d1 + dot_nt(rows_of(y_ref, (r + 3) * 16, 32), gb)
        d2_ref[...] += d2
        d1_ref[...] += d1
        sums_ref[0:1, :] += sum_one[0:1]
        sums_ref[1:2, 0:64] += sum_two[0:1]

    repeat_rows(rows, 2, backward)
    rest = jnp.concatenate([d2_ref[160:288, :], jnp.zeros((32, 64), f32)], axis=0)
    k2_ref[...] = jnp.concatenate([d2_ref[0:160, :], rest], axis=1)


def update_kernel(pixel_count, count_ref, sum_ref, *refs):
    olds, outs, loss_ref = refs[:18], refs[18:36], refs[36]
    starts = [sum(PART_ROWS[:k]) for k in range(len(PART_ROWS))]
    rate = 1.0 / (jnp.zeros((8, 128), f32) + (count_ref[0].astype(f32) + 1.0))

    def step(index, spot, grad):
        weight, momentum, average = (olds[3 * index + k][spot] for k in range(3))
        decayed = grad + decay_rate * weight
        momentum = momentum_rate * momentum + decayed
        new = weight - learn_rate * (decayed + momentum_rate * momentum)
        outs[3 * index][spot] = new
        outs[3 * index + 1][spot] = momentum
        outs[3 * index + 2][spot] = average + (new - average) * rate[0:1, 0:1]

    d1 = sum_ref[starts[2] : starts[2] + 32, :]
    total = jnp.zeros((32, 128), f32)
    for p in range(4):
        total = total + turn(turn(d1, -32 * p, 1), -(8 * (p // 2) + p % 2), 0)
    for a in range(3):
        for b in range(3):
            for i in range(2):
                k = 8 * a + 4 * i + b
                step(0, (a, b, slice(i, i + 1), slice(None)), total[k : k + 1, 0:32])
    for tap in range(9):
        a, b = tap // 3, tap % 3
        first = starts[1] + 32 * (tap % 5)
        half = 64 * (tap // 5)
        step(1, (a, b), sum_ref[first : first + 32, half : half + 64])
        if tap < 8:
            first = starts[0] + 32 * (tap // 2)
            lane = 64 * (tap % 2)
            grad = sum_ref[first : first + 32, lane : lane + 64]
        else:
            first = starts[0] + 128
            grad = jnp.concatenate([sum_ref[first : first + 16, 64 * k : 64 * (k + 1)] for k in range(2)], axis=0)
        step(2, (a, b), grad)
    first = starts[4]
    grad = jnp.concatenate([sum_ref[first : first + 16, 64 * k : 64 * (k + 1)] for k in range(2)], axis=0)
    step(3, (slice(None), slice(None)), grad)
    head = sum_ref[starts[3] : starts[3] + 16, :]
    total = jnp.zeros((16, 128), f32)
    for p in range(4):
        total = total + turn(turn(head, -32 * p, 1), -p, 0)
    total = jnp.concatenate([total[4 * o : 4 * o + 1] for o in range(OUT_CH)], axis=0)
    step(4, (slice(None), slice(None)), total[:, 0:32])
    sums = sum_ref[starts[5] : starts[5] + 8, :]
    one, three = over_phases(sums[0:1]), over_phases(sums[2:3])
    lane = lax.broadcasted_iota(jnp.int32, (1, 128), 1)
    low = jnp.where(lane < 32, one, jnp.where(lane < 96, turn(sums[1:2], 32, 1), three))
    ends = sums[3:4]
    ends = (ends + turn(ends, -1, 1)) + (turn(ends, -2, 1) + turn(ends, -3, 1))
    high = jnp.where(lane < 32, three, 0.0)
    for o in range(OUT_CH):
        high = jnp.where(lane == 32 + o, turn(ends, 32 + o - 4 * o, 1), high)
    grad = jnp.concatenate([low, high], axis=1)[:, 0 : olds[15].shape[0]]
    weight, momentum, average = (olds[15 + k][...].reshape(1, -1) for k in range(3))
    decayed = grad + decay_rate * weight
    momentum = momentum_rate * momentum + decayed
    new = weight - learn_rate * (decayed + momentum_rate * momentum)
    average = average + (new - average) * rate[0:1, 0:1]
    for k, value in enumerate((new, momentum, average)):
        outs[15 + k][...] = value.reshape(-1)
    loss_ref[0] = jnp.sum(sums[4:5]) / pixel_count


def on_device(
    images, nucleus, target_flow, cell_label, step_count,
    conv1_weight, conv1_momentum, conv1_average,
    conv2_weight, conv2_momentum, conv2_average,
    conv3_weight, conv3_momentum, conv3_average,
    style_weight, style_momentum, style_average,
    head_weight, head_momentum, head_average,
    biases, bias_momentum, bias_average,
):
    tiles = lax.axis_size("tile")
    crops, _, height, cols = images.shape
    rows, width = height // 2, cols // 2
    pixel_count = lax.axis_size("img") * tiles * crops * height * cols
    grad_scale = 1.0 / math.sqrt(pixel_count)
    coarse_count = tiles * rows * width

    def sds(shape, dtype=f32):
        return jax.ShapeDtypeStruct(shape, dtype)

    lanes = crops * width
    images_count = lax.axis_size("img")

    def params(mib):
        return pltpu.CompilerParams(vmem_limit_bytes=mib * 2**20)

    def remote(collective_id):
        return pltpu.CompilerParams(collective_id=collective_id, has_side_effects=True, vmem_limit_bytes=8 * 2**20)

    def other_way(w):
        return jnp.swapaxes(w, -1, -2)

    third = tuple(other_way(w) for w in (conv3_weight, conv3_momentum, conv3_average))
    style = tuple(other_way(w) for w in (style_weight, style_momentum, style_average))
    head = tuple(other_way(w) for w in (head_weight, head_momentum, head_average))

    edge = (crops, 2, HALO, cols)
    x_lo, x_hi, t_lo, t_hi = pl.pallas_call(
        lambda *refs: halo_kernel(tiles, *refs),
        out_shape=(sds(edge, bf16), sds(edge, bf16), sds(edge, jnp.int32), sds(edge, jnp.int32)),
        in_specs=[ANY] * 2,
        out_specs=[ANY] * 4,
        scratch_shapes=[DMA((4,)), DMA((4,))],
        compiler_params=remote(1),
        name="halo",
    )(images, target_flow)
    w1, w2, w3, wd3, wd2, wh, wht, b1, b2, b3, bh = pl.pallas_call(
        weight_kernel,
        out_shape=(
            sds((128, 32), bf16),
            sds((CH_TWO, 9 * CH_ONE), bf16),
            sds((256, 9 * CH_TWO), bf16),
            sds((128, 16 * CH_ONE), bf16),
            sds((CH_ONE, 9 * CH_TWO), bf16),
            sds((16, 128), bf16),
            sds((128, 16), bf16),
            sds((128, 128)),
            sds((64, 128)),
            sds((8, 128)),
            sds((16, 128)),
        ),
        in_specs=[VMEM] * 5,
        out_specs=[VMEM] * 11,
        scratch_shapes=[pltpu.VMEM((32, 128), f32)],
        compiler_params=params(8),
        name="weights",
    )(conv1_weight, conv2_weight, third[0], head[0], biases)

    y, targets, h1, x2, x3, style_part = pl.pallas_call(
        lambda *refs: first_kernel(tiles, *refs),
        out_shape=(
            sds((16 * (rows + 7), lanes), bf16),
            sds((lanes // 128, 16 * (rows + 2), 128)),
            sds((128 * (rows + 6), lanes), bf16),
            sds((96 * (rows + 6), lanes), bf16),
            sds((192 * (rows + 4), lanes), bf16),
            sds((8, 128)),
        ),
        in_specs=[SMEM] + [VMEM] * 11,
        out_specs=[VMEM] * 6,
        compiler_params=params(12),
        name="forward_one_two",
    )(nucleus, images, x_lo, x_hi, target_flow, t_lo, t_hi, cell_label, w1, b1, w2, b2)

    style_total = pl.pallas_call(
        lambda *refs: sum_kernel(tiles, *refs),
        out_shape=sds((8, 128)),
        in_specs=[VMEM],
        out_specs=VMEM,
        scratch_shapes=[pltpu.VMEM((tiles, 8, 128), f32), DMA((tiles,)), DMA((tiles,))],
        compiler_params=remote(2),
        name="style_sum",
    )(style_part)

    rim = (128, lanes)
    gc, rim_lo, rim_hi, go, k3, head_part, style_grad, sums_a, sg = pl.pallas_call(
        lambda *refs: second_kernel(tiles, crops, grad_scale, float(coarse_count), *refs),
        out_shape=(
            sds((64 * (rows + 2), lanes)),
            sds(rim, bf16),
            sds(rim, bf16),
            sds((16 * rows, lanes), bf16),
            sds((144, 128)),
            sds((16, 128)),
            sds((16, 128)),
            sds((8, 128)),
            sds((8, 128)),
        ),
        in_specs=[VMEM] * 11,
        out_specs=[VMEM] * 9,
        scratch_shapes=[
            pltpu.VMEM((128 * (rows + 2), lanes), bf16),
            pltpu.VMEM((128 * (rows + 2), lanes), bf16),
            pltpu.VMEM((lanes // 128, 16 * (rows + 2), 128), f32),
            pltpu.VMEM((lanes // 128, 16 * rows, 128), f32),
            pltpu.VMEM((256 * (rows + 4), lanes), bf16),
            pltpu.VMEM((9 * CH_TWO, 128), f32),
        ],
        compiler_params=params(30),
        name="forward_three_back",
    )(h1, x3, targets, style_total, b3, style[0], w3, wh, wht, wd3, bh)

    sg_total, rim_up, rim_dn = pl.pallas_call(
        lambda *refs: sum_rim_kernel(tiles, *refs),
        out_shape=(sds((8, 128)), sds(rim, bf16), sds(rim, bf16)),
        in_specs=[VMEM, ANY, ANY],
        out_specs=[VMEM, ANY, ANY],
        scratch_shapes=[
            pltpu.VMEM((tiles, 8, 128), f32), DMA((tiles,)), DMA((tiles,)), DMA((2,)), DMA((2,)),
        ],
        compiler_params=remote(3),
        name="style_grad_sum",
    )(sg, rim_lo, rim_hi)

    k2, d1, sums_b = pl.pallas_call(
        lambda *refs: third_kernel(tiles, crops, float(coarse_count), *refs),
        out_shape=(sds((160, 128)), sds((32, 128)), sds((8, 128))),
        in_specs=[VMEM] * 13,
        out_specs=[VMEM] * 3,
        scratch_shapes=[
            pltpu.VMEM((192 * (rows + 2), lanes), bf16),
            pltpu.VMEM((9 * CH_ONE, CH_TWO), f32),
        ],
        compiler_params=params(16),
        name="back_two_one",
    )(gc, rim_up, rim_dn, style_total, sg_total, style[0], x3, x2, h1, y, go, wd2, wht)

    part = 8 * pl.cdiv(sum(PART_ROWS), 8 * tiles)
    summed = pl.pallas_call(
        lambda *refs: reduce_kernel(tiles, images_count, part, *refs),
        out_shape=sds((part * tiles, 128)),
        in_specs=[VMEM] * 7,
        out_specs=VMEM,
        scratch_shapes=[
            pltpu.VMEM((part * tiles, 128), f32),
            pltpu.VMEM((tiles, part, 128), f32),
            pltpu.VMEM((part, 128), f32),
            pltpu.VMEM((images_count, part, 128), f32),
            pltpu.VMEM((part * tiles, 128), f32),
            DMA((tiles,)), DMA((tiles,)), DMA((images_count,)), DMA((images_count,)), DMA((tiles,)), DMA((tiles,)),
        ],
        compiler_params=remote(4),
        name="gradient_sum",
    )(k3, k2, d1, head_part, style_grad, sums_a, sums_b)

    olds = (
        (conv1_weight, conv1_momentum, conv1_average)
        + (conv2_weight, conv2_momentum, conv2_average)
        + third + style + head
        + (biases, bias_momentum, bias_average)
    )
    news = pl.pallas_call(
        lambda *refs: update_kernel(float(pixel_count), *refs),
        out_shape=tuple(sds(v.shape) for v in olds) + (sds((1,)),),
        in_specs=[SMEM] + [VMEM] * 19,
        out_specs=[VMEM] * 18 + [SMEM],
        compiler_params=params(16),
        name="update",
    )(step_count, summed, *olds)
    return (news[18], *news[0:6], *(other_way(w) for w in news[6:15]), *news[15:18])


def solution(mesh):
    return jax.shard_map(
        on_device,
        mesh=mesh,
        in_specs=(
            P("img", None, "tile", None),
            P("img"),
            P("img", None, "tile", None),
            P("img", "tile", None),
        )
        + (P(),) * 19,
        out_specs=(P(),) * 19,
        check_vma=False,
    )
```

time: 162 us -> 107 us (0.66)
  Pallas kernels: 133 us -> 94.7 us
  local copies, waits for them, and re-layouts: 25.3 us -> 10.3 us
    pallas_call x3, Pallas kernels: 83.6 us -> 54.1 us  [the longest x1 27.2 us: on_device(): pl.pallas_call(lambda *refs: second_kernel(tiles, crops, grad_scale, floa...]
    unnamed x38 -> x58, local copies, waits for them, and re-layouts: 22.1 us -> 10.3 us
    pallas_call x1, Pallas kernels: 3.44 us -> 1.39 us  [on_device(): pl.pallas_call(lambda *refs: update_kernel(float(pixel_count), *refs), ou...]
    pallas_call x1, Pallas kernels: 2.38 us -> 0.35 us  [on_device(): pl.pallas_call(weight_kernel, out_shape=(sds((128, 32), bf16), sds((CH_TW...]
    slice x2 -> x0, local copies, waits for them, and re-layouts: 1.88 us -> none  [the longest x1 1.19 us: on_device(): return (tail[1, 0:1], *news, *last)]
    pallas_call x1, Pallas kernels: 19.2 us -> 17.5 us  [on_device(): pl.pallas_call(lambda *refs: reduce_kernel(tiles, images_count, part, *re...]
where the time goes in v3:
time: 107 us
  Pallas kernels  94.7 us (89%)
  local copies, waits for them, and re-layouts  10.3 us (10%)
  between operations  1.64 us (2%)
    pallas_call x1, Pallas kernels, on_device(): pl.pallas_call(lambda *refs: second_kernel(tiles, crops, grad_scale, floa...  27.2 us
    pallas_call x1, Pallas kernels, on_device(): pl.pallas_call(lambda *refs: reduce_kernel(tiles, images_count, part, *re...  17.5 us
    pallas_call x1, Pallas kernels, on_device(): pl.pallas_call(lambda *refs: third_kernel(tiles, crops, float(coarse_coun...  13.7 us
    pallas_call x1, Pallas kernels, on_device(): pl.pallas_call(lambda *refs: first_kernel(tiles, *refs), out_shape=(sds((...  13.2 us
    unnamed x58, local copies, waits for them, and re-layouts  10.3 us
    pallas_call x1, Pallas kernels, on_device(): pl.pallas_call(lambda *refs: sum_rim_kernel(tiles, *refs), out_shape=(sds...  8.76 us
    pallas_call x1, Pallas kernels, on_device(): pl.pallas_call(lambda *refs: sum_kernel(tiles, *refs), out_shape=sds((8,...  8.45 us
    pallas_call x1, Pallas kernels, on_device(): pl.pallas_call(lambda *refs: halo_kernel(tiles, *refs), out_shape=(sds(ed...  4.14 us

profile of v3, /device:TPU:0, one launch (start us, length us, event | category | flops | bytes accessed | tf_op | source)
XLA Modules:
  0.0 106.6 jit_solution(16710531739154974669)
XLA Ops:
  0.7 0.0 copy-start.4
  0.7 0.9 copy-done.4
  1.6 0.9 copy-done.6
  2.5 0.7 copy-done.14
  3.2 0.7 copy-done.20
  3.9 0.7 copy-done.22
  4.5 0.4 weights.1
  4.9 1.0 copy-done
  5.9 0.9 copy-done.2
  6.9 4.1 %halo.1 = (bf16[2,2,8,1024]{3,2,1,0:T(8,128)(2,1)S(1)}, bf16[2,2,8,1024]{3,2,1,0:T(8,128)(2,1)S(1)}, s32[2,2,8,1024]{3,2,1,0:T(8,128)S(1)}, s32[2,2,8,1024]{3,2,1,0:T(8,128)S(1)}) custom-call(bf16[2,2,32,1024]{3,2,1,0:T(8,128)(2,1)S(1)} %copy-done.2, s32[2,2,32,1024]{3,2,1,0:T(8,128)S(1)} %copy-done), custom_call_target="tpu_custom_call" | custom-call | tf_op jit(solution)/shard_map/halo/pallas_call | solution.py:781
  11.0 0.0 copy-start.1
  11.1 1.0 copy-done.1
  12.1 0.9 copy-done.3
  13.0 0.9 copy-done.8
  14.0 0.7 copy-done.28
  14.6 13.2 %forward_one_two.1 = (bf16[368,1024]{1,0:T(8,128)(2,1)S(1)}, f32[8,288,128]{2,1,0:T(8,128)S(1)}, bf16[2816,1024]{1,0:T(8,128)(2,1)S(1)}, bf16[2112,1024]{1,0:T(8...) custom-call(s32[2]{0:T(128)S(1)} %copy-done.28, bf16[2,2,32,1024]{3,2,1,0:T(8,128)(2,1)S(1)} %copy-done.3, ...), custom_call_target="tpu_custom_call" | custom-call | tf_op jit(solution)/shard_map/forward_one_two/pallas_call | solution.py:812
  27.8 8.5 %style_sum.1.refs_3_ = f32[8,128]{1,0:T(8,128)S(1)} custom-call(f32[8,128]{1,0:T(8,128)S(1)} %get-tuple-element.85.refs_0_), custom_call_target="tpu_custom_call" | custom-call | tf_op jit(solution)/shard_map/style_sum/pallas_call | solution.py:828
  36.3 0.7 copy-done.13
  37.0 27.2 %forward_three_back.1 = (f32[1152,1024]{1,0:T(8,128)S(1)}, bf16[128,1024]{1,0:T(8,128)(2,1)S(1)}, bf16[128,1024]{1,0:T(8,128)(2,1)S(1)}, bf16[256,1024]{1,0:T(8,...) custom-call(bf16[2816,1024]{1,0:T(8,128)(2,1)S(1)} %get-tuple-elemen, ...), custom_call_target="tpu_custom_call" | custom-call | tf_op jit(solution)/shard_map/forward_three_back/pallas_call | solution.py:839
  64.2 8.8 %style_grad_sum.1 = (f32[8,128]{1,0:T(8,128)S(1)}, bf16[128,1024]{1,0:T(8,128)(2,1)S(1)}, bf16[128,1024]{1,0:T(8,128)(2,1)S(1)}) custom-call(f32[8,128]{1,0:T(8,128)S(1)} %get-tuple-element.94.refs_0_, bf16[128,1024]{1,0:T(8,128)(2,1)S(1)} %get-tuple-element.95.refs_1_, bf16[128,1024]{1,0:T(8,128)(2,1)S(1)} %get-tuple-element.96.refs_2_), custom_call_target="tpu_custom_call" | custom-call | tf_op jit(solution)/shard_map/style_grad_sum/pallas_call | solution.py:866
  73.0 0.0 copy-start.5
  73.2 13.7 %back_two_one.1 = (f32[160,128]{1,0:T(8,128)S(1)}, f32[32,128]{1,0:T(8,128)S(1)}, f32[8,128]{1,0:T(8,128)S(1)}) custom-call(f32[1152,1024]{1,0:T(8,128)S(1)} %get-tuple-element.93.refs_0_, bf16[128,1024]{1,0:T(8,128)(2,1)S(1)} %get-tuple-element.97.refs_1_, bf16[128,1024]{1,0:T(8,128)(2,1)S(1)} %get-tuple-element.98.refs_2_, f32[8,128]{1,0:T(8,128)S(1)} %style_sum.1.refs_3_, ...), custom_call_target="tpu_custom_call" | custom-call | tf_op jit(solution)/shard_map/back_two_one/pallas_call | solution.py:878
  86.9 17.5 %gradient_sum.1.refs_1_ = f32[384,128]{1,0:T(8,128)S(1)} custom-call(f32[144,128]{1,0:T(8,128)S(1)} %get-tuple-element.92.refs_0_, f32[160,128]{1,0:T(8,128)S(1)} %get-tuple-element.104.refs_1_, f32[32,128]{1,0:T(8,128)S(1)} %get-tuple-element.105.refs_2_, f32[16,128]{1,0:T(8,128)S(1)} %get-tuple-element.106.refs_3_, ...), custom_call_target="tpu_custom_call" | custom-call | tf_op jit(solution)/shard_map/gradient_sum/pallas_call | solution.py:892
  105.2 1.4 %update.1 = (f32[3,3,2,32]{3,2,1,0:T(2,128)}, f32[3,3,2,32]{3,2,1,0:T(2,128)}, f32[3,3,2,32]{3,2,1,0:T(2,128)}, f32[3,3,32,64]{3,2,1,0:T(8,128)}, f32[3,3,32,64]...) custom-call(s32[1]{0:T(128)S(6)} %copy.42.refs_0_, ...), custom_call_target="tpu_custom_call" | custom-call | tf_op jit(solution)/shard_map/update/pallas_call | solution.py:915
  (43 shorter events, 0.1 us)
Async XLA Ops:
  0.7 0.9 copy-start.4
  1.6 0.9 copy-start.6
  4.9 1.0 copy-start
  5.9 0.9 copy-start.2
  11.0 1.0 copy-start.1
  12.1 0.9 copy-start.3
  13.0 0.9 copy-start.8
  73.0 32.0 %copy-start.5 = (f32[3,3,32,64]{3,2,1,0:T(8,128)S(1)}, f32[3,3,32,64]{3,2,1,0:T(8,128)}, u32[]{:S(2)}) copy-start(f32[3,3,32,64]{3,2,1,0:T(8,128)} %refs_5_.1) | copy-start | bytes 221188
  73.0 32.0 %copy-start.7 = (f32[3,3,64,32]{2,3,1,0:T(8,128)S(1)}, f32[3,3,64,32]{2,3,1,0:T(8,128)}, u32[]{:S(2)}) copy-start(f32[3,3,64,32]{2,3,1,0:T(8,128)} %param.34) | copy-start | bytes 221188
  73.0 32.0 %copy-start.9 = (f32[3,3,32,64]{3,2,1,0:T(8,128)S(1)}, f32[3,3,32,64]{3,2,1,0:T(8,128)}, u32[]{:S(2)}) copy-start(f32[3,3,32,64]{3,2,1,0:T(8,128)} %refs_6_.1) | copy-start | bytes 221188
  73.0 32.0 %copy-start.10 = (f32[3,3,32,64]{3,2,1,0:T(8,128)S(1)}, f32[3,3,32,64]{3,2,1,0:T(8,128)}, u32[]{:S(2)}) copy-start(f32[3,3,32,64]{3,2,1,0:T(8,128)} %refs_7_.3) | copy-start | bytes 221188
  73.1 32.0 %copy-start.11 = (f32[3,3,64,32]{2,3,1,0:T(8,128)S(1)}, f32[3,3,64,32]{2,3,1,0:T(8,128)}, u32[]{:S(2)}) copy-start(f32[3,3,64,32]{2,3,1,0:T(8,128)} %param.35) | copy-start | bytes 221188
  73.1 32.0 %copy-start.12 = (f32[3,3,64,32]{2,3,1,0:T(8,128)S(1)}, f32[3,3,64,32]{2,3,1,0:T(8,128)}, u32[]{:S(2)}) copy-start(f32[3,3,64,32]{2,3,1,0:T(8,128)} %param.36) | copy-start | bytes 221188
  73.1 32.0 %copy-start.15 = (f32[3,3,2,32]{3,2,1,0:T(2,128)S(1)}, f32[3,3,2,32]{3,2,1,0:T(2,128)}, u32[]{:S(2)}) copy-start(f32[3,3,2,32]{3,2,1,0:T(2,128)} %refs_2_.1) | copy-start | bytes 6916
  73.1 32.0 %copy-start.16 = (f32[64,32]{0,1:T(8,128)S(1)}, f32[64,32]{0,1:T(8,128)}, u32[]{:S(2)}) copy-start(f32[64,32]{0,1:T(8,128)} %param.38) | copy-start | bytes 24580
  73.1 32.0 %copy-start.17 = (f32[64,32]{0,1:T(8,128)S(1)}, f32[64,32]{0,1:T(8,128)}, u32[]{:S(2)}) copy-start(f32[64,32]{0,1:T(8,128)} %param.39) | copy-start | bytes 24580
  73.1 32.0 %copy-start.18 = (f32[3,3,2,32]{3,2,1,0:T(2,128)S(1)}, f32[3,3,2,32]{3,2,1,0:T(2,128)}, u32[]{:S(2)}) copy-start(f32[3,3,2,32]{3,2,1,0:T(2,128)} %refs_3_.1) | copy-start | bytes 6916
  73.1 32.0 %copy-start.19 = (f32[3,3,2,32]{3,2,1,0:T(2,128)S(1)}, f32[3,3,2,32]{3,2,1,0:T(2,128)}, u32[]{:S(2)}) copy-start(f32[3,3,2,32]{3,2,1,0:T(2,128)} %refs_4_.3) | copy-start | bytes 6916
  73.1 32.0 %copy-start.21 = (f32[32,3]{0,1:T(4,128)S(1)}, f32[32,3]{0,1:T(4,128)}, u32[]{:S(2)}) copy-start(f32[32,3]{0,1:T(4,128)} %param.40) | copy-start | bytes 1156
  73.2 32.0 %copy-start.23 = (f32[163]{0:T(256)S(1)}, f32[163]{0:T(256)}, u32[]{:S(2)}) copy-start(f32[163]{0:T(256)} %refs_17_.1) | copy-start | bytes 1960
  73.2 32.0 %copy-start.24 = (f32[32,3]{0,1:T(4,128)S(1)}, f32[32,3]{0,1:T(4,128)}, u32[]{:S(2)}) copy-start(f32[32,3]{0,1:T(4,128)} %param.41) | copy-start | bytes 1156
  73.2 32.0 %copy-start.25 = (f32[32,3]{0,1:T(4,128)S(1)}, f32[32,3]{0,1:T(4,128)}, u32[]{:S(2)}) copy-start(f32[32,3]{0,1:T(4,128)} %param.42) | copy-start | bytes 1156
  73.2 32.0 %copy-start.26 = (f32[163]{0:T(256)S(1)}, f32[163]{0:T(256)}, u32[]{:S(2)}) copy-start(f32[163]{0:T(256)} %refs_18_.1) | copy-start | bytes 1960
  73.2 32.0 %copy-start.27 = (f32[163]{0:T(256)S(1)}, f32[163]{0:T(256)}, u32[]{:S(2)}) copy-start(f32[163]{0:T(256)} %refs_19_.1) | copy-start | bytes 1960
  (5 other events, 3.4 us)

commit v4 on v3

--- a/solution.py
+++ b/solution.py
@@ -123,13 +123,17 @@
     return jnp.where((row >= edge[0]) & (row < edge[1]), 1.0, 0.0).astype(f32)
 
 
-def meet(sizes):
+def greet(sizes):
     gate = pltpu.get_barrier_semaphore()
     for axis, count in sizes:
         me = lax.axis_index(axis)
         for j in range(1, count):
             pl.semaphore_signal(gate, inc=1, device_id={axis: lax.rem(me + j, count)}, device_id_type=MESH)
-    pl.semaphore_wait(gate, sum(count - 1 for _, count in sizes))
+    return lambda: pl.semaphore_wait(gate, sum(count - 1 for _, count in sizes))
+
+
+def meet(sizes):
+    greet(sizes)()
 
 
 def send_all(count, axis, source, target, send_sem, recv_sem):
@@ -151,21 +155,6 @@
     for k in range(1, count):
         total = total + ref[k]
     return total
-
-
-def meet_next(tiles):
-    gate = pltpu.get_barrier_semaphore()
-    me = lax.axis_index("tile")
-
-    @pl.when(me > 0)
-    def _():
-        pl.semaphore_signal(gate, inc=1, device_id={"tile": me - 1}, device_id_type=MESH)
-
-    @pl.when(me < tiles - 1)
-    def _():
-        pl.semaphore_signal(gate, inc=1, device_id={"tile": me + 1}, device_id_type=MESH)
-
-    pl.semaphore_wait(gate, jnp.minimum(me, 1) + jnp.minimum(tiles - 1 - me, 1))
 
 
 def swap_edges(tiles, pairs, send_sem, recv_sem):
@@ -208,39 +197,19 @@
     return finish
 
 
-def halo_kernel(tiles, x_ref, t_ref, x_lo, x_hi, t_lo, t_hi, send_sem, recv_sem):
-    meet_next(tiles)
-    last = x_ref.shape[2] - HALO
-    finish = swap_edges(
-        tiles,
-        [
-            (ref.at[:, :, pl.ds(0, HALO), :], ref.at[:, :, pl.ds(last, HALO), :], lo, hi)
-            for ref, lo, hi in ((x_ref, x_lo, x_hi), (t_ref, t_lo, t_hi))
-        ],
-        send_sem, recv_sem,
-    )
-    finish()
-
-
-def sum_kernel(tiles, x_ref, o_ref, got, send_sem, recv_sem):
+def sum_over_tiles(tiles, source, got, send_sem, recv_sem):
     me = lax.axis_index("tile")
-    got[me] = x_ref[...]
-    meet((("tile", tiles),))
-    copies = send_all(tiles, "tile", lambda to: x_ref, got.at[me], send_sem, recv_sem)
+    got[me] = source[...]
+    copies = send_all(tiles, "tile", lambda to: source, got.at[me], send_sem, recv_sem)
     for copy in copies:
         copy.wait()
-    o_ref[...] = in_order(got, tiles)
+    return in_order(got, tiles)
 
 
 def sum_rim_kernel(tiles, x_ref, lo_ref, hi_ref, o_ref, up_ref, dn_ref, got, send_sem, recv_sem, rim_send, rim_recv):
-    me = lax.axis_index("tile")
-    got[me] = x_ref[...]
     meet((("tile", tiles),))
     finish = swap_edges(tiles, [(lo_ref, hi_ref, up_ref, dn_ref)], rim_send, rim_recv)
-    copies = send_all(tiles, "tile", lambda to: x_ref, got.at[me], send_sem, recv_sem)
-    for copy in copies:
-        copy.wait()
-    o_ref[...] = in_order(got, tiles)
+    o_ref[...] = sum_over_tiles(tiles, x_ref, got, send_sem, recv_sem)
     finish()
 
 
@@ -277,7 +246,7 @@
     o_ref[...] = full[...]
 
 
-def weight_kernel(
+def weight_tables(
     k1_ref, k2_ref, k3_ref, kh_ref, bias_ref,
     w1_ref, w2_ref, w3_ref, wd3_ref, wd2_ref, wh_ref, wht_ref, b1_ref, b2_ref, b3_ref, bh_ref,
     base_ref,
@@ -352,9 +321,27 @@
 
 def first_kernel(
     tiles,
-    nucleus_ref, x_ref, x_lo, x_hi, t_ref, t_lo, t_hi, label_ref, w1_ref, b1_ref, w2_ref, b2_ref,
-    y_ref, t_out, h1_ref, x2_ref, x3_ref, style_ref,
+    nucleus_ref, x_ref, t_ref, label_ref, k1_ref, k2_ref, k3_ref, kh_ref, bias_ref,
+    y_ref, t_out, h1_ref, x2_ref, x3_ref, total_ref, w3_ref, wd3_ref, wd2_ref, wh_ref, wht_ref, b3_ref, bh_ref,
+    x_lo, x_hi, t_lo, t_hi, w1_ref, w2_ref, b1_ref, b2_ref, base_ref, style_ref, got,
+    halo_send, halo_recv, send_sem, recv_sem,
 ):
+    arrived = greet((("tile", tiles),))
+    weight_tables(
+        k1_ref, k2_ref, k3_ref, kh_ref, bias_ref,
+        w1_ref, w2_ref, w3_ref, wd3_ref, wd2_ref, wh_ref, wht_ref, b1_ref, b2_ref, b3_ref, bh_ref,
+        base_ref,
+    )
+    arrived()
+    last = x_ref.shape[2] - HALO
+    finish = swap_edges(
+        tiles,
+        [
+            (ref.at[:, :, pl.ds(0, HALO), :], ref.at[:, :, pl.ds(last, HALO), :], lo, hi)
+            for ref, lo, hi in ((x_ref, x_lo, x_hi), (t_ref, t_lo, t_hi))
+        ],
+        halo_send, halo_recv,
+    )
     crops = x_ref.shape[0]
     width = x_ref.shape[3] // 2
     lanes = crops * width
@@ -415,6 +402,7 @@
         pieces += [jnp.where(has_dn, t_hi[c, k], 0).astype(f32) for k in range(2)]
         return jnp.concatenate(pieces, axis=0).astype(bf16)
 
+    finish()
     even, odd = both_columns(image_rows)
     row = lax.broadcasted_iota(jnp.int32, (x_rows, lanes), 0)
     crop = lax.broadcasted_iota(jnp.int32, (x_rows, lanes), 1) // width
@@ -455,6 +443,7 @@
 
     repeat_rows(rows + 6, 2, conv_one)
     repeat_rows(rows + 4, 2, conv_two)
+    total_ref[...] = sum_over_tiles(tiles, style_ref, got, send_sem, recv_sem)
 
 
 def second_kernel(
@@ -767,8 +756,8 @@
     def params(mib):
         return pltpu.CompilerParams(vmem_limit_bytes=mib * 2**20)
 
-    def remote(collective_id):
-        return pltpu.CompilerParams(collective_id=collective_id, has_side_effects=True, vmem_limit_bytes=8 * 2**20)
+    def remote(collective_id, mib=8):
+        return pltpu.CompilerParams(collective_id=collective_id, has_side_effects=True, vmem_limit_bytes=mib * 2**20)
 
     def other_way(w):
         return jnp.swapaxes(w, -1, -2)
@@ -778,38 +767,7 @@
     head = tuple(other_way(w) for w in (head_weight, head_momentum, head_average))
 
     edge = (crops, 2, HALO, cols)
-    x_lo, x_hi, t_lo, t_hi = pl.pallas_call(
-        lambda *refs: halo_kernel(tiles, *refs),
-        out_shape=(sds(edge, bf16), sds(edge, bf16), sds(edge, jnp.int32), sds(edge, jnp.int32)),
-        in_specs=[ANY] * 2,
-        out_specs=[ANY] * 4,
-        scratch_shapes=[DMA((4,)), DMA((4,))],
-        compiler_params=remote(1),
-        name="halo",
-    )(images, target_flow)
-    w1, w2, w3, wd3, wd2, wh, wht, b1, b2, b3, bh = pl.pallas_call(
-        weight_kernel,
-        out_shape=(
-            sds((128, 32), bf16),
-            sds((CH_TWO, 9 * CH_ONE), bf16),
-            sds((256, 9 * CH_TWO), bf16),
-            sds((128, 16 * CH_ONE), bf16),
-            sds((CH_ONE, 9 * CH_TWO), bf16),
-            sds((16, 128), bf16),
-            sds((128, 16), bf16),
-            sds((128, 128)),
-            sds((64, 128)),
-            sds((8, 128)),
-            sds((16, 128)),
-        ),
-        in_specs=[VMEM] * 5,
-        out_specs=[VMEM] * 11,
-        scratch_shapes=[pltpu.VMEM((32, 128), f32)],
-        compiler_params=params(8),
-        name="weights",
-    )(conv1_weight, conv2_weight, third[0], head[0], biases)
-
-    y, targets, h1, x2, x3, style_part = pl.pallas_call(
+    y, targets, h1, x2, x3, style_total, w3, wd3, wd2, wh, wht, b3, bh = pl.pallas_call(
         lambda *refs: first_kernel(tiles, *refs),
         out_shape=(
             sds((16 * (rows + 7), lanes), bf16),
@@ -818,22 +776,26 @@
             sds((96 * (rows + 6), lanes), bf16),
             sds((192 * (rows + 4), lanes), bf16),
             sds((8, 128)),
+            sds((256, 9 * CH_TWO), bf16),
+            sds((128, 16 * CH_ONE), bf16),
+            sds((CH_ONE, 9 * CH_TWO), bf16),
+            sds((16, 128), bf16),
+            sds((128, 16), bf16),
+            sds((8, 128)),
+            sds((16, 128)),
         ),
-        in_specs=[SMEM] + [VMEM] * 11,
-        out_specs=[VMEM] * 6,
-        compiler_params=params(12),
+        in_specs=[SMEM] + [VMEM] * 8,
+        out_specs=[VMEM] * 13,
+        scratch_shapes=[
+            pltpu.VMEM(edge, bf16), pltpu.VMEM(edge, bf16), pltpu.VMEM(edge, jnp.int32), pltpu.VMEM(edge, jnp.int32),
+            pltpu.VMEM((128, 32), bf16), pltpu.VMEM((CH_TWO, 9 * CH_ONE), bf16),
+            pltpu.VMEM((128, 128), f32), pltpu.VMEM((64, 128), f32), pltpu.VMEM((32, 128), f32),
+            pltpu.VMEM((8, 128), f32), pltpu.VMEM((tiles, 8, 128), f32),
+            DMA((4,)), DMA((4,)), DMA((tiles,)), DMA((tiles,)),
+        ],
+        compiler_params=remote(1, 14),
         name="forward_one_two",
-    )(nucleus, images, x_lo, x_hi, target_flow, t_lo, t_hi, cell_label, w1, b1, w2, b2)
-
-    style_total = pl.pallas_call(
-        lambda *refs: sum_kernel(tiles, *refs),
-        out_shape=sds((8, 128)),
-        in_specs=[VMEM],
-        out_specs=VMEM,
-        scratch_shapes=[pltpu.VMEM((tiles, 8, 128), f32), DMA((tiles,)), DMA((tiles,))],
-        compiler_params=remote(2),
-        name="style_sum",
-    )(style_part)
+    )(nucleus, images, target_flow, cell_label, conv1_weight, conv2_weight, third[0], head[0], biases)
 
     rim = (128, lanes)
     gc, rim_lo, rim_hi, go, k3, head_part, style_grad, sums_a, sg = pl.pallas_call(

time: 107 us -> 103 us (0.963)
  local copies, waits for them, and re-layouts: 10.3 us -> 8.29 us
  Pallas kernels: 94.7 us -> 92.9 us
    pallas_call x3 -> x0, Pallas kernels: 12.9 us -> none  [the longest x1 8.45 us: on_device(): pl.pallas_call(lambda *refs: sum_kernel(tiles, *refs), out_shape=sds((8,...]
    pallas_call x1, Pallas kernels: 13.2 us -> 25.2 us  [on_device(): pl.pallas_call(lambda *refs: first_kernel(tiles, *refs), out_shape=(sds((...]
    unnamed x58 -> x54, local copies, waits for them, and re-layouts: 10.3 us -> 8.29 us
where the time goes in v4:
time: 103 us
  Pallas kernels  92.9 us (90%)
  local copies, waits for them, and re-layouts  8.29 us (8%)
  between operations  1.62 us (2%)
    pallas_call x1, Pallas kernels, on_device(): pl.pallas_call(lambda *refs: second_kernel(tiles, crops, grad_scale, floa...  27.4 us
    pallas_call x1, Pallas kernels, on_device(): pl.pallas_call(lambda *refs: first_kernel(tiles, *refs), out_shape=(sds((...  25.2 us
    pallas_call x1, Pallas kernels, on_device(): pl.pallas_call(lambda *refs: reduce_kernel(tiles, images_count, part, *re...  16.7 us
    pallas_call x1, Pallas kernels, on_device(): pl.pallas_call(lambda *refs: third_kernel(tiles, crops, float(coarse_coun...  13.7 us
    pallas_call x1, Pallas kernels, on_device(): pl.pallas_call(lambda *refs: sum_rim_kernel(tiles, *refs), out_shape=(sds...  8.48 us
    unnamed x54, local copies, waits for them, and re-layouts  8.29 us

profile of v4, /device:TPU:0, one launch (start us, length us, event | category | flops | bytes accessed | tf_op | source)
XLA Modules:
  0.0 102.8 jit_solution(9011087500154908164)
XLA Ops:
  0.7 0.9 copy-done
  1.6 0.9 copy-done.2
  2.5 1.0 %copy-done.4 = s32[2,2,32,1024]{3,2,1,0:T(8,128)S(1)} copy-done((s32[2,2,32,1024]{3,2,1,0:T(8,128)S(1)}, s32[2,2,32,1024]{3,2,1,0:T(8,128)}, u32[]{:S(2)}) %copy-start.4) | copy-done | bytes 524312
  3.5 0.9 copy-done.5
  4.5 0.9 copy-done.6
  5.4 0.7 copy-done.12
  6.1 0.7 copy-done.18
  6.8 0.7 copy-done.20
  7.5 0.7 copy-done.26
  8.1 25.2 %forward_one_two.1 = (bf16[368,1024]{1,0:T(8,128)(2,1)S(1)}, f32[8,288,128]{2,1,0:T(8,128)S(1)}, bf16[2816,1024]{1,0:T(8,128)(2,1)S(1)}, bf16[2112,1024]{1,0:T(8...) custom-call(s32[2]{0:T(128)S(1)} %copy-done.26, ...), custom_call_target="tpu_custom_call" | custom-call | tf_op jit(solution)/shard_map/forward_one_two/pallas_call | solution.py:770
  33.4 0.0 copy-start.11
  33.4 0.7 copy-done.11
  34.1 27.4 %forward_three_back.1 = (f32[1152,1024]{1,0:T(8,128)S(1)}, bf16[128,1024]{1,0:T(8,128)(2,1)S(1)}, bf16[128,1024]{1,0:T(8,128)(2,1)S(1)}, bf16[256,1024]{1,0:T(8,...) custom-call(bf16[2816,1024]{1,0:T(8,128)(2,1)S(1)} %get-tuple-elemen, ...), custom_call_target="tpu_custom_call" | custom-call | tf_op jit(solution)/shard_map/forward_three_back/pallas_call | solution.py:801
  61.5 8.5 %style_grad_sum.1 = (f32[8,128]{1,0:T(8,128)S(1)}, bf16[128,1024]{1,0:T(8,128)(2,1)S(1)}, bf16[128,1024]{1,0:T(8,128)(2,1)S(1)}) custom-call(f32[8,128]{1,0:T(8,128)S(1)} %get-tuple-element.78.refs_0_, bf16[128,1024]{1,0:T(8,128)(2,1)S(1)} %get-tuple-element.79.refs_1_, bf16[128,1024]{1,0:T(8,128)(2,1)S(1)} %get-tuple-element.80.refs_2_), custom_call_target="tpu_custom_call" | custom-call | tf_op jit(solution)/shard_map/style_grad_sum/pallas_call | solution.py:828
  70.0 0.0 copy-start.7
  70.0 0.0 copy-start.8
  70.1 0.0 copy-start.13
  70.1 0.0 copy-start.14
  70.1 0.0 copy-start.17
  70.1 0.0 copy-start.19
  70.2 0.0 copy-start.22
  70.2 13.7 %back_two_one.1 = (f32[160,128]{1,0:T(8,128)S(1)}, f32[32,128]{1,0:T(8,128)S(1)}, f32[8,128]{1,0:T(8,128)S(1)}) custom-call(f32[1152,1024]{1,0:T(8,128)S(1)} %get-tuple-element.77.refs_0_, bf16[128,1024]{1,0:T(8,128)(2,1)S(1)} %get-tuple-element.81.refs_1_, bf16[128,1024]{1,0:T(8,128)(2,1)S(1)} %get-tuple-element.82.refs_2_, ...), custom_call_target="tpu_custom_call" | custom-call | tf_op jit(solution)/shard_map/back_two_one/pallas_call | solution.py:840
  83.9 16.7 %gradient_sum.1.refs_1_ = f32[384,128]{1,0:T(8,128)S(1)} custom-call(f32[144,128]{1,0:T(8,128)S(1)} %get-tuple-element.76.refs_0_, f32[160,128]{1,0:T(8,128)S(1)} %get-tuple-element.88.refs_1_, f32[32,128]{1,0:T(8,128)S(1)} %get-tuple-element.89.refs_2_, f32[16,128]{1,0:T(8,128)S(1)} %get-tuple-element.90.refs_3_, f32[16,128]{1,0:T(8,128)S(1)} %get-tuple-element.91.refs_4_, ...), custom_call_target="tpu_custom_call" | custom-call | tf_op jit(solution)/shard_map/gradient_sum/pallas_call | solution.py:854
  101.4 1.4 %update.1 = (f32[3,3,2,32]{3,2,1,0:T(2,128)}, f32[3,3,2,32]{3,2,1,0:T(2,128)}, f32[3,3,2,32]{3,2,1,0:T(2,128)}, f32[3,3,32,64]{3,2,1,0:T(8,128)}, f32[3,3,32,64]...) custom-call(s32[1]{0:T(128)S(6)} %copy.42.refs_0_, ...), custom_call_target="tpu_custom_call" | custom-call | tf_op jit(solution)/shard_map/update/pallas_call | solution.py:877
  (36 shorter events, 0.1 us)
Async XLA Ops:
  0.7 0.9 copy-start
  1.6 0.9 copy-start.2
  2.5 1.0 %copy-start.4 = (s32[2,2,32,1024]{3,2,1,0:T(8,128)S(1)}, s32[2,2,32,1024]{3,2,1,0:T(8,128)}, u32[]{:S(2)}) copy-start(s32[2,2,32,1024]{3,2,1,0:T(8,128)} %refs_2_.2) | copy-start | bytes 1572868
  3.5 0.9 copy-start.5
  4.5 0.9 copy-start.6
  5.4 0.7 copy-start.12
  33.4 0.7 copy-start.11
  70.0 31.2 %copy-start.1 = (f32[3,3,32,64]{3,2,1,0:T(8,128)S(1)}, f32[3,3,32,64]{3,2,1,0:T(8,128)}, u32[]{:S(2)}) copy-start(f32[3,3,32,64]{3,2,1,0:T(8,128)} %refs_5_.3) | copy-start | bytes 221188
  70.0 31.2 %copy-start.3 = (f32[3,3,64,32]{2,3,1,0:T(8,128)S(1)}, f32[3,3,64,32]{2,3,1,0:T(8,128)}, u32[]{:S(2)}) copy-start(f32[3,3,64,32]{2,3,1,0:T(8,128)} %param.34) | copy-start | bytes 221188
  70.0 31.2 %copy-start.7 = (f32[3,3,32,64]{3,2,1,0:T(8,128)S(1)}, f32[3,3,32,64]{3,2,1,0:T(8,128)}, u32[]{:S(2)}) copy-start(f32[3,3,32,64]{3,2,1,0:T(8,128)} %refs_6_.1) | copy-start | bytes 221188
  70.0 31.2 %copy-start.8 = (f32[3,3,32,64]{3,2,1,0:T(8,128)S(1)}, f32[3,3,32,64]{3,2,1,0:T(8,128)}, u32[]{:S(2)}) copy-start(f32[3,3,32,64]{3,2,1,0:T(8,128)} %refs_7_.1) | copy-start | bytes 221188
  70.1 31.2 %copy-start.9 = (f32[3,3,64,32]{2,3,1,0:T(8,128)S(1)}, f32[3,3,64,32]{2,3,1,0:T(8,128)}, u32[]{:S(2)}) copy-start(f32[3,3,64,32]{2,3,1,0:T(8,128)} %param.35) | copy-start | bytes 221188
  70.1 31.2 %copy-start.10 = (f32[3,3,64,32]{2,3,1,0:T(8,128)S(1)}, f32[3,3,64,32]{2,3,1,0:T(8,128)}, u32[]{:S(2)}) copy-start(f32[3,3,64,32]{2,3,1,0:T(8,128)} %param.36) | copy-start | bytes 221188
  70.1 31.2 %copy-start.13 = (f32[3,3,2,32]{3,2,1,0:T(2,128)S(1)}, f32[3,3,2,32]{3,2,1,0:T(2,128)}, u32[]{:S(2)}) copy-start(f32[3,3,2,32]{3,2,1,0:T(2,128)} %refs_2_.3) | copy-start | bytes 6916
  70.1 31.2 %copy-start.14 = (f32[64,32]{0,1:T(8,128)S(1)}, f32[64,32]{0,1:T(8,128)}, u32[]{:S(2)}) copy-start(f32[64,32]{0,1:T(8,128)} %param.38) | copy-start | bytes 24580
  70.1 31.2 %copy-start.15 = (f32[64,32]{0,1:T(8,128)S(1)}, f32[64,32]{0,1:T(8,128)}, u32[]{:S(2)}) copy-start(f32[64,32]{0,1:T(8,128)} %param.39) | copy-start | bytes 24580
  70.1 31.2 %copy-start.16 = (f32[3,3,2,32]{3,2,1,0:T(2,128)S(1)}, f32[3,3,2,32]{3,2,1,0:T(2,128)}, u32[]{:S(2)}) copy-start(f32[3,3,2,32]{3,2,1,0:T(2,128)} %refs_3_.3) | copy-start | bytes 6916
  70.1 31.2 %copy-start.17 = (f32[3,3,2,32]{3,2,1,0:T(2,128)S(1)}, f32[3,3,2,32]{3,2,1,0:T(2,128)}, u32[]{:S(2)}) copy-start(f32[3,3,2,32]{3,2,1,0:T(2,128)} %refs_4_.3) | copy-start | bytes 6916
  70.1 31.2 %copy-start.19 = (f32[32,3]{0,1:T(4,128)S(1)}, f32[32,3]{0,1:T(4,128)}, u32[]{:S(2)}) copy-start(f32[32,3]{0,1:T(4,128)} %param.40) | copy-start | bytes 1156
  70.2 31.2 %copy-start.21 = (f32[163]{0:T(256)S(1)}, f32[163]{0:T(256)}, u32[]{:S(2)}) copy-start(f32[163]{0:T(256)} %refs_17_.1) | copy-start | bytes 1960
  70.2 31.2 %copy-start.22 = (f32[32,3]{0,1:T(4,128)S(1)}, f32[32,3]{0,1:T(4,128)}, u32[]{:S(2)}) copy-start(f32[32,3]{0,1:T(4,128)} %param.41) | copy-start | bytes 1156
  70.2 31.2 %copy-start.23 = (f32[32,3]{0,1:T(4,128)S(1)}, f32[32,3]{0,1:T(4,128)}, u32[]{:S(2)}) copy-start(f32[32,3]{0,1:T(4,128)} %param.42) | copy-start | bytes 1156
  70.2 31.2 %copy-start.24 = (f32[163]{0:T(256)S(1)}, f32[163]{0:T(256)}, u32[]{:S(2)}) copy-start(f32[163]{0:T(256)} %refs_18_.1) | copy-start | bytes 1960
  70.2 31.2 %copy-start.25 = (f32[163]{0:T(256)S(1)}, f32[163]{0:T(256)}, u32[]{:S(2)}) copy-start(f32[163]{0:T(256)} %refs_19_.1) | copy-start | bytes 1960
  (3 other events, 2.0 us)

commit v5 on v4

v5 whole, which is shorter than its diff:
```python
import math

import jax
import jax.numpy as jnp
from jax import lax
from jax.experimental import pallas as pl
from jax.experimental.pallas import tpu as pltpu
from jax.sharding import PartitionSpec as P

CH_ONE = 32
CH_TWO = 64
OUT_CH = 3

momentum_rate = 0.9
learn_rate = 0.02
decay_rate = 0.0001
norm_eps = 1e-05
highest = lax.Precision.HIGHEST
f32 = jnp.float32
bf16 = jnp.bfloat16

HALO = 8
VMEM = pl.BlockSpec(memory_space=pltpu.VMEM)
SMEM = pl.BlockSpec(memory_space=pltpu.SMEM)
ANY = pl.BlockSpec(memory_space=pl.ANY)
MESH = pl.DeviceIdType.MESH
DMA = pltpu.SemaphoreType.DMA

BLOCK_ROWS = ((144, 16, 16, 8), (160, 8), (8, 8))


def dot(a, b):
    return jnp.dot(a, b, preferred_element_type=f32)


def dot_nt(a, b, precision=None):
    return lax.dot_general(a, b, (((1,), (1,)), ((), ())), preferred_element_type=f32, precision=precision)


def from_left(x, crops=1):
    lane = lax.broadcasted_iota(jnp.int32, x.shape, 1)
    return jnp.where(lane % (x.shape[1] // crops) == 0, 0.0, pltpu.roll(x, 1, 1))


def from_right(x, crops=1):
    width = x.shape[1] // crops
    lane = lax.broadcasted_iota(jnp.int32, x.shape, 1)
    return jnp.where(lane % width == width - 1, 0.0, pltpu.roll(x, x.shape[1] - 1, 1))


def three_columns(mid, crops):
    x = mid.astype(f32)
    return jnp.concatenate([from_left(x, crops).astype(bf16), mid, from_right(x, crops).astype(bf16)], axis=0)


def crop_rows(crops, lanes):
    row = lax.broadcasted_iota(jnp.int32, (8, lanes), 0)
    lane = lax.broadcasted_iota(jnp.int32, (8, lanes), 1)
    return jnp.where(lane // (lanes // crops) == row, 1.0, 0.0).astype(bf16)


def repeat_rows(count, step, body):
    def run(k, carry):
        body([k * step + j for j in range(step)])
        return carry

    lax.fori_loop(0, count // step, run, 0)


def turn(x, by, axis):
    by = by % x.shape[axis]
    return pltpu.roll(x, by, axis) if by else x


def lane_group(x, group, size=32):
    lane = lax.broadcasted_iota(jnp.int32, x.shape, 1)
    return jnp.where(lane // size == group, x, 0.0)


def over_phases(x):
    return (x + turn(x, 32, 1)) + (turn(x, 64, 1) + turn(x, 96, 1))


def as_column(row):
    return jnp.transpose(jnp.broadcast_to(row, (128, 128)))


def fold_lanes(x):
    total = x[:, 0:128]
    for k in range(1, x.shape[1] // 128):
        total = total + x[:, 128 * k : 128 * (k + 1)]
    return total


def wide(tile, width):
    return jnp.concatenate([tile] * (width // 128), axis=1)


def rows_of(ref, start, size):
    return ref[pl.ds(pl.multiple_of(start, 16), size), :]


def put_rows(ref, start, value):
    ref[pl.ds(pl.multiple_of(start, 16), value.shape[0]), :] = value


def put_lanes(ref, start, value):
    for k in range(value.shape[1] // 128):
        ref[k, pl.ds(pl.multiple_of(start, 16), value.shape[0]), :] = value[:, 128 * k : 128 * (k + 1)]


def get_lanes(ref, start, size, stride=None):
    spot = pl.ds(start, size, stride=stride) if stride else pl.ds(pl.multiple_of(start, 16), size)
    return jnp.concatenate([ref[k, spot, :] for k in range(ref.shape[0])], axis=1)


def strip_edges(tiles, rows):
    me = lax.axis_index("tile")
    return -me * rows, (tiles - me) * rows


def valid(row, edge):
    return jnp.where((row >= edge[0]) & (row < edge[1]), 1.0, 0.0).astype(f32)


def greet(sizes):
    gate = pltpu.get_barrier_semaphore()
    for axis, count in sizes:
        me = lax.axis_index(axis)
        for j in range(1, count):
            pl.semaphore_signal(gate, inc=1, device_id={axis: lax.rem(me + j, count)}, device_id_type=MESH)
    return lambda: pl.semaphore_wait(gate, sum(count - 1 for _, count in sizes))


def send_all(count, axis, source, target, send_sem, recv_sem):
    me = lax.axis_index(axis)
    copies = []
    for j in range(1, count):
        to = lax.rem(me + j, count)
        copy = pltpu.make_async_remote_copy(
            src_ref=source(to), dst_ref=target, send_sem=send_sem.at[j - 1], recv_sem=recv_sem.at[j - 1],
            device_id={axis: to}, device_id_type=MESH,
        )
        copy.start()
        copies.append(copy)
    return copies


def wait_all(copies):
    for copy in copies:
        copy.wait()


def in_order(ref, count):
    total = ref[0]
    for k in range(1, count):
        total = total + ref[k]
    return total


def swap_edges(tiles, pairs, send_sem, recv_sem):
    me = lax.axis_index("tile")
    copies = []
    for k, (low, high, from_before, from_after) in enumerate(pairs):
        down = pltpu.make_async_remote_copy(
            src_ref=high, dst_ref=from_before, send_sem=send_sem.at[2 * k], recv_sem=recv_sem.at[2 * k],
            device_id={"tile": jnp.minimum(me + 1, tiles - 1)}, device_id_type=MESH,
        )
        up = pltpu.make_async_remote_copy(
            src_ref=low, dst_ref=from_after, send_sem=send_sem.at[2 * k + 1], recv_sem=recv_sem.at[2 * k + 1],
            device_id={"tile": jnp.maximum(me - 1, 0)}, device_id_type=MESH,
        )
        copies.append((down, up))

    @pl.when(me < tiles - 1)
    def _():
        for down, _up in copies:
            down.start()

    @pl.when(me > 0)
    def _():
        for _down, up in copies:
            up.start()

    def finish():
        @pl.when(me < tiles - 1)
        def _():
            for down, up in copies:
                down.wait_send()
                up.wait_recv()

        @pl.when(me > 0)
        def _():
            for down, up in copies:
                up.wait_send()
                down.wait_recv()

    return finish


def share(count, axis, source, got, send_sem, recv_sem):
    me = lax.axis_index(axis)
    got[me] = source[...]
    return send_all(count, axis, lambda to: source, got.at[me], send_sem, recv_sem)


class Reduction:
    def __init__(self, tiles, images, pay, got, own, met, sems):
        self.tiles, self.images = tiles, images
        self.pay, self.got, self.own, self.met, self.sems = pay, got, own, met, sems
        self.part = own.shape[0]
        self.me = lax.axis_index("tile")

    def block(self, k):
        return pl.ds(pl.multiple_of(k * self.part, 8), self.part)

    def scatter(self):
        self.got[self.me] = self.pay[self.block(self.me), :]
        self.copies = send_all(
            self.tiles, "tile", lambda to: self.pay.at[self.block(to), :], self.got.at[self.me], self.sems[0], self.sems[1]
        )

    def across(self):
        wait_all(self.copies)
        self.own[...] = in_order(self.got, self.tiles)
        self.copies = share(self.images, "img", self.own, self.met, self.sems[2], self.sems[3])

    def gather(self, full):
        wait_all(self.copies)
        full[self.block(self.me), :] = in_order(self.met, self.images)
        here = full.at[self.block(self.me), :]
        self.copies = send_all(self.tiles, "tile", lambda to: here, here, self.sems[4], self.sems[5])

    def finish(self):
        wait_all(self.copies)


def first_tables(k1_ref, k2_ref, bias_ref, w1_ref, w2_ref, b1_ref, b2_ref, base_ref):
    base_ref[...] = jnp.zeros_like(base_ref)
    for a in range(3):
        for b in range(3):
            for i in range(2):
                base_ref[8 * a + 4 * i + b : 8 * a + 4 * i + b + 1, 0:32] = k1_ref[a, b, i : i + 1, :]
    base = base_ref[...]
    w1t = jnp.zeros((32, 128), f32)
    for p in range(4):
        w1t = w1t + turn(turn(base, 8 * (p // 2) + p % 2, 0), 32 * p, 1)
    w1_ref[...] = jnp.transpose(w1t).astype(bf16)

    k2 = [[k2_ref[a, b].astype(bf16).astype(f32) for b in range(3)] for a in range(3)]
    w2t = jnp.concatenate([k2[a][b] for a in range(3) for b in range(3)], axis=0)
    w2_ref[...] = jnp.transpose(w2t).astype(bf16)
    bias = bias_ref[...].reshape(1, -1)
    b1_ref[...] = as_column(jnp.concatenate([bias[:, 0:32]] * 4, axis=1))
    b2_ref[...] = as_column(jnp.concatenate([bias[:, 32:96]] * 2, axis=1))[0:64]


def later_tables(k2_ref, k3_ref, kh_ref, bias_ref, w3_ref, wd3_ref, wd2_ref, wh_ref, wht_ref, b3_ref, bh_ref):
    k2 = [[k2_ref[a, b].astype(bf16).astype(f32) for b in range(3)] for a in range(3)]
    wd2_ref[...] = jnp.concatenate([k2[2 - s][2 - t] for s in range(3) for t in range(3)], axis=1).astype(bf16)

    def tap_sum(first, second):
        total = None
        for a in first:
            for b in second:
                total = k3[a][b] if total is None else total + k3[a][b]
        return jnp.zeros((CH_ONE, CH_TWO), f32) if total is None else total

    k3 = [[k3_ref[a, b].astype(bf16).astype(f32) for b in range(3)] for a in range(3)]
    up = [[[a for a in range(3) if (p + a + 1) // 2 == r] for r in range(3)] for p in range(2)]
    for p in range(4):
        w3 = jnp.concatenate([tap_sum(up[p // 2][r], up[p % 2][c]) for r in range(3) for c in range(3)], axis=1)
        w3_hi = w3.astype(bf16)
        w3_ref[32 * p : 32 * (p + 1), :] = w3_hi
        w3_ref[128 + 32 * p : 160 + 32 * p, :] = (w3 - w3_hi.astype(f32)).astype(bf16)
    down = ((2,), (1, 2), (0, 1), (0,))
    wd3 = jnp.transpose(jnp.concatenate([tap_sum(down[r], down[c]) for r in range(4) for c in range(4)], axis=0))
    wd3_hi = wd3.astype(bf16)
    wd3_ref[0:64, :] = wd3_hi
    wd3_ref[64:128, :] = (wd3 - wd3_hi.astype(f32)).astype(bf16)

    row = lax.broadcasted_iota(jnp.int32, (16, 128), 0)
    lane = lax.broadcasted_iota(jnp.int32, (16, 128), 1)
    wh = jnp.zeros((16, 128), f32)
    for o in range(OUT_CH):
        one = jnp.concatenate([kh_ref[o : o + 1, :]] * 4, axis=1)
        wh = jnp.where(row // 4 == o, jnp.broadcast_to(one, (16, 128)), wh)
    wh = jnp.where(row % 4 == lane // 32, wh, 0.0)
    wh_ref[...] = wh.astype(bf16)
    wht_ref[...] = jnp.transpose(wh).astype(bf16)

    bias = bias_ref[...].reshape(1, -1)
    b3_ref[...] = jnp.zeros_like(b3_ref)
    b3_ref[0:1, :] = jnp.concatenate([bias[:, 96:128] + bias[:, 128:160]] * 4, axis=1)
    bh = jnp.zeros((16, 128), f32)
    for o in range(OUT_CH):
        bh = jnp.where(row // 4 == o, jnp.broadcast_to(bias[:, 160 + o : 161 + o], (16, 128)), bh)
    bh_ref[...] = bh


def split_columns(x, select):
    even, odd = [], []
    for k in range(x.shape[1] // 256):
        piece = dot(x[:, 256 * k : 256 * (k + 1)], select)
        even.append(piece[:, 0:128])
        odd.append(piece[:, 128:256])
    return jnp.concatenate(even, axis=1), jnp.concatenate(odd, axis=1)


def step_kernel(
    tiles, images, scale, coarse_count,
    nucleus_ref, x_ref, t_ref, label_ref, k1_ref, k2_ref, k3_ref, kh_ref, bias_ref, ws_ref,
    o_ref,
    x_lo, x_hi, t_lo, t_hi,
    w1_ref, w2_ref, w3_ref, wd3_ref, wd2_ref, wh_ref, wht_ref, b1_ref, b2_ref, b3_ref, bh_ref, base_ref,
    y_ref, t_out, h1_ref, x2_ref, x3_ref, h3_ref, m_ref, fe_ref, go_ref, go_out, g3_ref, gc_ref,
    rim_lo, rim_hi, rim_up, rim_dn,
    style_ref, style_got, sg_ref, sg_got, head_ref, sums_ref, d3_ref, d2_ref, d1_ref,
    pay_a, got_a, own_a, met_a, full_a, pay_b, got_b, own_b, met_b, full_b,
    pay_c, got_c, own_c, met_c,
    halo_send, halo_recv, s1_send, s1_recv, s2_send, s2_recv, rim_send, rim_recv,
    *sems,
):
    reduce_a = Reduction(tiles, images, pay_a, got_a, own_a, met_a, sems[0:6])
    reduce_b = Reduction(tiles, images, pay_b, got_b, own_b, met_b, sems[6:12])
    arrived = greet((("tile", tiles), ("img", images)))
    first_tables(k1_ref, k2_ref, bias_ref, w1_ref, w2_ref, b1_ref, b2_ref, base_ref)
    arrived()
    last = x_ref.shape[2] - HALO
    finish_halo = swap_edges(
        tiles,
        [
            (ref.at[:, :, pl.ds(0, HALO), :], ref.at[:, :, pl.ds(last, HALO), :], lo, hi)
            for ref, lo, hi in ((x_ref, x_lo, x_hi), (t_ref, t_lo, t_hi))
        ],
        halo_send, halo_recv,
    )
    crops = x_ref.shape[0]
    width = x_ref.shape[3] // 2
    lanes = crops * width
    height = x_ref.shape[2]
    rows = height // 2
    edge = strip_edges(tiles, rows)
    r_id = lax.broadcasted_iota(jnp.int32, (256, 256), 0)
    c_id = lax.broadcasted_iota(jnp.int32, (256, 256), 1)
    select = jnp.where(r_id == 2 * (c_id % 128) + c_id // 128, 1.0, 0.0).astype(bf16)
    x_rows = 2 * (height + 2 * HALO)
    y_rows = y_ref.shape[0]
    ri = lax.broadcasted_iota(jnp.int32, (y_rows, 4 * x_rows), 0)
    ci = lax.broadcasted_iota(jnp.int32, (y_rows, 4 * x_rows), 1)
    fine = 2 * (ri // 16) + (ri // 8) % 2 - 7
    channel = (ri // 4) % 2
    source = jnp.where(
        fine < 0,
        2 * height + channel * HALO + fine + HALO,
        jnp.where(
            fine < height, channel * height + fine, 2 * height + 2 * HALO + channel * HALO + fine - height
        ),
    )
    perm_x = jnp.where(ci == (ri % 4) * x_rows + source, 1.0, 0.0).astype(bf16)
    has_up, has_dn = edge[0] < 0, edge[1] > rows

    def both_columns(of_crop):
        even, odd = [], []
        for c in range(crops):
            first, second = split_columns(of_crop(c), select)
            even.append(first)
            odd.append(second)
        return jnp.concatenate(even, axis=1), jnp.concatenate(odd, axis=1)

    def own_rows(c):
        return jnp.concatenate([x_ref[c, k] for k in range(2)], axis=0)

    def halo_rows(c):
        pieces = [jnp.where(has_up, x_lo[c, k].astype(f32), 0.0) for k in range(2)]
        pieces += [jnp.where(has_dn, x_hi[c, k].astype(f32), 0.0) for k in range(2)]
        return jnp.concatenate(pieces, axis=0).astype(bf16)

    def target_rows(c):
        pieces = [t_ref[c, 0].astype(f32), t_ref[c, 1].astype(f32), label_ref[c].astype(f32)]
        pieces += [jnp.where(has_up, t_lo[c, k], 0).astype(f32) for k in range(2)]
        pieces += [jnp.where(has_dn, t_hi[c, k], 0).astype(f32) for k in range(2)]
        return jnp.concatenate(pieces, axis=0).astype(bf16)

    own_part = both_columns(own_rows)
    finish_halo()
    even, odd = (jnp.concatenate([a, b], axis=0) for a, b in zip(own_part, both_columns(halo_rows)))
    row = lax.broadcasted_iota(jnp.int32, (x_rows, lanes), 0)
    crop = lax.broadcasted_iota(jnp.int32, (x_rows, lanes), 1) // width
    second = jnp.where(row < 2 * height, row // height, (row - 2 * height) // HALO % 2) == 1
    gate = jnp.ones((x_rows, lanes), f32)
    for c in range(crops):
        gate = jnp.where(second & (crop == c), nucleus_ref[c].astype(f32), gate)
    even, odd = even * gate, odd * gate
    stack = jnp.concatenate([from_left(odd, crops), even, odd, from_right(even, crops)], axis=0)
    y_ref[...] = dot(perm_x, stack.astype(bf16)).astype(bf16)
    ones = crop_rows(crops, lanes)
    style_ref[...] = jnp.zeros_like(style_ref)

    def conv_one(ks):
        pre = [dot(w1_ref[...], rows_of(y_ref, k * 16, 32)) for k in ks]
        for k, p in zip(ks, pre):
            keep = valid(k - 3, edge)
            hidden = (jnp.maximum(p + wide(b1_ref[...], lanes), 0.0) * keep).astype(bf16)
            put_rows(h1_ref, k * 128, hidden)
            h = hidden.astype(f32)
            pooled = (0.25 * ((h[0:32] + h[32:64]) + (h[64:96] + h[96:128]))).astype(bf16)
            put_rows(x2_ref, k * 96, three_columns(pooled, crops))

    def conv_two(qs):
        pre = [dot(w2_ref[...], rows_of(x2_ref, q * 96, 288)) for q in qs]
        sums = 0.0
        for q, p in zip(qs, pre):
            row = q - 2
            keep = valid(row, edge)
            own = jnp.where((row >= 0) & (row < rows), 1.0, 0.0).astype(f32)
            hidden = (jnp.maximum(p + wide(b2_ref[...], lanes), 0.0) * keep).astype(bf16)
            put_rows(x3_ref, q * 192, three_columns(hidden, crops))
            sums = sums + dot_nt(ones, hidden) * own
        style_ref[:, 0:64] += sums

    repeat_rows(rows + 6, 2, conv_one)
    repeat_rows(rows + 4, 2, conv_two)
    style_copies = share(tiles, "tile", style_ref, style_got, s1_send, s1_recv)

    t_rows = 3 * height + 4 * HALO
    ri = lax.broadcasted_iota(jnp.int32, (t_out.shape[1], 2 * t_rows), 0)
    ci = lax.broadcasted_iota(jnp.int32, (t_out.shape[1], 2 * t_rows), 1)
    part = (ri // 4) % 4
    fine = 2 * (ri // 16) + (ri // 2) % 2 - 2
    source = jnp.where(
        fine < 0,
        3 * height + part * HALO + fine + HALO,
        jnp.where(fine < height, part * height + fine, 3 * height + 2 * HALO + part * HALO + fine - height),
    )
    outside = (fine < 0) | (fine >= height)
    known = (part < 2) | ((part == 2) & jnp.logical_not(outside))
    perm_t = jnp.where((ci == (ri % 2) * t_rows + source) & known, 1.0, 0.0).astype(bf16)
    even, odd = both_columns(target_rows)
    put_lanes(t_out, 0, dot(perm_t, jnp.concatenate([even, odd], axis=0).astype(bf16)))
    later_tables(k2_ref, k3_ref, kh_ref, bias_ref, w3_ref, wd3_ref, wd2_ref, wh_ref, wht_ref, b3_ref, bh_ref)
    wait_all(style_copies)
    style_raw = in_order(style_got, tiles)[:, 0:64] / coarse_count
    style_inv = lax.rsqrt(jnp.mean(style_raw * style_raw, axis=1, keepdims=True) + norm_eps)
    unit = style_raw * style_inv
    vec = dot_nt(unit, ws_ref[...], highest)
    vec = jnp.concatenate([vec] * 4, axis=1) + b3_ref[0:1, :]
    bias3 = [as_column(vec[c : c + 1]) for c in range(crops)]

    def forward(ks):
        pre = [dot(w3_ref[...], rows_of(x3_ref, k * 192, 576)) for k in ks]
        hs = []
        for k, both in zip(ks, pre):
            p = both[0:128] + both[128:256] + jnp.concatenate([wide(b, width) for b in bias3], axis=1)
            h1 = rows_of(h1_ref, (k + 2) * 128, 128).astype(f32)
            h3 = (jnp.maximum(p, 0.0) + h1).astype(bf16)
            put_rows(h3_ref, k * 128, h3)
            put_rows(m_ref, k * 128, jnp.where(p > 0, 1.0, 0.0).astype(bf16))
            hs.append(h3)
        outs = [dot(wh_ref[...], h) for h in hs]
        for k, o in zip(ks, outs):
            o = o + wide(bh_ref[...], lanes)
            t = get_lanes(t_out, k * 16, 16)
            fe = (o[0:8] - 0.25 * t[0:8]) * valid(k - 1, edge)
            put_lanes(fe_ref, k * 16, jnp.concatenate([fe, o[8:16]], axis=0))

    repeat_rows(rows + 2, 2, forward)

    r_id = lax.broadcasted_iota(jnp.int32, (rows, lanes), 0)
    above = jnp.where(r_id - 1 >= edge[0], 1.0, 0.0)
    below = jnp.where(r_id + 1 < edge[1], 1.0, 0.0)
    go_ref[...] = jnp.zeros_like(go_ref)

    def at(part, off):
        return get_lanes(fe_ref, 16 * (1 + off) + part, rows, 16)

    def column_part(pr, off):
        odd, even = at(4 + 2 * pr + 1, off), at(4 + 2 * pr, off)
        return 0.5 * (odd - from_left(odd, crops)), 0.5 * (from_right(even, crops) - even)

    loss = jnp.zeros((rows, 128), f32)
    e0 = [at(k, 0) for k in range(4)]
    e1 = [at(4 + k, 0) for k in range(4)]
    cols0, cols1 = column_part(0, 0), column_part(1, 0)
    cols_up, cols_dn = column_part(1, -1), column_part(0, 1)
    spread = [None] * 4
    g_up, g_dn = [None] * 2, [None] * 2
    for pc in range(2):
        f_up, f_dn = at(2 + pc, -1), at(pc, 1)
        spread[pc] = 0.5 * (e0[2 + pc] - f_up) + cols0[pc]
        spread[2 + pc] = 0.5 * (f_dn - e0[pc]) + cols1[pc]
        g_up[pc] = 2.0 * scale * above * (0.5 * (e0[pc] - at(pc, -1)) + cols_up[pc])
        g_dn[pc] = 2.0 * scale * below * (0.5 * (at(2 + pc, 1) - e0[2 + pc]) + cols_dn[pc])
    g = [2.0 * scale * v for v in spread]
    for pr in range(2):
        even, odd = g[2 * pr], g[2 * pr + 1]
        col = [0.5 * (odd - from_left(odd, crops)), 0.5 * (from_right(even, crops) - even)]
        for pc in range(2):
            k = 2 * pr + pc
            if pr == 0:
                row_part = 0.5 * (g[2 + pc] - g_up[pc])
            else:
                row_part = 0.5 * (g_dn[pc] - g[pc])
            logit = at(8 + k, 0)
            label = get_lanes(t_out, 16 + 8 + k, rows, 16)
            ex = jnp.exp(-jnp.abs(logit))
            sig = jnp.where(logit >= 0, 1.0, ex) / (1.0 + ex)
            grads = (2.0 * scale * e0[k] - row_part, 2.0 * scale * e1[k] - col[pc], scale * (sig - label))
            for part in range(OUT_CH):
                for j in range(lanes // 128):
                    go_ref[j, pl.ds(4 * part + k, rows, stride=16), :] = grads[part][:, 128 * j : 128 * (j + 1)]
            term = jnp.maximum(logit, 0.0) + jnp.log1p(ex) - label * logit
            loss = loss + fold_lanes(e0[k] * e0[k] + e1[k] * e1[k] + spread[k] * spread[k] + term)

    sums_ref[...] = jnp.zeros_like(sums_ref)
    sums_ref[4:5, :] = jnp.sum(loss, axis=0, keepdims=True)
    head_ref[...] = jnp.zeros_like(head_ref)
    sg_ref[...] = jnp.zeros_like(sg_ref)
    d3_ref[...] = jnp.zeros_like(d3_ref)
    for k in (0, 1, rows + 2, rows + 3):
        g3_ref[256 * k : 256 * (k + 1), :] = jnp.zeros((256, lanes), bf16)

    def backward(rs):
        gos = [get_lanes(go_ref, r * 16, 16).astype(bf16) for r in rs]
        gts = [dot(wht_ref[...], go) for go in gos]
        head, gsum, sg = 0.0, 0.0, 0.0
        for r, go, gt in zip(rs, gos, gts):
            put_rows(go_out, r * 16, go)
            spot = (r + 1) * 128
            head = head + dot_nt(go, rows_of(h3_ref, spot, 128))
            gsum = gsum + dot_nt(ones, go)
            g = gt.astype(bf16).astype(f32) * rows_of(m_ref, spot, 128).astype(f32)
            gb = g.astype(bf16)
            sg = sg + dot_nt(ones, gb)
            parts = []
            for pr in range(2):
                even, odd = g[64 * pr : 64 * pr + 32], g[64 * pr + 32 : 64 * pr + 64]
                parts += [
                    from_left(odd, crops).astype(bf16),
                    gb[64 * pr : 64 * pr + 64],
                    from_right(even, crops).astype(bf16),
                ]
            put_rows(g3_ref, (r + 2) * 256, jnp.concatenate(parts, axis=0))
        head_ref[...] += head
        sums_ref[3:4, 0:16] += jnp.sum(gsum, axis=0, keepdims=True)
        sg_ref[...] += sg

    repeat_rows(rows, 2, backward)
    sg_copies = share(tiles, "tile", sg_ref, sg_got, s2_send, s2_recv)

    def down(ks):
        both = [dot(wd3_ref[...], rows_of(g3_ref, k * 256 + 128, 512)) for k in ks]
        for k, b in zip(ks, both):
            put_rows(gc_ref, k * 64, b[0:64] + b[64:128])

    down([0, 1])
    rim_lo[...] = gc_ref[0:128, :].astype(bf16)
    down([rows, rows + 1])
    rim_hi[...] = gc_ref[64 * rows : 64 * rows + 128, :].astype(bf16)
    finish_rims = swap_edges(tiles, [(rim_lo, rim_hi, rim_up, rim_dn)], rim_send, rim_recv)
    repeat_rows(rows - 2, 2, lambda ks: down([k + 2 for k in ks]))

    def weights_three(rs):
        d3 = 0.0
        for r in rs:
            spot = (r + 2) * 256
            gb = jnp.concatenate([rows_of(g3_ref, spot + 32, 64), rows_of(g3_ref, spot + 160, 64)], axis=0)
            d3 = d3 + dot_nt(rows_of(x3_ref, (r + 1) * 192, 576), gb)
        d3_ref[...] += d3

    repeat_rows(rows, 2, weights_three)
    d3 = jnp.transpose(d3_ref[...])
    for block in range(5):
        packed = jnp.zeros((CH_ONE, 128), f32)
        for tap in range(2 * block, min(2 * block + 2, 9)):
            a, b = tap // 3, tap % 3
            total = jnp.zeros((CH_ONE, CH_TWO), f32)
            for p in range(4):
                n = 3 * ((p // 2 + a + 1) // 2) + (p % 2 + b + 1) // 2
                total = total + d3[32 * p : 32 * (p + 1), 64 * n : 64 * (n + 1)]
            if tap % 2 == 0:
                packed = jnp.concatenate([total, packed[:, 64:128]], axis=1)
            else:
                packed = jnp.concatenate([packed[:, 0:64], total], axis=1)
        if block < 4:
            pay_a[32 * block : 32 * (block + 1), :] = packed
        else:
            pay_a[128:144, :] = jnp.concatenate([packed[0:16, 0:64], packed[16:32, 0:64]], axis=1)
    outer = jnp.zeros((CH_ONE, 128), f32)
    for c in range(crops):
        outer = outer + as_column(over_phases(sg_ref[c : c + 1, :]))[0:32] * jnp.concatenate([unit[c : c + 1]] * 2, axis=1)
        sums_ref[2:3, :] += sg_ref[c : c + 1, :]
    pay_a[144:160, :] = head_ref[...]
    pay_a[160:176, :] = jnp.concatenate([outer[0:16, 0:64], outer[16:32, 0:64]], axis=1)
    pay_a[176:184, :] = sums_ref[...]
    if pay_a.shape[0] > 184:
        pay_a[184:, :] = jnp.zeros((pay_a.shape[0] - 184, 128), f32)
    reduce_a.scatter()

    wait_all(sg_copies)
    style_grad = over_phases(in_order(sg_got, tiles))[:, 0:32]
    grad_unit = jnp.dot(style_grad, ws_ref[...], precision=highest, preferred_element_type=f32)
    mixed = jnp.mean(style_raw * grad_unit, axis=1, keepdims=True)
    grad_raw = style_inv * grad_unit - style_inv * style_inv * style_inv * style_raw * mixed
    grad_raw = jnp.concatenate([grad_raw / coarse_count] * 2, axis=1)
    raw = [as_column(grad_raw[c : c + 1])[0:64] for c in range(crops)]
    pay_c[...] = jnp.zeros_like(pay_c)
    d2_ref[...] = jnp.zeros_like(d2_ref)
    d1_ref[...] = jnp.zeros_like(d1_ref)
    finish_rims()
    g2_ref = g3_ref

    def masked(k, extra=None):
        coarse = rows_of(gc_ref, k * 64, 64)
        if extra is not None:
            coarse = coarse + extra
        grad = (coarse + jnp.concatenate([wide(v, width) for v in raw], axis=1)).astype(bf16).astype(f32)
        h2 = rows_of(x3_ref, (k + 1) * 192 + 64, 64).astype(f32)
        put_rows(g2_ref, k * 192, three_columns(jnp.where(h2 > 0, grad, 0.0).astype(bf16), crops))

    up = jnp.where(edge[0] < 0, rim_up[...].astype(f32), 0.0)
    dn = jnp.where(edge[1] > rows, rim_dn[...].astype(f32), 0.0)
    masked(0, up[0:64])
    masked(1, up[64:128])
    masked(rows, dn[0:64])
    masked(rows + 1, dn[64:128])

    def inner(ks):
        for k in ks:
            masked(k + 2)

    repeat_rows(rows - 2, 2, inner)
    reduce_a.across()
    pay_b[...] = jnp.zeros_like(pay_b)

    def weights_two(rs):
        d2, sums = 0.0, 0.0
        for r in rs:
            g2 = rows_of(g2_ref, (r + 1) * 192 + 64, 64)
            d2 = d2 + dot_nt(rows_of(x2_ref, (r + 2) * 96, 288), g2)
            sums = sums + dot_nt(ones, g2)
        d2_ref[...] += d2
        pay_b[160:168, 0:64] += sums

    repeat_rows(rows, 2, weights_two)
    rest = jnp.concatenate([d2_ref[160:288, :], jnp.zeros((32, 64), f32)], axis=0)
    pay_b[0:160, :] = jnp.concatenate([d2_ref[0:160, :], rest], axis=1)
    reduce_b.scatter()
    reduce_a.gather(full_a)

    def last_back(rs):
        gps = [dot(wd2_ref[...], rows_of(g2_ref, r * 192, 576)) for r in rs]
        gts = [dot(wht_ref[...], rows_of(go_out, r * 16, 16)) for r in rs]
        d1, sums = 0.0, 0.0
        for r, gp, gt in zip(rs, gps, gts):
            gp = 0.25 * gp.astype(bf16).astype(f32)
            g1 = (jnp.concatenate([gp] * 4, axis=0) + gt.astype(bf16).astype(f32)).astype(bf16).astype(f32)
            h1 = rows_of(h1_ref, (r + 3) * 128, 128).astype(f32)
            gb = jnp.where(h1 > 0, g1, 0.0).astype(bf16)
            sums = sums + dot_nt(ones, gb)
            d1 = d1 + dot_nt(rows_of(y_ref, (r + 3) * 16, 32), gb)
        d1_ref[...] += d1
        pay_c[8:16, :] += sums

    half = rows // 2
    repeat_rows(half, 2, last_back)
    reduce_b.across()
    repeat_rows(rows - half, 2, lambda rs: last_back([r + half for r in rs]))
    total = jnp.zeros((32, 128), f32)
    for p in range(4):
        total = total + turn(turn(d1_ref[...], -32 * p, 1), -(8 * (p // 2) + p % 2), 0)
    packed = lane_group(total[0:8], 0)
    for k in range(1, 4):
        packed = packed + turn(lane_group(total[8 * k : 8 * (k + 1)], 0), 32 * k, 1)
    pay_c[0:8, :] = packed
    copies = share(tiles, "tile", pay_c, got_c, sems[12], sems[13])
    reduce_b.gather(full_b)
    wait_all(copies)
    own_c[...] = in_order(got_c, tiles)
    copies = share(images, "img", own_c, met_c, sems[14], sems[15])
    reduce_a.finish()
    size_a, size_b = full_a.shape[0], full_b.shape[0]
    o_ref[0:size_a, :] = full_a[...]
    reduce_b.finish()
    o_ref[size_a : size_a + size_b, :] = full_b[...]
    wait_all(copies)
    o_ref[size_a + size_b :, :] = in_order(met_c, images)


def update_kernel(pixel_count, second_at, third_at, count_ref, sum_ref, *refs):
    olds, outs, loss_ref = refs[:18], refs[18:36], refs[36]
    rate = 1.0 / (jnp.zeros((8, 128), f32) + (count_ref[0].astype(f32) + 1.0))

    def step(index, spot, grad):
        weight, momentum, average = (olds[3 * index + k][spot] for k in range(3))
        decayed = grad + decay_rate * weight
        momentum = momentum_rate * momentum + decayed
        new = weight - learn_rate * (decayed + momentum_rate * momentum)
        outs[3 * index][spot] = new
        outs[3 * index + 1][spot] = momentum
        outs[3 * index + 2][spot] = average + (new - average) * rate[0:1, 0:1]

    first = sum_ref[third_at : third_at + 8, :]
    for a in range(3):
        for b in range(3):
            for i in range(2):
                grad = first[4 * i + b : 4 * i + b + 1, 32 * a : 32 * (a + 1)]
                step(0, (a, b, slice(i, i + 1), slice(None)), grad)
    for tap in range(9):
        a, b = tap // 3, tap % 3
        first = second_at + 32 * (tap % 5)
        half = 64 * (tap // 5)
        step(1, (a, b), sum_ref[first : first + 32, half : half + 64])
        if tap < 8:
            first = 32 * (tap // 2)
            lane = 64 * (tap % 2)
            grad = sum_ref[first : first + 32, lane : lane + 64]
        else:
            first = 128
            grad = jnp.concatenate([sum_ref[first : first + 16, 64 * k : 64 * (k + 1)] for k in range(2)], axis=0)
        step(2, (a, b), grad)
    first = 160
    grad = jnp.concatenate([sum_ref[first : first + 16, 64 * k : 64 * (k + 1)] for k in range(2)], axis=0)
    step(3, (slice(None), slice(None)), grad)
    head = sum_ref[144:160, :]
    total = jnp.zeros((16, 128), f32)
    for p in range(4):
        total = total + turn(turn(head, -32 * p, 1), -p, 0)
    total = jnp.concatenate([total[4 * o : 4 * o + 1] for o in range(OUT_CH)], axis=0)
    step(4, (slice(None), slice(None)), total[:, 0:32])
    sums = sum_ref[176:184, :]
    one = over_phases(jnp.sum(sum_ref[third_at + 8 : third_at + 16, :], axis=0, keepdims=True))
    two = jnp.sum(sum_ref[second_at + 160 : second_at + 168, :], axis=0, keepdims=True)
    three = over_phases(sums[2:3])
    lane = lax.broadcasted_iota(jnp.int32, (1, 128), 1)
    low = jnp.where(lane < 32, one, jnp.where(lane < 96, turn(two, 32, 1), three))
    ends = sums[3:4]
    ends = (ends + turn(ends, -1, 1)) + (turn(ends, -2, 1) + turn(ends, -3, 1))
    high = jnp.where(lane < 32, three, 0.0)
    for o in range(OUT_CH):
        high = jnp.where(lane == 32 + o, turn(ends, 32 + o - 4 * o, 1), high)
    grad = jnp.concatenate([low, high], axis=1)[:, 0 : olds[15].shape[0]]
    weight, momentum, average = (olds[15 + k][...].reshape(1, -1) for k in range(3))
    decayed = grad + decay_rate * weight
    momentum = momentum_rate * momentum + decayed
    new = weight - learn_rate * (decayed + momentum_rate * momentum)
    average = average + (new - average) * rate[0:1, 0:1]
    for k, value in enumerate((new, momentum, average)):
        outs[15 + k][...] = value.reshape(-1)
    loss_ref[0] = jnp.sum(sums[4:5]) / pixel_count


def on_device(
    images, nucleus, target_flow, cell_label, step_count,
    conv1_weight, conv1_momentum, conv1_average,
    conv2_weight, conv2_momentum, conv2_average,
    conv3_weight, conv3_momentum, conv3_average,
    style_weight, style_momentum, style_average,
    head_weight, head_momentum, head_average,
    biases, bias_momentum, bias_average,
):
    tiles = lax.axis_size("tile")
    crops, _, height, cols = images.shape
    rows, width = height // 2, cols // 2
    pixel_count = lax.axis_size("img") * tiles * crops * height * cols
    grad_scale = 1.0 / math.sqrt(pixel_count)
    coarse_count = tiles * rows * width

    def sds(shape, dtype=f32):
        return jax.ShapeDtypeStruct(shape, dtype)

    lanes = crops * width
    images_count = lax.axis_size("img")

    def other_way(w):
        return jnp.swapaxes(w, -1, -2)

    third = tuple(other_way(w) for w in (conv3_weight, conv3_momentum, conv3_average))
    style = tuple(other_way(w) for w in (style_weight, style_momentum, style_average))
    head = tuple(other_way(w) for w in (head_weight, head_momentum, head_average))

    edge = (crops, 2, HALO, cols)
    rim = (128, lanes)
    parts = [8 * pl.cdiv(sum(block), 8 * tiles) for block in BLOCK_ROWS[:2]]
    small = sum(BLOCK_ROWS[2])

    def buf(shape, dtype=bf16):
        return pltpu.VMEM(shape, dtype)

    def block_bufs(part):
        return [
            buf((part * tiles, 128), f32), buf((tiles, part, 128), f32), buf((part, 128), f32),
            buf((images_count, part, 128), f32), buf((part * tiles, 128), f32),
        ]

    block_sems = [DMA((tiles,)), DMA((tiles,)), DMA((images_count,)), DMA((images_count,)), DMA((tiles,)), DMA((tiles,))]
    summed = pl.pallas_call(
        lambda *refs: step_kernel(tiles, images_count, grad_scale, float(coarse_count), *refs),
        out_shape=sds((sum(parts) * tiles + small, 128)),
        in_specs=[SMEM] + [VMEM] * 9,
        out_specs=VMEM,
        scratch_shapes=[
            buf(edge), buf(edge), buf(edge, jnp.int32), buf(edge, jnp.int32),
            buf((128, 32)), buf((CH_TWO, 9 * CH_ONE)), buf((256, 9 * CH_TWO)), buf((128, 16 * CH_ONE)),
            buf((CH_ONE, 9 * CH_TWO)), buf((16, 128)), buf((128, 16)),
            buf((128, 128), f32), buf((64, 128), f32), buf((8, 128), f32), buf((16, 128), f32), buf((32, 128), f32),
            buf((16 * (rows + 7), lanes)), buf((lanes // 128, 16 * (rows + 2), 128), f32),
            buf((128 * (rows + 6), lanes)), buf((96 * (rows + 6), lanes)), buf((192 * (rows + 4), lanes)),
            buf((128 * (rows + 2), lanes)), buf((128 * (rows + 2), lanes)),
            buf((lanes // 128, 16 * (rows + 2), 128), f32), buf((lanes // 128, 16 * rows, 128), f32),
            buf((16 * rows, lanes)), buf((256 * (rows + 4), lanes)), buf((64 * (rows + 2), lanes), f32),
            buf(rim), buf(rim), buf(rim), buf(rim),
            buf((8, 128), f32), buf((tiles, 8, 128), f32), buf((8, 128), f32), buf((tiles, 8, 128), f32),
            buf((16, 128), f32), buf((8, 128), f32),
            buf((9 * CH_TWO, 128), f32), buf((9 * CH_ONE, CH_TWO), f32), buf((32, 128), f32),
        ]
        + block_bufs(parts[0])
        + block_bufs(parts[1])
        + [buf((small, 128), f32), buf((tiles, small, 128), f32), buf((small, 128), f32), buf((images_count, small, 128), f32)]
        + [DMA((4,)), DMA((4,)), DMA((tiles,)), DMA((tiles,)), DMA((tiles,)), DMA((tiles,)), DMA((2,)), DMA((2,))]
        + block_sems * 2
        + [DMA((tiles,)), DMA((tiles,)), DMA((images_count,)), DMA((images_count,))],
        compiler_params=pltpu.CompilerParams(collective_id=1, has_side_effects=True, vmem_limit_bytes=62 * 2**20),
        name="step",
    )(
        nucleus, images, target_flow, cell_label,
        conv1_weight, conv2_weight, third[0], head[0], biases, style[0],
    )

    olds = (
        (conv1_weight, conv1_momentum, conv1_average)
        + (conv2_weight, conv2_momentum, conv2_average)
        + third + style + head
        + (biases, bias_momentum, bias_average)
    )
    news = pl.pallas_call(
        lambda *refs: update_kernel(float(pixel_count), parts[0] * tiles, sum(parts) * tiles, *refs),
        out_shape=tuple(sds(v.shape) for v in olds) + (sds((1,)),),
        in_specs=[SMEM] + [VMEM] * 19,
        out_specs=[VMEM] * 18 + [SMEM],
        compiler_params=pltpu.CompilerParams(vmem_limit_bytes=16 * 2**20),
        name="update",
    )(step_count, summed, *olds)
    return (news[18], *news[0:6], *(other_way(w) for w in news[6:15]), *news[15:18])


def solution(mesh):
    return jax.shard_map(
        on_device,
        mesh=mesh,
        in_specs=(
            P("img", None, "tile", None),
            P("img"),
            P("img", None, "tile", None),
            P("img", "tile", None),
        )
        + (P(),) * 19,
        out_specs=(P(),) * 19,
        check_vma=False,
    )
```

time: 103 us -> 85.2 us (0.83)
  Pallas kernels: 92.9 us -> 82.4 us
  local copies, waits for them, and re-layouts: 8.29 us -> 1 us
    pallas_call x6 -> x2, Pallas kernels: 92.9 us -> 82.4 us  [the longest x1 81.1 us: on_device(): pl.pallas_call(lambda *refs: step_kernel(tiles, images_count, grad_scale,...]
    unnamed x54 -> x38, local copies, waits for them, and re-layouts: 8.29 us -> 1 us
where the time goes in v5:
time: 85.2 us; the launch traced here: 85 us
  Pallas kernels  82.4 us (97%)
  between operations  1.61 us (2%)
  local copies, waits for them, and re-layouts  1 us (1%)
    pallas_call x1, Pallas kernels, on_device(): pl.pallas_call(lambda *refs: step_kernel(tiles, images_count, grad_scale,...  81.1 us

profile of v5, /device:TPU:0, one launch (start us, length us, event | category | flops | bytes accessed | tf_op | source)
XLA Modules:
  0.0 85.0 jit_solution(16568613058922627602)
XLA Ops:
  1.3 0.0 copy-start.1
  1.3 0.0 copy-start.2
  1.5 81.1 %step.1.refs_1_ = f32[400,128]{1,0:T(8,128)} custom-call(s32[2]{0:T(128)} %refs_0_.2, bf16[2,2,32,1024]{3,2,1,0:T(8,128)(2,1)} %refs_1_.1, s32[2,2,32,1024]{3,2,1,0:T(8,128)} %refs_2_.2, s32[2,32,1024]{2,1,0:T(8,128)} %refs_3_.2, f32[3,3,2,32]{3,2,1,0:T(2,128)} %refs_2_.3, f32[3,3,32,64]{3,2,1,0:T(8,128)} %refs_5_.3, f32[3,3,32,64]{3,2,1,0:T(8,128)} %bitcast.18, ...), custom_call_target="tpu_custom_call" | custom-call | tf_op jit(solution)/shard_map/step/pallas_call | solution.py:797
  82.6 0.0 copy-done.1
  82.6 0.0 copy-done.2
  82.6 0.0 copy-done.3
  82.6 0.0 copy-done.4
  82.6 0.0 copy-done.5
  82.7 0.0 copy-done.6
  82.7 0.0 copy-done.7
  82.7 0.0 copy-done.8
  82.7 0.0 copy-done.9
  82.7 0.0 copy-done.10
  82.7 0.0 copy-done.11
  82.7 0.0 copy-done.12
  82.7 0.0 copy-done.13
  82.7 0.0 copy-done.14
  82.7 0.0 copy-done.15
  82.8 0.0 copy-done.16
  82.8 0.0 copy-done.17
  82.8 0.0 copy-done.18
  82.8 0.0 copy-start
  82.8 0.9 %copy-done = f32[400,128]{1,0:T(8,128)S(1)} copy-done((f32[400,128]{1,0:T(8,128)S(1)}, f32[400,128]{1,0:T(8,128)}, u32[]{:S(2)}) %copy-start) | copy-done | bytes 204824
  83.7 1.3 %update.1 = (f32[3,3,2,32]{3,2,1,0:T(2,128)}, f32[3,3,2,32]{3,2,1,0:T(2,128)}, f32[3,3,2,32]{3,2,1,0:T(2,128)}, f32[3,3,32,64]{3,2,1,0:T(8,128)}, f32[3,3,32,64]...) custom-call(s32[1]{0:T(128)S(6)} %copy.42.refs_0_, ...), custom_call_target="tpu_custom_call" | custom-call | tf_op jit(solution)/shard_map/update/pallas_call | solution.py:836
  (16 shorter events, 0.0 us)
Async XLA Ops:
  1.3 81.3 %copy-start.1 = (f32[3,3,32,64]{3,2,1,0:T(8,128)S(1)}, f32[3,3,32,64]{3,2,1,0:T(8,128)}, u32[]{:S(2)}) copy-start(f32[3,3,32,64]{3,2,1,0:T(8,128)} %refs_5_.3) | copy-start | bytes 221188
  1.3 81.3 %copy-start.2 = (f32[3,3,64,32]{2,3,1,0:T(8,128)S(1)}, f32[3,3,64,32]{2,3,1,0:T(8,128)}, u32[]{:S(2)}) copy-start(f32[3,3,64,32]{2,3,1,0:T(8,128)} %param.34) | copy-start | bytes 221188
  1.3 81.3 %copy-start.3 = (f32[3,3,32,64]{3,2,1,0:T(8,128)S(1)}, f32[3,3,32,64]{3,2,1,0:T(8,128)}, u32[]{:S(2)}) copy-start(f32[3,3,32,64]{3,2,1,0:T(8,128)} %refs_6_.1) | copy-start | bytes 221188
  1.3 81.3 %copy-start.4 = (f32[3,3,32,64]{3,2,1,0:T(8,128)S(1)}, f32[3,3,32,64]{3,2,1,0:T(8,128)}, u32[]{:S(2)}) copy-start(f32[3,3,32,64]{3,2,1,0:T(8,128)} %refs_7_.1) | copy-start | bytes 221188
  1.4 81.3 %copy-start.5 = (f32[3,3,64,32]{2,3,1,0:T(8,128)S(1)}, f32[3,3,64,32]{2,3,1,0:T(8,128)}, u32[]{:S(2)}) copy-start(f32[3,3,64,32]{2,3,1,0:T(8,128)} %param.35) | copy-start | bytes 221188
  1.4 81.3 %copy-start.6 = (f32[3,3,64,32]{2,3,1,0:T(8,128)S(1)}, f32[3,3,64,32]{2,3,1,0:T(8,128)}, u32[]{:S(2)}) copy-start(f32[3,3,64,32]{2,3,1,0:T(8,128)} %param.36) | copy-start | bytes 221188
  1.4 81.3 %copy-start.7 = (f32[64,32]{0,1:T(8,128)S(1)}, f32[64,32]{0,1:T(8,128)}, u32[]{:S(2)}) copy-start(f32[64,32]{0,1:T(8,128)} %param.37) | copy-start | bytes 24580
  1.4 81.3 %copy-start.8 = (f32[3,3,2,32]{3,2,1,0:T(2,128)S(1)}, f32[3,3,2,32]{3,2,1,0:T(2,128)}, u32[]{:S(2)}) copy-start(f32[3,3,2,32]{3,2,1,0:T(2,128)} %refs_2_.3) | copy-start | bytes 6916
  1.4 81.3 %copy-start.9 = (f32[64,32]{0,1:T(8,128)S(1)}, f32[64,32]{0,1:T(8,128)}, u32[]{:S(2)}) copy-start(f32[64,32]{0,1:T(8,128)} %param.38) | copy-start | bytes 24580
  1.4 81.3 %copy-start.10 = (f32[64,32]{0,1:T(8,128)S(1)}, f32[64,32]{0,1:T(8,128)}, u32[]{:S(2)}) copy-start(f32[64,32]{0,1:T(8,128)} %param.39) | copy-start | bytes 24580
  1.4 81.3 %copy-start.11 = (f32[3,3,2,32]{3,2,1,0:T(2,128)S(1)}, f32[3,3,2,32]{3,2,1,0:T(2,128)}, u32[]{:S(2)}) copy-start(f32[3,3,2,32]{3,2,1,0:T(2,128)} %refs_3_.3) | copy-start | bytes 6916
  1.4 81.3 %copy-start.12 = (f32[3,3,2,32]{3,2,1,0:T(2,128)S(1)}, f32[3,3,2,32]{3,2,1,0:T(2,128)}, u32[]{:S(2)}) copy-start(f32[3,3,2,32]{3,2,1,0:T(2,128)} %refs_4_.3) | copy-start | bytes 6916
  1.4 81.3 %copy-start.13 = (f32[32,3]{0,1:T(4,128)S(1)}, f32[32,3]{0,1:T(4,128)}, u32[]{:S(2)}) copy-start(f32[32,3]{0,1:T(4,128)} %param.40) | copy-start | bytes 1156
  1.4 81.3 %copy-start.14 = (f32[163]{0:T(256)S(1)}, f32[163]{0:T(256)}, u32[]{:S(2)}) copy-start(f32[163]{0:T(256)} %refs_17_.1) | copy-start | bytes 1960
  1.5 81.3 %copy-start.15 = (f32[32,3]{0,1:T(4,128)S(1)}, f32[32,3]{0,1:T(4,128)}, u32[]{:S(2)}) copy-start(f32[32,3]{0,1:T(4,128)} %param.41) | copy-start | bytes 1156
  1.5 81.3 %copy-start.16 = (f32[32,3]{0,1:T(4,128)S(1)}, f32[32,3]{0,1:T(4,128)}, u32[]{:S(2)}) copy-start(f32[32,3]{0,1:T(4,128)} %param.42) | copy-start | bytes 1156
  1.5 81.3 %copy-start.17 = (f32[163]{0:T(256)S(1)}, f32[163]{0:T(256)}, u32[]{:S(2)}) copy-start(f32[163]{0:T(256)} %refs_18_.1) | copy-start | bytes 1960
  1.5 81.3 %copy-start.18 = (f32[163]{0:T(256)S(1)}, f32[163]{0:T(256)}, u32[]{:S(2)}) copy-start(f32[163]{0:T(256)} %refs_19_.1) | copy-start | bytes 1960
  82.8 0.9 %copy-start = (f32[400,128]{1,0:T(8,128)S(1)}, f32[400,128]{1,0:T(8,128)}, u32[]{:S(2)}) copy-start(f32[400,128]{1,0:T(8,128)} %step.1.refs_1_) | copy-start | bytes 614404

commit v6 on v5

--- a/solution.py
+++ b/solution.py
@@ -22,7 +22,7 @@
 HALO = 8
 VMEM = pl.BlockSpec(memory_space=pltpu.VMEM)
 SMEM = pl.BlockSpec(memory_space=pltpu.SMEM)
-ANY = pl.BlockSpec(memory_space=pl.ANY)
+HBM = pl.BlockSpec(memory_space=pltpu.HBM)
 MESH = pl.DeviceIdType.MESH
 DMA = pltpu.SemaphoreType.DMA
 
@@ -37,31 +37,43 @@
     return lax.dot_general(a, b, (((1,), (1,)), ((), ())), preferred_element_type=f32, precision=precision)
 
 
-def from_left(x, crops=1):
-    lane = lax.broadcasted_iota(jnp.int32, x.shape, 1)
-    return jnp.where(lane % (x.shape[1] // crops) == 0, 0.0, pltpu.roll(x, 1, 1))
-
-
-def from_right(x, crops=1):
+def edge_select(x, crops, first):
     width = x.shape[1] // crops
-    lane = lax.broadcasted_iota(jnp.int32, x.shape, 1)
-    return jnp.where(lane % width == width - 1, 0.0, pltpu.roll(x, x.shape[1] - 1, 1))
-
-
-def three_columns(mid, crops):
-    x = mid.astype(f32)
+    lane = lax.broadcasted_iota(jnp.int32, (x.shape[0], 128), 1)
+    parts = []
+    for c in range(crops):
+        low, high = width * c, width * (c + 1)
+        if first:
+            parts += [jnp.where(lane == 0, 0.0, x[:, low : low + 128]), x[:, low + 128 : high]]
+        else:
+            parts += [x[:, low : high - 128], jnp.where(lane == 127, 0.0, x[:, high - 128 : high])]
+    return jnp.concatenate(parts, axis=1)
+
+
+def from_left(x, crops):
+    return edge_select(pltpu.roll(x, 1, 1), crops, True)
+
+
+def from_right(x, crops):
+    return edge_select(pltpu.roll(x, x.shape[1] - 1, 1), crops, False)
+
+
+def three_columns(mid, x, crops):
     return jnp.concatenate([from_left(x, crops).astype(bf16), mid, from_right(x, crops).astype(bf16)], axis=0)
 
 
-def crop_rows(crops, lanes):
-    row = lax.broadcasted_iota(jnp.int32, (8, lanes), 0)
-    lane = lax.broadcasted_iota(jnp.int32, (8, lanes), 1)
-    return jnp.where(lane // (lanes // crops) == row, 1.0, 0.0).astype(bf16)
-
-
-def repeat_rows(count, step, body):
+def pieces_of(x):
+    high = x.astype(bf16)
+    rest = x - high.astype(f32)
+    mid = rest.astype(bf16)
+    return high.astype(f32), mid.astype(f32), rest - mid.astype(f32)
+
+
+def repeat_rows(count, limit, body, first=0):
+    step = max(k for k in range(1, limit + 1) if count % k == 0)
+
     def run(k, carry):
-        body([k * step + j for j in range(step)])
+        body([first + k * step + j for j in range(step)])
         return carry
 
     lax.fori_loop(0, count // step, run, 0)
@@ -86,10 +98,14 @@
 
 
 def fold_lanes(x):
-    total = x[:, 0:128]
-    for k in range(1, x.shape[1] // 128):
-        total = total + x[:, 128 * k : 128 * (k + 1)]
-    return total
+    parts = [x[:, 128 * k : 128 * (k + 1)] for k in range(x.shape[1] // 128)]
+    while len(parts) > 1:
+        parts = [a + b for a, b in zip(parts[0::2], parts[1::2])] + parts[len(parts) // 2 * 2 :]
+    return parts[0]
+
+
+def lane_sums(x):
+    return dot_nt(jnp.ones((8, 128), f32), x, highest)
 
 
 def wide(tile, width):
@@ -235,7 +251,7 @@
         wait_all(self.copies)
 
 
-def first_tables(k1_ref, k2_ref, bias_ref, w1_ref, w2_ref, b1_ref, b2_ref, base_ref):
+def first_tables(k1_ref, k2_ref, bias_ref, w1_ref, w2_ref, base_ref):
     base_ref[...] = jnp.zeros_like(base_ref)
     for a in range(3):
         for b in range(3):
@@ -245,14 +261,22 @@
     w1t = jnp.zeros((32, 128), f32)
     for p in range(4):
         w1t = w1t + turn(turn(base, 8 * (p // 2) + p % 2, 0), 32 * p, 1)
-    w1_ref[...] = jnp.transpose(w1t).astype(bf16)
+    bias = bias_ref[...].reshape(1, -1)
+    row = lax.broadcasted_iota(jnp.int32, (16, 128), 0)
+
+    def piece_rows(values):
+        table = jnp.zeros((16, 128), f32)
+        for k, piece in enumerate(pieces_of(values)):
+            table = jnp.where(row == k, jnp.broadcast_to(piece, (16, 128)), table)
+        return table
+
+    b1 = piece_rows(jnp.concatenate([bias[:, 0:32]] * 4, axis=1))
+    w1_ref[...] = jnp.transpose(jnp.concatenate([w1t, b1], axis=0)).astype(bf16)
 
     k2 = [[k2_ref[a, b].astype(bf16).astype(f32) for b in range(3)] for a in range(3)]
     w2t = jnp.concatenate([k2[a][b] for a in range(3) for b in range(3)], axis=0)
-    w2_ref[...] = jnp.transpose(w2t).astype(bf16)
-    bias = bias_ref[...].reshape(1, -1)
-    b1_ref[...] = as_column(jnp.concatenate([bias[:, 0:32]] * 4, axis=1))
-    b2_ref[...] = as_column(jnp.concatenate([bias[:, 32:96]] * 2, axis=1))[0:64]
+    b2 = piece_rows(jnp.concatenate([bias[:, 32:96]] * 2, axis=1))[:, 0:64]
+    w2_ref[...] = jnp.transpose(jnp.concatenate([w2t, b2], axis=0)).astype(bf16)
 
 
 def later_tables(k2_ref, k3_ref, kh_ref, bias_ref, w3_ref, wd3_ref, wd2_ref, wh_ref, wht_ref, b3_ref, bh_ref):
@@ -271,8 +295,9 @@
     for p in range(4):
         w3 = jnp.concatenate([tap_sum(up[p // 2][r], up[p % 2][c]) for r in range(3) for c in range(3)], axis=1)
         w3_hi = w3.astype(bf16)
-        w3_ref[32 * p : 32 * (p + 1), :] = w3_hi
-        w3_ref[128 + 32 * p : 160 + 32 * p, :] = (w3 - w3_hi.astype(f32)).astype(bf16)
+        low = w3 - w3_hi.astype(f32)
+        low = jnp.concatenate([low[:, 64:128], low[:, 192:384], low[:, 448:512]], axis=1)
+        w3_ref[32 * p : 32 * (p + 1), 0:896] = jnp.concatenate([w3_hi, low.astype(bf16)], axis=1)
     down = ((2,), (1, 2), (0, 1), (0,))
     wd3 = jnp.transpose(jnp.concatenate([tap_sum(down[r], down[c]) for r in range(4) for c in range(4)], axis=0))
     wd3_hi = wd3.astype(bf16)
@@ -309,32 +334,48 @@
 
 def step_kernel(
     tiles, images, scale, coarse_count,
-    nucleus_ref, x_ref, t_ref, label_ref, k1_ref, k2_ref, k3_ref, kh_ref, bias_ref, ws_ref,
+    nucleus_ref, x_hbm, t_hbm, label_hbm, k1_hbm, k2_hbm, k3_hbm, kh_hbm, bias_hbm, ws_hbm,
     o_ref,
+    x_ref, t_ref, label_ref, k1_ref, k2_ref, k3_ref, kh_ref, bias_ref, ws_ref,
     x_lo, x_hi, t_lo, t_hi,
-    w1_ref, w2_ref, w3_ref, wd3_ref, wd2_ref, wh_ref, wht_ref, b1_ref, b2_ref, b3_ref, bh_ref, base_ref,
+    w1_ref, w2_ref, w3_ref, wd3_ref, wd2_ref, wh_ref, wht_ref, b3_ref, bh_ref, base_ref, ones_ref, mark_ref,
     y_ref, t_out, h1_ref, x2_ref, x3_ref, h3_ref, m_ref, fe_ref, go_ref, go_out, g3_ref, gc_ref,
     rim_lo, rim_hi, rim_up, rim_dn,
     style_ref, style_got, sg_ref, sg_got, head_ref, sums_ref, d3_ref, d2_ref, d1_ref,
+    style_sum, sg_sum, go_sum, g2_sum,
     pay_a, got_a, own_a, met_a, full_a, pay_b, got_b, own_b, met_b, full_b,
     pay_c, got_c, own_c, met_c,
-    halo_send, halo_recv, s1_send, s1_recv, s2_send, s2_recv, rim_send, rim_recv,
+    load_sems, halo_send, halo_recv, s1_send, s1_recv, s2_send, s2_recv, rim_send, rim_recv,
     *sems,
 ):
     reduce_a = Reduction(tiles, images, pay_a, got_a, own_a, met_a, sems[0:6])
     reduce_b = Reduction(tiles, images, pay_b, got_b, own_b, met_b, sems[6:12])
     arrived = greet((("tile", tiles), ("img", images)))
-    first_tables(k1_ref, k2_ref, bias_ref, w1_ref, w2_ref, b1_ref, b2_ref, base_ref)
+    loads = [
+        pltpu.make_async_copy(source, target, load_sems.at[k])
+        for k, (source, target) in enumerate(
+            (
+                (k1_hbm, k1_ref), (k2_hbm, k2_ref), (bias_hbm, bias_ref), (x_hbm, x_ref),
+                (t_hbm, t_ref), (label_hbm, label_ref), (k3_hbm, k3_ref), (kh_hbm, kh_ref), (ws_hbm, ws_ref),
+            )
+        )
+    ]
+    for load in loads:
+        load.start()
+    ones_ref[...] = jnp.ones_like(ones_ref)
     arrived()
     last = x_ref.shape[2] - HALO
     finish_halo = swap_edges(
         tiles,
         [
             (ref.at[:, :, pl.ds(0, HALO), :], ref.at[:, :, pl.ds(last, HALO), :], lo, hi)
-            for ref, lo, hi in ((x_ref, x_lo, x_hi), (t_ref, t_lo, t_hi))
+            for ref, lo, hi in ((x_hbm, x_lo, x_hi), (t_hbm, t_lo, t_hi))
         ],
         halo_send, halo_recv,
     )
+    for load in loads[0:4]:
+        load.wait()
+    first_tables(k1_ref, k2_ref, bias_ref, w1_ref, w2_ref, base_ref)
     crops = x_ref.shape[0]
     width = x_ref.shape[3] // 2
     lanes = crops * width
@@ -344,20 +385,19 @@
     r_id = lax.broadcasted_iota(jnp.int32, (256, 256), 0)
     c_id = lax.broadcasted_iota(jnp.int32, (256, 256), 1)
     select = jnp.where(r_id == 2 * (c_id % 128) + c_id // 128, 1.0, 0.0).astype(bf16)
-    x_rows = 2 * (height + 2 * HALO)
     y_rows = y_ref.shape[0]
-    ri = lax.broadcasted_iota(jnp.int32, (y_rows, 4 * x_rows), 0)
-    ci = lax.broadcasted_iota(jnp.int32, (y_rows, 4 * x_rows), 1)
+    ri = lax.broadcasted_iota(jnp.int32, (y_rows, 8 * height), 0)
+    ci = lax.broadcasted_iota(jnp.int32, (y_rows, 8 * height), 1)
     fine = 2 * (ri // 16) + (ri // 8) % 2 - 7
-    channel = (ri // 4) % 2
-    source = jnp.where(
-        fine < 0,
-        2 * height + channel * HALO + fine + HALO,
-        jnp.where(
-            fine < height, channel * height + fine, 2 * height + 2 * HALO + channel * HALO + fine - height
-        ),
-    )
-    perm_x = jnp.where(ci == (ri % 4) * x_rows + source, 1.0, 0.0).astype(bf16)
+    source = (ri % 4) * 2 * height + (ri // 4) % 2 * height + fine
+    perm_x = jnp.where((ci == source) & (fine >= 0) & (fine < height), 1.0, 0.0).astype(bf16)
+    ri = lax.broadcasted_iota(jnp.int32, (128, 16 * HALO), 0)
+    ci = lax.broadcasted_iota(jnp.int32, (128, 16 * HALO), 1)
+    fine = 2 * (ri // 16) + (ri // 8) % 2 - 7
+    fine = jnp.where(ri < 64, fine, fine + y_rows // 8 - 16)
+    source = jnp.where(fine < 0, fine + HALO, 2 * HALO + fine - height)
+    source = (ri % 4) * 4 * HALO + (ri // 4) % 2 * HALO + source
+    perm_h = jnp.where((ci == source) & ((fine < 0) | (fine >= height)), 1.0, 0.0).astype(bf16)
     has_up, has_dn = edge[0] < 0, edge[1] > rows
 
     def both_columns(of_crop):
@@ -382,47 +422,64 @@
         pieces += [jnp.where(has_dn, t_hi[c, k], 0).astype(f32) for k in range(2)]
         return jnp.concatenate(pieces, axis=0).astype(bf16)
 
-    own_part = both_columns(own_rows)
-    finish_halo()
-    even, odd = (jnp.concatenate([a, b], axis=0) for a, b in zip(own_part, both_columns(halo_rows)))
-    row = lax.broadcasted_iota(jnp.int32, (x_rows, lanes), 0)
-    crop = lax.broadcasted_iota(jnp.int32, (x_rows, lanes), 1) // width
-    second = jnp.where(row < 2 * height, row // height, (row - 2 * height) // HALO % 2) == 1
-    gate = jnp.ones((x_rows, lanes), f32)
-    for c in range(crops):
-        gate = jnp.where(second & (crop == c), nucleus_ref[c].astype(f32), gate)
-    even, odd = even * gate, odd * gate
-    stack = jnp.concatenate([from_left(odd, crops), even, odd, from_right(even, crops)], axis=0)
-    y_ref[...] = dot(perm_x, stack.astype(bf16)).astype(bf16)
-    ones = crop_rows(crops, lanes)
-    style_ref[...] = jnp.zeros_like(style_ref)
-
-    def conv_one(ks):
-        pre = [dot(w1_ref[...], rows_of(y_ref, k * 16, 32)) for k in ks]
+    def pixel_windows(of_crop, second):
+        even, odd = both_columns(of_crop)
+        row = lax.broadcasted_iota(jnp.int32, even.shape, 0)
+        crop = lax.broadcasted_iota(jnp.int32, even.shape, 1) // width
+        gate = jnp.ones(even.shape, f32)
+        for c in range(crops):
+            gate = jnp.where(second(row) & (crop == c), nucleus_ref[c].astype(f32), gate)
+        even, odd = even * gate, odd * gate
+        return jnp.concatenate([from_left(odd, crops), even, odd, from_right(even, crops)], axis=0).astype(bf16)
+
+    y_ref[...] = dot(perm_x, pixel_windows(own_rows, lambda row: row >= height)).astype(bf16)
+
+    def conv_one(ks, inside=True):
+        pre = [
+            dot(w1_ref[...], jnp.concatenate([rows_of(y_ref, k * 16, 32), ones_ref[...]], axis=0)) for k in ks
+        ]
         for k, p in zip(ks, pre):
-            keep = valid(k - 3, edge)
-            hidden = (jnp.maximum(p + wide(b1_ref[...], lanes), 0.0) * keep).astype(bf16)
+            p = jnp.maximum(p, 0.0)
+            hidden = (p if inside else p * valid(k - 3, edge)).astype(bf16)
             put_rows(h1_ref, k * 128, hidden)
             h = hidden.astype(f32)
             pooled = (0.25 * ((h[0:32] + h[32:64]) + (h[64:96] + h[96:128]))).astype(bf16)
-            put_rows(x2_ref, k * 96, three_columns(pooled, crops))
-
-    def conv_two(qs):
-        pre = [dot(w2_ref[...], rows_of(x2_ref, q * 96, 288)) for q in qs]
-        sums = 0.0
+            put_rows(x2_ref, k * 96, three_columns(pooled, pooled.astype(f32), crops))
+
+    def conv_two(qs, inside=True):
+        pre = [
+            dot(w2_ref[...], jnp.concatenate([rows_of(x2_ref, q * 96, 288), ones_ref[...]], axis=0)) for q in qs
+        ]
+        sums = [0.0] * crops
         for q, p in zip(qs, pre):
-            row = q - 2
-            keep = valid(row, edge)
-            own = jnp.where((row >= 0) & (row < rows), 1.0, 0.0).astype(f32)
-            hidden = (jnp.maximum(p + wide(b2_ref[...], lanes), 0.0) * keep).astype(bf16)
-            put_rows(x3_ref, q * 192, three_columns(hidden, crops))
-            sums = sums + dot_nt(ones, hidden) * own
-        style_ref[:, 0:64] += sums
-
-    repeat_rows(rows + 6, 2, conv_one)
-    repeat_rows(rows + 4, 2, conv_two)
+            p = jnp.maximum(p, 0.0)
+            hidden = (p if inside else p * valid(q - 2, edge)).astype(bf16)
+            h = hidden.astype(f32)
+            put_rows(x3_ref, q * 192, three_columns(hidden, h, crops))
+            for c in range(crops):
+                sums[c] = sums[c] + fold_lanes(h[:, width * c : width * (c + 1)])
+        if inside:
+            for c in range(crops):
+                style_sum[c] += sums[c]
+
+    repeat_rows(rows - 2, 7, conv_one, 4)
+    finish_halo()
+    extra = dot(perm_h, pixel_windows(halo_rows, lambda row: row // HALO % 2 == 1))
+    y_ref[0:64, :] = (y_ref[0:64, :].astype(f32) + extra[0:64]).astype(bf16)
+    y_ref[y_rows - 64 : y_rows, :] = (y_ref[y_rows - 64 : y_rows, :].astype(f32) + extra[64:128]).astype(bf16)
+    conv_one([0, 1, 2, 3], False)
+    conv_one([rows + 2, rows + 3, rows + 4, rows + 5], False)
+    style_sum[...] = jnp.zeros_like(style_sum)
+    repeat_rows(rows, 8, conv_two, 2)
+    style_ref[...] = jnp.zeros_like(style_ref)
+    for c in range(crops):
+        style_ref[c : c + 1, 0:64] = lane_sums(style_sum[c])[0:1]
     style_copies = share(tiles, "tile", style_ref, style_got, s1_send, s1_recv)
 
+    conv_two([0, 1], False)
+    conv_two([rows + 2, rows + 3], False)
+    for load in loads[4:]:
+        load.wait()
     t_rows = 3 * height + 4 * HALO
     ri = lax.broadcasted_iota(jnp.int32, (t_out.shape[1], 2 * t_rows), 0)
     ci = lax.broadcasted_iota(jnp.int32, (t_out.shape[1], 2 * t_rows), 1)
@@ -445,17 +502,28 @@
     unit = style_raw * style_inv
     vec = dot_nt(unit, ws_ref[...], highest)
     vec = jnp.concatenate([vec] * 4, axis=1) + b3_ref[0:1, :]
-    bias3 = [as_column(vec[c : c + 1]) for c in range(crops)]
+    row = lax.broadcasted_iota(jnp.int32, (16, lanes), 0)
+    lane = lax.broadcasted_iota(jnp.int32, (16, lanes), 1)
+    mark_ref[...] = jnp.where(row // 3 == lane // width, 1.0, 0.0).astype(bf16)
+    row = lax.broadcasted_iota(jnp.int32, (128, 128), 0)
+    table = jnp.zeros((128, 128), f32)
+    for c in range(crops):
+        for k, piece in enumerate(pieces_of(vec[c : c + 1])):
+            table = jnp.where(row == 3 * c + k, jnp.broadcast_to(piece, (128, 128)), table)
+    w3_ref[:, 896:912] = jnp.transpose(table)[:, 0:16].astype(bf16)
 
     def forward(ks):
-        pre = [dot(w3_ref[...], rows_of(x3_ref, k * 192, 576)) for k in ks]
+        pre = []
+        for k in ks:
+            x = rows_of(x3_ref, k * 192, 576)
+            x = jnp.concatenate([x, x[64:128], x[192:384], x[448:512], mark_ref[...]], axis=0)
+            pre.append(dot(w3_ref[...], x))
         hs = []
-        for k, both in zip(ks, pre):
-            p = both[0:128] + both[128:256] + jnp.concatenate([wide(b, width) for b in bias3], axis=1)
-            h1 = rows_of(h1_ref, (k + 2) * 128, 128).astype(f32)
-            h3 = (jnp.maximum(p, 0.0) + h1).astype(bf16)
+        for k, p in zip(ks, pre):
+            p = jnp.maximum(p, 0.0)
+            h3 = (p + rows_of(h1_ref, (k + 2) * 128, 128).astype(f32)).astype(bf16)
             put_rows(h3_ref, k * 128, h3)
-            put_rows(m_ref, k * 128, jnp.where(p > 0, 1.0, 0.0).astype(bf16))
+            put_rows(m_ref, k * 128, p.astype(bf16))
             hs.append(h3)
         outs = [dot(wh_ref[...], h) for h in hs]
         for k, o in zip(ks, outs):
@@ -464,7 +532,7 @@
             fe = (o[0:8] - 0.25 * t[0:8]) * valid(k - 1, edge)
             put_lanes(fe_ref, k * 16, jnp.concatenate([fe, o[8:16]], axis=0))
 
-    repeat_rows(rows + 2, 2, forward)
+    repeat_rows(rows + 2, 6, forward)
 
     r_id = lax.broadcasted_iota(jnp.int32, (rows, lanes), 0)
     above = jnp.where(r_id - 1 >= edge[0], 1.0, 0.0)
@@ -520,18 +588,22 @@
     for k in (0, 1, rows + 2, rows + 3):
         g3_ref[256 * k : 256 * (k + 1), :] = jnp.zeros((256, lanes), bf16)
 
+    sg_sum[...] = jnp.zeros_like(sg_sum)
+    go_sum[...] = jnp.zeros_like(go_sum)
+
     def backward(rs):
         gos = [get_lanes(go_ref, r * 16, 16).astype(bf16) for r in rs]
         gts = [dot(wht_ref[...], go) for go in gos]
-        head, gsum, sg = 0.0, 0.0, 0.0
+        head, gsum, sums = 0.0, 0.0, [0.0] * crops
         for r, go, gt in zip(rs, gos, gts):
             put_rows(go_out, r * 16, go)
             spot = (r + 1) * 128
-            head = head + dot_nt(go, rows_of(h3_ref, spot, 128))
-            gsum = gsum + dot_nt(ones, go)
-            g = gt.astype(bf16).astype(f32) * rows_of(m_ref, spot, 128).astype(f32)
+            head = head + dot_nt(rows_of(h3_ref, spot, 128), go)
+            gsum = gsum + fold_lanes(go.astype(f32))
+            g = jnp.where(rows_of(m_ref, spot, 128).astype(f32) > 0, gt.astype(bf16).astype(f32), 0.0)
             gb = g.astype(bf16)
-            sg = sg + dot_nt(ones, gb)
+            for c in range(crops):
+                sums[c] = sums[c] + fold_lanes(g[:, width * c : width * (c + 1)])
             parts = []
             for pr in range(2):
                 even, odd = g[64 * pr : 64 * pr + 32], g[64 * pr + 32 : 64 * pr + 64]
@@ -542,10 +614,14 @@
                 ]
             put_rows(g3_ref, (r + 2) * 256, jnp.concatenate(parts, axis=0))
         head_ref[...] += head
-        sums_ref[3:4, 0:16] += jnp.sum(gsum, axis=0, keepdims=True)
-        sg_ref[...] += sg
-
-    repeat_rows(rows, 2, backward)
+        go_sum[...] += gsum
+        for c in range(crops):
+            sg_sum[c] += sums[c]
+
+    repeat_rows(rows, 4, backward)
+    for c in range(crops):
+        sg_ref[c : c + 1, :] = lane_sums(sg_sum[c])[0:1]
+    sums_ref[3:4, 0:16] = lane_sums(go_sum[...])[0:1]
     sg_copies = share(tiles, "tile", sg_ref, sg_got, s2_send, s2_recv)
 
     def down(ks):
@@ -558,39 +634,33 @@
     down([rows, rows + 1])
     rim_hi[...] = gc_ref[64 * rows : 64 * rows + 128, :].astype(bf16)
     finish_rims = swap_edges(tiles, [(rim_lo, rim_hi, rim_up, rim_dn)], rim_send, rim_recv)
-    repeat_rows(rows - 2, 2, lambda ks: down([k + 2 for k in ks]))
-
-    def weights_three(rs):
+    repeat_rows(rows - 2, 7, down, 2)
+
+    def weights_three(ks):
         d3 = 0.0
-        for r in rs:
-            spot = (r + 2) * 256
-            gb = jnp.concatenate([rows_of(g3_ref, spot + 32, 64), rows_of(g3_ref, spot + 160, 64)], axis=0)
-            d3 = d3 + dot_nt(rows_of(x3_ref, (r + 1) * 192, 576), gb)
+        for k in ks:
+            gs = [rows_of(g3_ref, k * 256 + 128 * j + 160, 64) for j in range(4)]
+            d3 = d3 + dot_nt(jnp.concatenate(gs, axis=0), rows_of(x3_ref, (k + 1) * 192, 192))
         d3_ref[...] += d3
 
-    repeat_rows(rows, 2, weights_three)
-    d3 = jnp.transpose(d3_ref[...])
-    for block in range(5):
-        packed = jnp.zeros((CH_ONE, 128), f32)
-        for tap in range(2 * block, min(2 * block + 2, 9)):
-            a, b = tap // 3, tap % 3
-            total = jnp.zeros((CH_ONE, CH_TWO), f32)
-            for p in range(4):
-                n = 3 * ((p // 2 + a + 1) // 2) + (p % 2 + b + 1) // 2
-                total = total + d3[32 * p : 32 * (p + 1), 64 * n : 64 * (n + 1)]
-            if tap % 2 == 0:
-                packed = jnp.concatenate([total, packed[:, 64:128]], axis=1)
-            else:
-                packed = jnp.concatenate([packed[:, 0:64], total], axis=1)
-        if block < 4:
-            pay_a[32 * block : 32 * (block + 1), :] = packed
+    repeat_rows(rows + 2, 6, weights_three)
+    for tap in range(9):
+        a, b = tap // 3, tap % 3
+        total = jnp.zeros((CH_ONE, CH_TWO), f32)
+        for first in (2 - a, 3 - a):
+            for pc in range(2):
+                s = (pc + b + 1) // 2
+                total = total + d3_ref[64 * first + 32 * pc : 64 * first + 32 * pc + 32, 64 * s : 64 * (s + 1)]
+        if tap < 8:
+            pay_a[32 * (tap // 2) : 32 * (tap // 2 + 1), 64 * (tap % 2) : 64 * (tap % 2 + 1)] = total
         else:
-            pay_a[128:144, :] = jnp.concatenate([packed[0:16, 0:64], packed[16:32, 0:64]], axis=1)
+            pay_a[128:144, :] = jnp.concatenate([total[0:16], total[16:32]], axis=1)
     outer = jnp.zeros((CH_ONE, 128), f32)
     for c in range(crops):
         outer = outer + as_column(over_phases(sg_ref[c : c + 1, :]))[0:32] * jnp.concatenate([unit[c : c + 1]] * 2, axis=1)
         sums_ref[2:3, :] += sg_ref[c : c + 1, :]
-    pay_a[144:160, :] = head_ref[...]
+    head = jnp.concatenate([head_ref[...], jnp.zeros((128, 112), f32)], axis=1)
+    pay_a[144:160, :] = jnp.transpose(head)[0:16]
     pay_a[160:176, :] = jnp.concatenate([outer[0:16, 0:64], outer[16:32, 0:64]], axis=1)
     pay_a[176:184, :] = sums_ref[...]
     if pay_a.shape[0] > 184:
@@ -607,68 +677,67 @@
     pay_c[...] = jnp.zeros_like(pay_c)
     d2_ref[...] = jnp.zeros_like(d2_ref)
     d1_ref[...] = jnp.zeros_like(d1_ref)
+    g2_sum[...] = jnp.zeros_like(g2_sum)
+    raw = jnp.concatenate([wide(v, width) for v in raw], axis=1)
+    g2_ref = g3_ref
+
+    def masked(ks, extras=None):
+        sums = 0.0
+        for j, k in enumerate(ks):
+            coarse = rows_of(gc_ref, k * 64, 64)
+            if extras is not None:
+                coarse = coarse + extras[j]
+            grad = (coarse + raw).astype(bf16).astype(f32)
+            h2 = rows_of(x3_ref, (k + 1) * 192 + 64, 64).astype(f32)
+            g = jnp.where(h2 > 0, grad, 0.0)
+            if extras is None or 0 < j < 3:
+                sums = sums + fold_lanes(g)
+            put_rows(g2_ref, k * 192, three_columns(g.astype(bf16), g, crops))
+        g2_sum[...] += sums
+
+    repeat_rows(rows - 2, 7, masked, 2)
     finish_rims()
-    g2_ref = g3_ref
-
-    def masked(k, extra=None):
-        coarse = rows_of(gc_ref, k * 64, 64)
-        if extra is not None:
-            coarse = coarse + extra
-        grad = (coarse + jnp.concatenate([wide(v, width) for v in raw], axis=1)).astype(bf16).astype(f32)
-        h2 = rows_of(x3_ref, (k + 1) * 192 + 64, 64).astype(f32)
-        put_rows(g2_ref, k * 192, three_columns(jnp.where(h2 > 0, grad, 0.0).astype(bf16), crops))
-
     up = jnp.where(edge[0] < 0, rim_up[...].astype(f32), 0.0)
     dn = jnp.where(edge[1] > rows, rim_dn[...].astype(f32), 0.0)
-    masked(0, up[0:64])
-    masked(1, up[64:128])
-    masked(rows, dn[0:64])
-    masked(rows + 1, dn[64:128])
-
-    def inner(ks):
-        for k in ks:
-            masked(k + 2)
-
-    repeat_rows(rows - 2, 2, inner)
+    masked([0, 1, rows, rows + 1], [up[0:64], up[64:128], dn[0:64], dn[64:128]])
+    pay_b[...] = jnp.zeros_like(pay_b)
+
+    pay_b[160:161, 0:64] = lane_sums(g2_sum[...])[0:1]
+
+    def weights_two(rs):
+        d2 = 0.0
+        for r in rs:
+            d2 = d2 + dot_nt(rows_of(x2_ref, (r + 2) * 96, 288), rows_of(g2_ref, (r + 1) * 192 + 64, 64))
+        d2_ref[...] += d2
+
+    repeat_rows(rows, 8, weights_two)
     reduce_a.across()
-    pay_b[...] = jnp.zeros_like(pay_b)
-
-    def weights_two(rs):
-        d2, sums = 0.0, 0.0
-        for r in rs:
-            g2 = rows_of(g2_ref, (r + 1) * 192 + 64, 64)
-            d2 = d2 + dot_nt(rows_of(x2_ref, (r + 2) * 96, 288), g2)
-            sums = sums + dot_nt(ones, g2)
-        d2_ref[...] += d2
-        pay_b[160:168, 0:64] += sums
-
-    repeat_rows(rows, 2, weights_two)
     rest = jnp.concatenate([d2_ref[160:288, :], jnp.zeros((32, 64), f32)], axis=0)
     pay_b[0:160, :] = jnp.concatenate([d2_ref[0:160, :], rest], axis=1)
     reduce_b.scatter()
-    reduce_a.gather(full_a)
 
     def last_back(rs):
         gps = [dot(wd2_ref[...], rows_of(g2_ref, r * 192, 576)) for r in rs]
         gts = [dot(wht_ref[...], rows_of(go_out, r * 16, 16)) for r in rs]
-        d1, sums = 0.0, 0.0
+        d1 = 0.0
         for r, gp, gt in zip(rs, gps, gts):
             gp = 0.25 * gp.astype(bf16).astype(f32)
             g1 = (jnp.concatenate([gp] * 4, axis=0) + gt.astype(bf16).astype(f32)).astype(bf16).astype(f32)
             h1 = rows_of(h1_ref, (r + 3) * 128, 128).astype(f32)
             gb = jnp.where(h1 > 0, g1, 0.0).astype(bf16)
-            sums = sums + dot_nt(ones, gb)
-            d1 = d1 + dot_nt(rows_of(y_ref, (r + 3) * 16, 32), gb)
+            d1 = d1 + dot_nt(gb, jnp.concatenate([rows_of(y_ref, (r + 3) * 16, 32), ones_ref[...]], axis=0))
         d1_ref[...] += d1
-        pay_c[8:16, :] += sums
 
     half = rows // 2
-    repeat_rows(half, 2, last_back)
+    repeat_rows(half, 4, last_back)
+    reduce_a.gather(full_a)
     reduce_b.across()
-    repeat_rows(rows - half, 2, lambda rs: last_back([r + half for r in rs]))
+    repeat_rows(rows - half, 4, last_back, half)
+    d1 = jnp.transpose(jnp.concatenate([d1_ref[...], jnp.zeros((128, 80), f32)], axis=1))
+    pay_c[8:9, :] = d1[32:33]
     total = jnp.zeros((32, 128), f32)
     for p in range(4):
-        total = total + turn(turn(d1_ref[...], -32 * p, 1), -(8 * (p // 2) + p % 2), 0)
+        total = total + turn(turn(d1[0:32], -32 * p, 1), -(8 * (p // 2) + p % 2), 0)
     packed = lane_group(total[0:8], 0)
     for k in range(1, 4):
         packed = packed + turn(lane_group(total[8 * k : 8 * (k + 1)], 0), 32 * k, 1)
@@ -793,17 +862,21 @@
             buf((images_count, part, 128), f32), buf((part * tiles, 128), f32),
         ]
 
+    sources = (
+        images, target_flow, cell_label, conv1_weight, conv2_weight, third[0], head[0], biases, style[0],
+    )
     block_sems = [DMA((tiles,)), DMA((tiles,)), DMA((images_count,)), DMA((images_count,)), DMA((tiles,)), DMA((tiles,))]
     summed = pl.pallas_call(
         lambda *refs: step_kernel(tiles, images_count, grad_scale, float(coarse_count), *refs),
         out_shape=sds((sum(parts) * tiles + small, 128)),
-        in_specs=[SMEM] + [VMEM] * 9,
+        in_specs=[SMEM] + [HBM] * 9,
         out_specs=VMEM,
-        scratch_shapes=[
+        scratch_shapes=[buf(v.shape, v.dtype) for v in sources]
+        + [
             buf(edge), buf(edge), buf(edge, jnp.int32), buf(edge, jnp.int32),
-            buf((128, 32)), buf((CH_TWO, 9 * CH_ONE)), buf((256, 9 * CH_TWO)), buf((128, 16 * CH_ONE)),
+            buf((128, 48)), buf((CH_TWO, 9 * CH_ONE + 16)), buf((128, 14 * CH_TWO + 16)), buf((128, 16 * CH_ONE)),
             buf((CH_ONE, 9 * CH_TWO)), buf((16, 128)), buf((128, 16)),
-            buf((128, 128), f32), buf((64, 128), f32), buf((8, 128), f32), buf((16, 128), f32), buf((32, 128), f32),
+            buf((8, 128), f32), buf((16, 128), f32), buf((32, 128), f32), buf((16, lanes)), buf((16, lanes)),
             buf((16 * (rows + 7), lanes)), buf((lanes // 128, 16 * (rows + 2), 128), f32),
             buf((128 * (rows + 6), lanes)), buf((96 * (rows + 6), lanes)), buf((192 * (rows + 4), lanes)),
             buf((128 * (rows + 2), lanes)), buf((128 * (rows + 2), lanes)),
@@ -811,21 +884,19 @@
             buf((16 * rows, lanes)), buf((256 * (rows + 4), lanes)), buf((64 * (rows + 2), lanes), f32),
             buf(rim), buf(rim), buf(rim), buf(rim),
             buf((8, 128), f32), buf((tiles, 8, 128), f32), buf((8, 128), f32), buf((tiles, 8, 128), f32),
-            buf((16, 128), f32), buf((8, 128), f32),
-            buf((9 * CH_TWO, 128), f32), buf((9 * CH_ONE, CH_TWO), f32), buf((32, 128), f32),
+            buf((128, 16), f32), buf((8, 128), f32),
+            buf((256, 3 * CH_TWO), f32), buf((9 * CH_ONE, CH_TWO), f32), buf((128, 48), f32),
+            buf((crops, CH_TWO, 128), f32), buf((crops, 128, 128), f32), buf((16, 128), f32), buf((CH_TWO, 128), f32),
         ]
         + block_bufs(parts[0])
         + block_bufs(parts[1])
         + [buf((small, 128), f32), buf((tiles, small, 128), f32), buf((small, 128), f32), buf((images_count, small, 128), f32)]
-        + [DMA((4,)), DMA((4,)), DMA((tiles,)), DMA((tiles,)), DMA((tiles,)), DMA((tiles,)), DMA((2,)), DMA((2,))]
+        + [DMA((9,)), DMA((4,)), DMA((4,)), DMA((tiles,)), DMA((tiles,)), DMA((tiles,)), DMA((tiles,)), DMA((2,)), DMA((2,))]
         + block_sems * 2
         + [DMA((tiles,)), DMA((tiles,)), DMA((images_count,)), DMA((images_count,))],
-        compiler_params=pltpu.CompilerParams(collective_id=1, has_side_effects=True, vmem_limit_bytes=62 * 2**20),
+        compiler_params=pltpu.CompilerParams(collective_id=1, has_side_effects=True, vmem_limit_bytes=60 * 2**20),
         name="step",
-    )(
-        nucleus, images, target_flow, cell_label,
-        conv1_weight, conv2_weight, third[0], head[0], biases, style[0],
-    )
+    )(nucleus, *sources)
 
     olds = (
         (conv1_weight, conv1_momentum, conv1_average)

time: 85.2 us -> 65.5 us (0.77)
  Pallas kernels: 82.4 us -> 62.5 us
    pallas_call x1, Pallas kernels: 81.1 us -> 61.2 us  [on_device(): pl.pallas_call(lambda *refs: step_kernel(tiles, images_count, grad_scale,...]
where the time goes in v6:
time: 65.5 us; the launch traced here: 65.3 us
  Pallas kernels  62.5 us (95%)
  between operations  1.77 us (3%)
  local copies, waits for them, and re-layouts  1 us (2%)
    pallas_call x1, Pallas kernels, on_device(): pl.pallas_call(lambda *refs: step_kernel(tiles, images_count, grad_scale,...  61.2 us

profile of v6, /device:TPU:0, one launch (start us, length us, event | category | flops | bytes accessed | tf_op | source)
XLA Modules:
  0.0 65.3 jit_solution(709215024708514038)
XLA Ops:
  1.3 0.0 copy-start.1
  1.3 0.0 copy-start.2
  1.3 0.0 copy-start.3
  1.3 0.0 copy-start.4
  1.4 0.0 copy-start.5
  1.4 0.0 copy-start.6
  1.4 0.0 copy-start.7
  1.4 0.0 copy-start.8
  1.4 0.0 copy-start.9
  1.4 0.0 copy-start.10
  1.4 0.0 copy-start.11
  1.4 0.0 copy-start.12
  1.4 0.0 copy-start.13
  1.4 0.0 copy-start.14
  1.5 0.0 copy-start.15
  1.5 0.0 copy-start.16
  1.5 0.0 copy-start.17
  1.5 0.0 copy-start.18
  1.5 61.2 %step.1.refs_1_ = f32[400,128]{1,0:T(8,128)} custom-call(s32[2]{0:T(128)} %refs_0_.2, bf16[2,2,32,1024]{3,2,1,0:T(8,128)(2,1)} %refs_1_.1, s32[2,2,32,1024]{3,2,1,0:T(8,128)} %refs_2_.2, s32[2,32,1024]{2,1,0:T(8,128)} %refs_3_.2, f32[3,3,2,32]{3,2,1,0:T(2,128)} %refs_2_.3, f32[3,3,32,64]{3,2,1,0:T(8,128)} %refs_5_.3, f32[3,3,32,64]{3,2,1,0:T(8,128)} %bitcast.18, ...), custom_call_target="tpu_custom_call" | custom-call | tf_op jit(solution)/shard_map/step/pallas_call | solution.py:869
  62.7 0.0 copy-done.1
  62.7 0.0 copy-done.2
  62.7 0.0 copy-done.3
  62.9 0.9 %copy-done = f32[400,128]{1,0:T(8,128)S(1)} copy-done((f32[400,128]{1,0:T(8,128)S(1)}, f32[400,128]{1,0:T(8,128)}, u32[]{:S(2)}) %copy-start) | copy-done | bytes 204824
  63.8 1.3 %update.1 = (f32[3,3,2,32]{3,2,1,0:T(2,128)}, f32[3,3,2,32]{3,2,1,0:T(2,128)}, f32[3,3,2,32]{3,2,1,0:T(2,128)}, f32[3,3,32,64]{3,2,1,0:T(8,128)}, f32[3,3,32,64]...) custom-call(s32[1]{0:T(128)S(6)} %copy.42.refs_0_, ...), custom_call_target="tpu_custom_call" | custom-call | tf_op jit(solution)/shard_map/update/pallas_call | solution.py:907
  (16 shorter events, 0.0 us)
Async XLA Ops:
  1.3 61.4 %copy-start.1 = (f32[3,3,32,64]{3,2,1,0:T(8,128)S(1)}, f32[3,3,32,64]{3,2,1,0:T(8,128)}, u32[]{:S(2)}) copy-start(f32[3,3,32,64]{3,2,1,0:T(8,128)} %refs_5_.3) | copy-start | bytes 221188
  1.3 61.4 %copy-start.2 = (f32[3,3,64,32]{2,3,1,0:T(8,128)S(1)}, f32[3,3,64,32]{2,3,1,0:T(8,128)}, u32[]{:S(2)}) copy-start(f32[3,3,64,32]{2,3,1,0:T(8,128)} %param.34) | copy-start | bytes 221188
  1.3 61.4 %copy-start.3 = (f32[3,3,32,64]{3,2,1,0:T(8,128)S(1)}, f32[3,3,32,64]{3,2,1,0:T(8,128)}, u32[]{:S(2)}) copy-start(f32[3,3,32,64]{3,2,1,0:T(8,128)} %refs_6_.1) | copy-start | bytes 221188
  1.3 61.4 %copy-start.4 = (f32[3,3,32,64]{3,2,1,0:T(8,128)S(1)}, f32[3,3,32,64]{3,2,1,0:T(8,128)}, u32[]{:S(2)}) copy-start(f32[3,3,32,64]{3,2,1,0:T(8,128)} %refs_7_.1) | copy-start | bytes 221188
  1.4 61.4 %copy-start.5 = (f32[3,3,64,32]{2,3,1,0:T(8,128)S(1)}, f32[3,3,64,32]{2,3,1,0:T(8,128)}, u32[]{:S(2)}) copy-start(f32[3,3,64,32]{2,3,1,0:T(8,128)} %param.35) | copy-start | bytes 221188
  1.4 61.4 %copy-start.6 = (f32[3,3,64,32]{2,3,1,0:T(8,128)S(1)}, f32[3,3,64,32]{2,3,1,0:T(8,128)}, u32[]{:S(2)}) copy-start(f32[3,3,64,32]{2,3,1,0:T(8,128)} %param.36) | copy-start | bytes 221188
  1.4 61.4 %copy-start.7 = (f32[64,32]{0,1:T(8,128)S(1)}, f32[64,32]{0,1:T(8,128)}, u32[]{:S(2)}) copy-start(f32[64,32]{0,1:T(8,128)} %param.37) | copy-start | bytes 24580
  1.4 61.4 %copy-start.8 = (f32[3,3,2,32]{3,2,1,0:T(2,128)S(1)}, f32[3,3,2,32]{3,2,1,0:T(2,128)}, u32[]{:S(2)}) copy-start(f32[3,3,2,32]{3,2,1,0:T(2,128)} %refs_2_.3) | copy-start | bytes 6916
  1.4 61.4 %copy-start.9 = (f32[64,32]{0,1:T(8,128)S(1)}, f32[64,32]{0,1:T(8,128)}, u32[]{:S(2)}) copy-start(f32[64,32]{0,1:T(8,128)} %param.38) | copy-start | bytes 24580
  1.4 61.4 %copy-start.10 = (f32[64,32]{0,1:T(8,128)S(1)}, f32[64,32]{0,1:T(8,128)}, u32[]{:S(2)}) copy-start(f32[64,32]{0,1:T(8,128)} %param.39) | copy-start | bytes 24580
  1.4 61.4 %copy-start.11 = (f32[3,3,2,32]{3,2,1,0:T(2,128)S(1)}, f32[3,3,2,32]{3,2,1,0:T(2,128)}, u32[]{:S(2)}) copy-start(f32[3,3,2,32]{3,2,1,0:T(2,128)} %refs_3_.3) | copy-start | bytes 6916
  1.4 61.4 %copy-start.12 = (f32[3,3,2,32]{3,2,1,0:T(2,128)S(1)}, f32[3,3,2,32]{3,2,1,0:T(2,128)}, u32[]{:S(2)}) copy-start(f32[3,3,2,32]{3,2,1,0:T(2,128)} %refs_4_.3) | copy-start | bytes 6916
  1.4 61.4 %copy-start.13 = (f32[32,3]{0,1:T(4,128)S(1)}, f32[32,3]{0,1:T(4,128)}, u32[]{:S(2)}) copy-start(f32[32,3]{0,1:T(4,128)} %param.40) | copy-start | bytes 1156
  1.4 61.4 %copy-start.14 = (f32[163]{0:T(256)S(1)}, f32[163]{0:T(256)}, u32[]{:S(2)}) copy-start(f32[163]{0:T(256)} %refs_17_.1) | copy-start | bytes 1960
  1.5 61.4 %copy-start.15 = (f32[32,3]{0,1:T(4,128)S(1)}, f32[32,3]{0,1:T(4,128)}, u32[]{:S(2)}) copy-start(f32[32,3]{0,1:T(4,128)} %param.41) | copy-start | bytes 1156
  1.5 61.4 %copy-start.16 = (f32[32,3]{0,1:T(4,128)S(1)}, f32[32,3]{0,1:T(4,128)}, u32[]{:S(2)}) copy-start(f32[32,3]{0,1:T(4,128)} %param.42) | copy-start | bytes 1156
  1.5 61.4 %copy-start.17 = (f32[163]{0:T(256)S(1)}, f32[163]{0:T(256)}, u32[]{:S(2)}) copy-start(f32[163]{0:T(256)} %refs_18_.1) | copy-start | bytes 1960
  1.5 61.4 %copy-start.18 = (f32[163]{0:T(256)S(1)}, f32[163]{0:T(256)}, u32[]{:S(2)}) copy-start(f32[163]{0:T(256)} %refs_19_.1) | copy-start | bytes 1960
  62.9 0.9 %copy-start = (f32[400,128]{1,0:T(8,128)S(1)}, f32[400,128]{1,0:T(8,128)}, u32[]{:S(2)}) copy-start(f32[400,128]{1,0:T(8,128)} %step.1.refs_1_) | copy-start | bytes 614404

commit v7 on v6

--- a/solution.py
+++ b/solution.py
@@ -20,13 +20,14 @@
 bf16 = jnp.bfloat16
 
 HALO = 8
+EARLY = 6
 VMEM = pl.BlockSpec(memory_space=pltpu.VMEM)
 SMEM = pl.BlockSpec(memory_space=pltpu.SMEM)
 HBM = pl.BlockSpec(memory_space=pltpu.HBM)
 MESH = pl.DeviceIdType.MESH
 DMA = pltpu.SemaphoreType.DMA
 
-BLOCK_ROWS = ((144, 16, 16, 8), (160, 8), (8, 8))
+BLOCK_ROWS = ((144, 16, 16, 8), (160, 8), (8,))
 
 
 def dot(a, b):
@@ -339,7 +340,7 @@
     x_ref, t_ref, label_ref, k1_ref, k2_ref, k3_ref, kh_ref, bias_ref, ws_ref,
     x_lo, x_hi, t_lo, t_hi,
     w1_ref, w2_ref, w3_ref, wd3_ref, wd2_ref, wh_ref, wht_ref, b3_ref, bh_ref, base_ref, ones_ref, mark_ref,
-    y_ref, t_out, h1_ref, x2_ref, x3_ref, h3_ref, m_ref, fe_ref, go_ref, go_out, g3_ref, gc_ref,
+    y_ref, t_out, h1_ref, x2_ref, x3_ref, h3_ref, m_ref, fe_ref, go_ref, g3_ref, gc_ref,
     rim_lo, rim_hi, rim_up, rim_dn,
     style_ref, style_got, sg_ref, sg_got, head_ref, sums_ref, d3_ref, d2_ref, d1_ref,
     style_sum, sg_sum, go_sum, g2_sum,
@@ -348,6 +349,7 @@
     load_sems, halo_send, halo_recv, s1_send, s1_recv, s2_send, s2_recv, rim_send, rim_recv,
     *sems,
 ):
+    pre_ref = gc_ref
     reduce_a = Reduction(tiles, images, pay_a, got_a, own_a, met_a, sems[0:6])
     reduce_b = Reduction(tiles, images, pay_b, got_b, own_b, met_b, sems[6:12])
     arrived = greet((("tile", tiles), ("img", images)))
@@ -363,6 +365,9 @@
     for load in loads:
         load.start()
     ones_ref[...] = jnp.ones_like(ones_ref)
+    for load in loads[0:3]:
+        load.wait()
+    first_tables(k1_ref, k2_ref, bias_ref, w1_ref, w2_ref, base_ref)
     arrived()
     last = x_ref.shape[2] - HALO
     finish_halo = swap_edges(
@@ -373,9 +378,7 @@
         ],
         halo_send, halo_recv,
     )
-    for load in loads[0:4]:
-        load.wait()
-    first_tables(k1_ref, k2_ref, bias_ref, w1_ref, w2_ref, base_ref)
+    loads[3].wait()
     crops = x_ref.shape[0]
     width = x_ref.shape[3] // 2
     lanes = crops * width
@@ -467,8 +470,7 @@
     extra = dot(perm_h, pixel_windows(halo_rows, lambda row: row // HALO % 2 == 1))
     y_ref[0:64, :] = (y_ref[0:64, :].astype(f32) + extra[0:64]).astype(bf16)
     y_ref[y_rows - 64 : y_rows, :] = (y_ref[y_rows - 64 : y_rows, :].astype(f32) + extra[64:128]).astype(bf16)
-    conv_one([0, 1, 2, 3], False)
-    conv_one([rows + 2, rows + 3, rows + 4, rows + 5], False)
+    conv_one([0, 1, 2, 3, rows + 2, rows + 3, rows + 4, rows + 5], False)
     style_sum[...] = jnp.zeros_like(style_sum)
     repeat_rows(rows, 8, conv_two, 2)
     style_ref[...] = jnp.zeros_like(style_ref)
@@ -496,12 +498,20 @@
     even, odd = both_columns(target_rows)
     put_lanes(t_out, 0, dot(perm_t, jnp.concatenate([even, odd], axis=0).astype(bf16)))
     later_tables(k2_ref, k3_ref, kh_ref, bias_ref, w3_ref, wd3_ref, wd2_ref, wh_ref, wht_ref, b3_ref, bh_ref)
+
+    def third_input(k):
+        x = rows_of(x3_ref, k * 192, 576)
+        return jnp.concatenate([x, x[64:128], x[192:384], x[448:512]], axis=0)
+
+    for k in range(EARLY):
+        put_rows(pre_ref, k * 128, dot(w3_ref[:, 0:896], third_input(k)))
     wait_all(style_copies)
     style_raw = in_order(style_got, tiles)[:, 0:64] / coarse_count
     style_inv = lax.rsqrt(jnp.mean(style_raw * style_raw, axis=1, keepdims=True) + norm_eps)
     unit = style_raw * style_inv
     vec = dot_nt(unit, ws_ref[...], highest)
     vec = jnp.concatenate([vec] * 4, axis=1) + b3_ref[0:1, :]
+    bias3 = jnp.concatenate([wide(as_column(vec[c : c + 1]), width) for c in range(crops)], axis=1)
     row = lax.broadcasted_iota(jnp.int32, (16, lanes), 0)
     lane = lax.broadcasted_iota(jnp.int32, (16, lanes), 1)
     mark_ref[...] = jnp.where(row // 3 == lane // width, 1.0, 0.0).astype(bf16)
@@ -512,12 +522,13 @@
             table = jnp.where(row == 3 * c + k, jnp.broadcast_to(piece, (128, 128)), table)
     w3_ref[:, 896:912] = jnp.transpose(table)[:, 0:16].astype(bf16)
 
-    def forward(ks):
+    def forward(ks, early=False):
         pre = []
         for k in ks:
-            x = rows_of(x3_ref, k * 192, 576)
-            x = jnp.concatenate([x, x[64:128], x[192:384], x[448:512], mark_ref[...]], axis=0)
-            pre.append(dot(w3_ref[...], x))
+            if early:
+                pre.append(rows_of(pre_ref, k * 128, 128) + bias3)
+            else:
+                pre.append(dot(w3_ref[...], jnp.concatenate([third_input(k), mark_ref[...]], axis=0)))
         hs = []
         for k, p in zip(ks, pre):
             p = jnp.maximum(p, 0.0)
@@ -532,7 +543,8 @@
             fe = (o[0:8] - 0.25 * t[0:8]) * valid(k - 1, edge)
             put_lanes(fe_ref, k * 16, jnp.concatenate([fe, o[8:16]], axis=0))
 
-    repeat_rows(rows + 2, 6, forward)
+    forward(range(EARLY), True)
+    repeat_rows(rows + 2 - EARLY, 12, forward, EARLY)
 
     r_id = lax.broadcasted_iota(jnp.int32, (rows, lanes), 0)
     above = jnp.where(r_id - 1 >= edge[0], 1.0, 0.0)
@@ -594,14 +606,15 @@
     def backward(rs):
         gos = [get_lanes(go_ref, r * 16, 16).astype(bf16) for r in rs]
         gts = [dot(wht_ref[...], go) for go in gos]
-        head, gsum, sums = 0.0, 0.0, [0.0] * crops
+        head, gsum, sums, kept = 0.0, 0.0, [0.0] * crops, []
         for r, go, gt in zip(rs, gos, gts):
-            put_rows(go_out, r * 16, go)
             spot = (r + 1) * 128
             head = head + dot_nt(rows_of(h3_ref, spot, 128), go)
             gsum = gsum + fold_lanes(go.astype(f32))
-            g = jnp.where(rows_of(m_ref, spot, 128).astype(f32) > 0, gt.astype(bf16).astype(f32), 0.0)
-            gb = g.astype(bf16)
+            gt = gt.astype(bf16)
+            gb = jnp.where(rows_of(m_ref, spot, 128) > 0, gt, jnp.zeros_like(gt))
+            g = gb.astype(f32)
+            kept.append(gt)
             for c in range(crops):
                 sums[c] = sums[c] + fold_lanes(g[:, width * c : width * (c + 1)])
             parts = []
@@ -613,6 +626,8 @@
                     from_right(even, crops).astype(bf16),
                 ]
             put_rows(g3_ref, (r + 2) * 256, jnp.concatenate(parts, axis=0))
+        for r, gt in zip(rs, kept):
+            put_rows(h3_ref, (r + 1) * 128, gt)
         head_ref[...] += head
         go_sum[...] += gsum
         for c in range(crops):
@@ -674,7 +689,6 @@
     grad_raw = style_inv * grad_unit - style_inv * style_inv * style_inv * style_raw * mixed
     grad_raw = jnp.concatenate([grad_raw / coarse_count] * 2, axis=1)
     raw = [as_column(grad_raw[c : c + 1])[0:64] for c in range(crops)]
-    pay_c[...] = jnp.zeros_like(pay_c)
     d2_ref[...] = jnp.zeros_like(d2_ref)
     d1_ref[...] = jnp.zeros_like(d1_ref)
     g2_sum[...] = jnp.zeros_like(g2_sum)
@@ -687,12 +701,12 @@
             coarse = rows_of(gc_ref, k * 64, 64)
             if extras is not None:
                 coarse = coarse + extras[j]
-            grad = (coarse + raw).astype(bf16).astype(f32)
-            h2 = rows_of(x3_ref, (k + 1) * 192 + 64, 64).astype(f32)
-            g = jnp.where(h2 > 0, grad, 0.0)
+            grad = (coarse + raw).astype(bf16)
+            gb = jnp.where(rows_of(x3_ref, (k + 1) * 192 + 64, 64) > 0, grad, jnp.zeros_like(grad))
+            g = gb.astype(f32)
             if extras is None or 0 < j < 3:
                 sums = sums + fold_lanes(g)
-            put_rows(g2_ref, k * 192, three_columns(g.astype(bf16), g, crops))
+            put_rows(g2_ref, k * 192, three_columns(gb, g, crops))
         g2_sum[...] += sums
 
     repeat_rows(rows - 2, 7, masked, 2)
@@ -718,30 +732,29 @@
 
     def last_back(rs):
         gps = [dot(wd2_ref[...], rows_of(g2_ref, r * 192, 576)) for r in rs]
-        gts = [dot(wht_ref[...], rows_of(go_out, r * 16, 16)) for r in rs]
         d1 = 0.0
-        for r, gp, gt in zip(rs, gps, gts):
+        for r, gp in zip(rs, gps):
             gp = 0.25 * gp.astype(bf16).astype(f32)
-            g1 = (jnp.concatenate([gp] * 4, axis=0) + gt.astype(bf16).astype(f32)).astype(bf16).astype(f32)
-            h1 = rows_of(h1_ref, (r + 3) * 128, 128).astype(f32)
-            gb = jnp.where(h1 > 0, g1, 0.0).astype(bf16)
+            gt = rows_of(h3_ref, (r + 1) * 128, 128).astype(f32)
+            g1 = (jnp.concatenate([gp] * 4, axis=0) + gt).astype(bf16)
+            gb = jnp.where(rows_of(h1_ref, (r + 3) * 128, 128) > 0, g1, jnp.zeros_like(g1))
             d1 = d1 + dot_nt(gb, jnp.concatenate([rows_of(y_ref, (r + 3) * 16, 32), ones_ref[...]], axis=0))
         d1_ref[...] += d1
 
-    half = rows // 2
+    half, quarter = rows // 2, rows // 4
     repeat_rows(half, 4, last_back)
     reduce_a.gather(full_a)
+    repeat_rows(quarter, 4, last_back, half)
     reduce_b.across()
-    repeat_rows(rows - half, 4, last_back, half)
+    repeat_rows(rows - half - quarter, 4, last_back, half + quarter)
     d1 = jnp.transpose(jnp.concatenate([d1_ref[...], jnp.zeros((128, 80), f32)], axis=1))
-    pay_c[8:9, :] = d1[32:33]
     total = jnp.zeros((32, 128), f32)
     for p in range(4):
         total = total + turn(turn(d1[0:32], -32 * p, 1), -(8 * (p // 2) + p % 2), 0)
     packed = lane_group(total[0:8], 0)
-    for k in range(1, 4):
+    for k in range(1, 3):
         packed = packed + turn(lane_group(total[8 * k : 8 * (k + 1)], 0), 32 * k, 1)
-    pay_c[0:8, :] = packed
+    pay_c[...] = packed + lane_group(jnp.broadcast_to(over_phases(d1[32:33]), (8, 128)), 3)
     copies = share(tiles, "tile", pay_c, got_c, sems[12], sems[13])
     reduce_b.gather(full_b)
     wait_all(copies)
@@ -798,7 +811,7 @@
     total = jnp.concatenate([total[4 * o : 4 * o + 1] for o in range(OUT_CH)], axis=0)
     step(4, (slice(None), slice(None)), total[:, 0:32])
     sums = sum_ref[176:184, :]
-    one = over_phases(jnp.sum(sum_ref[third_at + 8 : third_at + 16, :], axis=0, keepdims=True))
+    one = turn(sum_ref[third_at : third_at + 1, :], -96, 1)
     two = jnp.sum(sum_ref[second_at + 160 : second_at + 168, :], axis=0, keepdims=True)
     three = over_phases(sums[2:3])
     lane = lax.broadcasted_iota(jnp.int32, (1, 128), 1)
@@ -868,7 +881,7 @@
     block_sems = [DMA((tiles,)), DMA((tiles,)), DMA((images_count,)), DMA((images_count,)), DMA((tiles,)), DMA((tiles,))]
     summed = pl.pallas_call(
         lambda *refs: step_kernel(tiles, images_count, grad_scale, float(coarse_count), *refs),
-        out_shape=sds((sum(parts) * tiles + small, 128)),
+        out_shape=pltpu.VMEM((sum(parts) * tiles + small, 128), f32),
         in_specs=[SMEM] + [HBM] * 9,
         out_specs=VMEM,
         scratch_shapes=[buf(v.shape, v.dtype) for v in sources]
@@ -881,7 +894,7 @@
             buf((128 * (rows + 6), lanes)), buf((96 * (rows + 6), lanes)), buf((192 * (rows + 4), lanes)),
             buf((128 * (rows + 2), lanes)), buf((128 * (rows + 2), lanes)),
             buf((lanes // 128, 16 * (rows + 2), 128), f32), buf((lanes // 128, 16 * rows, 128), f32),
-            buf((16 * rows, lanes)), buf((256 * (rows + 4), lanes)), buf((64 * (rows + 2), lanes), f32),
+            buf((256 * (rows + 4), lanes)), buf((64 * (rows + 2), lanes), f32),
             buf(rim), buf(rim), buf(rim), buf(rim),
             buf((8, 128), f32), buf((tiles, 8, 128), f32), buf((8, 128), f32), buf((tiles, 8, 128), f32),
             buf((128, 16), f32), buf((8, 128), f32),

time: 65.5 us -> 60.3 us (0.921)
  Pallas kernels: 62.5 us -> 58.2 us
  local copies, waits for them, and re-layouts: 1 us -> 0.08 us
    pallas_call x1, Pallas kernels: 61.2 us -> 56.8 us  [on_device(): pl.pallas_call(lambda *refs: step_kernel(tiles, images_count, grad_scale,...]
    unnamed x38 -> x36, local copies, waits for them, and re-layouts: 1 us -> 0.08 us
where the time goes in v7:
time: 60.3 us; the launch traced here: 60.1 us
  Pallas kernels  58.2 us (97%)
  between operations  1.78 us (3%)
    pallas_call x1, Pallas kernels, on_device(): pl.pallas_call(lambda *refs: step_kernel(tiles, images_count, grad_scale,...  56.8 us
    pallas_call x1, Pallas kernels, on_device(): pl.pallas_call(lambda *refs: update_kernel(float(pixel_count), parts[0] *...  1.39 us

profile of v7, /device:TPU:0, one launch (start us, length us, event | category | flops | bytes accessed | tf_op | source)
XLA Modules:
  0.0 60.1 jit_solution(5199054741549892372)
XLA Ops:
  1.3 0.0 copy-start
  1.3 0.0 copy-start.1
  1.3 0.0 copy-start.2
  1.3 0.0 copy-start.3
  1.4 0.0 copy-start.4
  1.4 0.0 copy-start.5
  1.4 0.0 copy-start.6
  1.4 0.0 copy-start.7
  1.4 0.0 copy-start.8
  1.4 0.0 copy-start.9
  1.4 0.0 copy-start.10
  1.4 0.0 copy-start.11
  1.4 0.0 copy-start.12
  1.4 0.0 copy-start.13
  1.5 0.0 copy-start.14
  1.5 0.0 copy-start.15
  1.5 0.0 copy-start.16
  1.5 0.0 copy-start.17
  1.5 56.8 %step.1.refs_1_ = f32[392,128]{1,0:T(8,128)S(1)} custom-call(s32[2]{0:T(128)} %refs_0_.2, bf16[2,2,32,1024]{3,2,1,0:T(8,128)(2,1)} %refs_1_.1, s32[2,2,32,1024]{3,2,1,0:T(8,128)} %refs_2_.2, s32[2,32,1024]{2,1,0:T(8,128)} %refs_3_.2, f32[3,3,2,32]{3,2,1,0:T(2,128)} %refs_2_.3, f32[3,3,32,64]{3,2,1,0:T(8,128)} %refs_5_.3, f32[3,3,32,64]{3,2,1,0:T(8,128)} %bitcast.18, ...), custom_call_target="tpu_custom_call" | custom-call | tf_op jit(solution)/shard_map/step/pallas_call | solution.py:882
  58.3 0.0 copy-done
  58.3 0.0 copy-done.1
  58.3 0.0 copy-done.2
  58.4 0.0 copy-done.3
  58.5 1.4 %update.1 = (f32[3,3,2,32]{3,2,1,0:T(2,128)}, f32[3,3,2,32]{3,2,1,0:T(2,128)}, f32[3,3,2,32]{3,2,1,0:T(2,128)}, f32[3,3,32,64]{3,2,1,0:T(8,128)}, f32[3,3,32,64]...) custom-call(s32[1]{0:T(128)S(6)} %copy.42.refs_0_, ...), custom_call_target="tpu_custom_call" | custom-call | tf_op jit(solution)/shard_map/update/pallas_call | solution.py:920
  (14 shorter events, 0.0 us)
Async XLA Ops:
  1.3 57.0 %copy-start = (f32[3,3,32,64]{3,2,1,0:T(8,128)S(1)}, f32[3,3,32,64]{3,2,1,0:T(8,128)}, u32[]{:S(2)}) copy-start(f32[3,3,32,64]{3,2,1,0:T(8,128)} %refs_5_.3) | copy-start | bytes 221188
  1.3 57.0 %copy-start.1 = (f32[3,3,64,32]{2,3,1,0:T(8,128)S(1)}, f32[3,3,64,32]{2,3,1,0:T(8,128)}, u32[]{:S(2)}) copy-start(f32[3,3,64,32]{2,3,1,0:T(8,128)} %param.34) | copy-start | bytes 221188
  1.3 57.0 %copy-start.2 = (f32[3,3,32,64]{3,2,1,0:T(8,128)S(1)}, f32[3,3,32,64]{3,2,1,0:T(8,128)}, u32[]{:S(2)}) copy-start(f32[3,3,32,64]{3,2,1,0:T(8,128)} %refs_6_.1) | copy-start | bytes 221188
  1.3 57.0 %copy-start.3 = (f32[3,3,32,64]{3,2,1,0:T(8,128)S(1)}, f32[3,3,32,64]{3,2,1,0:T(8,128)}, u32[]{:S(2)}) copy-start(f32[3,3,32,64]{3,2,1,0:T(8,128)} %refs_7_.1) | copy-start | bytes 221188
  1.4 57.0 %copy-start.4 = (f32[3,3,64,32]{2,3,1,0:T(8,128)S(1)}, f32[3,3,64,32]{2,3,1,0:T(8,128)}, u32[]{:S(2)}) copy-start(f32[3,3,64,32]{2,3,1,0:T(8,128)} %param.35) | copy-start | bytes 221188
  1.4 57.0 %copy-start.5 = (f32[3,3,64,32]{2,3,1,0:T(8,128)S(1)}, f32[3,3,64,32]{2,3,1,0:T(8,128)}, u32[]{:S(2)}) copy-start(f32[3,3,64,32]{2,3,1,0:T(8,128)} %param.36) | copy-start | bytes 221188
  1.4 57.0 %copy-start.6 = (f32[64,32]{0,1:T(8,128)S(1)}, f32[64,32]{0,1:T(8,128)}, u32[]{:S(2)}) copy-start(f32[64,32]{0,1:T(8,128)} %param.37) | copy-start | bytes 24580
  1.4 57.0 %copy-start.7 = (f32[3,3,2,32]{3,2,1,0:T(2,128)S(1)}, f32[3,3,2,32]{3,2,1,0:T(2,128)}, u32[]{:S(2)}) copy-start(f32[3,3,2,32]{3,2,1,0:T(2,128)} %refs_2_.3) | copy-start | bytes 6916
  1.4 57.0 %copy-start.8 = (f32[64,32]{0,1:T(8,128)S(1)}, f32[64,32]{0,1:T(8,128)}, u32[]{:S(2)}) copy-start(f32[64,32]{0,1:T(8,128)} %param.38) | copy-start | bytes 24580
  1.4 57.0 %copy-start.9 = (f32[64,32]{0,1:T(8,128)S(1)}, f32[64,32]{0,1:T(8,128)}, u32[]{:S(2)}) copy-start(f32[64,32]{0,1:T(8,128)} %param.39) | copy-start | bytes 24580
  1.4 57.0 %copy-start.10 = (f32[3,3,2,32]{3,2,1,0:T(2,128)S(1)}, f32[3,3,2,32]{3,2,1,0:T(2,128)}, u32[]{:S(2)}) copy-start(f32[3,3,2,32]{3,2,1,0:T(2,128)} %refs_3_.3) | copy-start | bytes 6916
  1.4 57.0 %copy-start.11 = (f32[3,3,2,32]{3,2,1,0:T(2,128)S(1)}, f32[3,3,2,32]{3,2,1,0:T(2,128)}, u32[]{:S(2)}) copy-start(f32[3,3,2,32]{3,2,1,0:T(2,128)} %refs_4_.3) | copy-start | bytes 6916
  1.4 57.0 %copy-start.12 = (f32[32,3]{0,1:T(4,128)S(1)}, f32[32,3]{0,1:T(4,128)}, u32[]{:S(2)}) copy-start(f32[32,3]{0,1:T(4,128)} %param.40) | copy-start | bytes 1156
  1.4 57.0 %copy-start.13 = (f32[163]{0:T(256)S(1)}, f32[163]{0:T(256)}, u32[]{:S(2)}) copy-start(f32[163]{0:T(256)} %refs_17_.1) | copy-start | bytes 1960
  1.5 57.0 %copy-start.14 = (f32[32,3]{0,1:T(4,128)S(1)}, f32[32,3]{0,1:T(4,128)}, u32[]{:S(2)}) copy-start(f32[32,3]{0,1:T(4,128)} %param.41) | copy-start | bytes 1156
  1.5 57.0 %copy-start.15 = (f32[32,3]{0,1:T(4,128)S(1)}, f32[32,3]{0,1:T(4,128)}, u32[]{:S(2)}) copy-start(f32[32,3]{0,1:T(4,128)} %param.42) | copy-start | bytes 1156
  1.5 57.0 %copy-start.16 = (f32[163]{0:T(256)S(1)}, f32[163]{0:T(256)}, u32[]{:S(2)}) copy-start(f32[163]{0:T(256)} %refs_18_.1) | copy-start | bytes 1960
  1.5 57.0 %copy-start.17 = (f32[163]{0:T(256)S(1)}, f32[163]{0:T(256)}, u32[]{:S(2)}) copy-start(f32[163]{0:T(256)} %refs_19_.1) | copy-start | bytes 1960

commit v8 on v7

--- a/solution.py
+++ b/solution.py
@@ -20,6 +20,7 @@
 bf16 = jnp.bfloat16
 
 HALO = 8
+BACK = 2
 EARLY = 6
 VMEM = pl.BlockSpec(memory_space=pltpu.VMEM)
 SMEM = pl.BlockSpec(memory_space=pltpu.SMEM)
@@ -365,9 +366,6 @@
     for load in loads:
         load.start()
     ones_ref[...] = jnp.ones_like(ones_ref)
-    for load in loads[0:3]:
-        load.wait()
-    first_tables(k1_ref, k2_ref, bias_ref, w1_ref, w2_ref, base_ref)
     arrived()
     last = x_ref.shape[2] - HALO
     finish_halo = swap_edges(
@@ -378,7 +376,9 @@
         ],
         halo_send, halo_recv,
     )
-    loads[3].wait()
+    for load in loads[0:4]:
+        load.wait()
+    first_tables(k1_ref, k2_ref, bias_ref, w1_ref, w2_ref, base_ref)
     crops = x_ref.shape[0]
     width = x_ref.shape[3] // 2
     lanes = crops * width
@@ -603,7 +603,12 @@
     sg_sum[...] = jnp.zeros_like(sg_sum)
     go_sum[...] = jnp.zeros_like(go_sum)
 
-    def backward(rs):
+    def down(ks):
+        both = [dot(wd3_ref[...], rows_of(g3_ref, k * 256 + 128, 512)) for k in ks]
+        return [b[0:64] + b[64:128] for b in both]
+
+    def backward(rs, ready=()):
+        coarse = down(ready)
         gos = [get_lanes(go_ref, r * 16, 16).astype(bf16) for r in rs]
         gts = [dot(wht_ref[...], go) for go in gos]
         head, gsum, sums, kept = 0.0, 0.0, [0.0] * crops, []
@@ -628,28 +633,26 @@
             put_rows(g3_ref, (r + 2) * 256, jnp.concatenate(parts, axis=0))
         for r, gt in zip(rs, kept):
             put_rows(h3_ref, (r + 1) * 128, gt)
+        for k, b in zip(ready, coarse):
+            put_rows(gc_ref, k * 64, b)
         head_ref[...] += head
         go_sum[...] += gsum
         for c in range(crops):
             sg_sum[c] += sums[c]
 
-    repeat_rows(rows, 4, backward)
+    backward(range(BACK))
+    repeat_rows(rows - BACK, BACK, lambda rs: backward(rs, [r - BACK for r in rs]), BACK)
     for c in range(crops):
         sg_ref[c : c + 1, :] = lane_sums(sg_sum[c])[0:1]
     sums_ref[3:4, 0:16] = lane_sums(go_sum[...])[0:1]
     sg_copies = share(tiles, "tile", sg_ref, sg_got, s2_send, s2_recv)
-
-    def down(ks):
-        both = [dot(wd3_ref[...], rows_of(g3_ref, k * 256 + 128, 512)) for k in ks]
-        for k, b in zip(ks, both):
-            put_rows(gc_ref, k * 64, b[0:64] + b[64:128])
-
-    down([0, 1])
+    rest = list(range(rows - BACK, rows + 2))
+    for k, b in zip(rest, down(rest)):
+        put_rows(gc_ref, k * 64, b)
+
     rim_lo[...] = gc_ref[0:128, :].astype(bf16)
-    down([rows, rows + 1])
     rim_hi[...] = gc_ref[64 * rows : 64 * rows + 128, :].astype(bf16)
     finish_rims = swap_edges(tiles, [(rim_lo, rim_hi, rim_up, rim_dn)], rim_send, rim_recv)
-    repeat_rows(rows - 2, 7, down, 2)
 
     def weights_three(ks):
         d3 = 0.0
@@ -696,7 +699,7 @@
     g2_ref = g3_ref
 
     def masked(ks, extras=None):
-        sums = 0.0
+        sums, d2 = 0.0, 0.0
         for j, k in enumerate(ks):
             coarse = rows_of(gc_ref, k * 64, 64)
             if extras is not None:
@@ -706,8 +709,10 @@
             g = gb.astype(f32)
             if extras is None or 0 < j < 3:
                 sums = sums + fold_lanes(g)
+                d2 = d2 + dot_nt(rows_of(x2_ref, (k + 1) * 96, 288), gb)
             put_rows(g2_ref, k * 192, three_columns(gb, g, crops))
         g2_sum[...] += sums
+        d2_ref[...] += d2
 
     repeat_rows(rows - 2, 7, masked, 2)
     finish_rims()
@@ -718,17 +723,10 @@
 
     pay_b[160:161, 0:64] = lane_sums(g2_sum[...])[0:1]
 
-    def weights_two(rs):
-        d2 = 0.0
-        for r in rs:
-            d2 = d2 + dot_nt(rows_of(x2_ref, (r + 2) * 96, 288), rows_of(g2_ref, (r + 1) * 192 + 64, 64))
-        d2_ref[...] += d2
-
-    repeat_rows(rows, 8, weights_two)
-    reduce_a.across()
     rest = jnp.concatenate([d2_ref[160:288, :], jnp.zeros((32, 64), f32)], axis=0)
     pay_b[0:160, :] = jnp.concatenate([d2_ref[0:160, :], rest], axis=1)
     reduce_b.scatter()
+    reduce_a.across()
 
     def last_back(rs):
         gps = [dot(wd2_ref[...], rows_of(g2_ref, r * 192, 576)) for r in rs]
@@ -741,12 +739,12 @@
             d1 = d1 + dot_nt(gb, jnp.concatenate([rows_of(y_ref, (r + 3) * 16, 32), ones_ref[...]], axis=0))
         d1_ref[...] += d1
 
-    half, quarter = rows // 2, rows // 4
-    repeat_rows(half, 4, last_back)
+    quarter = rows // 4
+    repeat_rows(rows // 2, 4, last_back)
     reduce_a.gather(full_a)
-    repeat_rows(quarter, 4, last_back, half)
+    repeat_rows(quarter, 4, last_back, rows // 2)
     reduce_b.across()
-    repeat_rows(rows - half - quarter, 4, last_back, half + quarter)
+    repeat_rows(rows - rows // 2 - quarter, 4, last_back, rows // 2 + quarter)
     d1 = jnp.transpose(jnp.concatenate([d1_ref[...], jnp.zeros((128, 80), f32)], axis=1))
     total = jnp.zeros((32, 128), f32)
     for p in range(4):

time: 60.3 us -> 58.6 us (0.972)
  Pallas kernels: 58.2 us -> 56.6 us
    pallas_call x1, Pallas kernels: 56.8 us -> 55.2 us  [on_device(): pl.pallas_call(lambda *refs: step_kernel(tiles, images_count, grad_scale,...]
where the time goes in v8:
time: 58.6 us; the launch traced here: 58.4 us
  Pallas kernels  56.6 us (97%)
  between operations  1.78 us (3%)
    pallas_call x1, Pallas kernels, on_device(): pl.pallas_call(lambda *refs: step_kernel(tiles, images_count, grad_scale,...  55.2 us
    pallas_call x1, Pallas kernels, on_device(): pl.pallas_call(lambda *refs: update_kernel(float(pixel_count), parts[0] *...  1.39 us

profile of v8, /device:TPU:0, one launch (start us, length us, event | category | flops | bytes accessed | tf_op | source)
XLA Modules:
  0.0 58.4 jit_solution(3970133465154190776)
XLA Ops:
  1.3 0.0 copy-start
  1.3 0.0 copy-start.1
  1.3 0.0 copy-start.2
  1.3 0.0 copy-start.3
  1.5 55.2 %step.1.refs_1_ = f32[392,128]{1,0:T(8,128)S(1)} custom-call(s32[2]{0:T(128)} %refs_0_.2, bf16[2,2,32,1024]{3,2,1,0:T(8,128)(2,1)} %refs_1_.1, s32[2,2,32,1024]{3,2,1,0:T(8,128)} %refs_2_.2, s32[2,32,1024]{2,1,0:T(8,128)} %refs_3_.2, f32[3,3,2,32]{3,2,1,0:T(2,128)} %refs_2_.3, f32[3,3,32,64]{3,2,1,0:T(8,128)} %refs_5_.3, f32[3,3,32,64]{3,2,1,0:T(8,128)} %bitcast.18, ...), custom_call_target="tpu_custom_call" | custom-call | tf_op jit(solution)/shard_map/step/pallas_call | solution.py:880
  56.7 0.0 copy-done
  56.7 0.0 copy-done.1
  56.7 0.0 copy-done.2
  56.7 0.0 copy-done.3
  56.7 0.0 copy-done.4
  56.7 0.0 copy-done.5
  56.7 0.0 copy-done.6
  56.7 0.0 copy-done.7
  56.7 0.0 copy-done.8
  56.8 0.0 copy-done.9
  56.8 0.0 copy-done.10
  56.8 0.0 copy-done.11
  56.8 0.0 copy-done.12
  56.8 0.0 copy-done.13
  56.8 0.0 copy-done.14
  56.8 0.0 copy-done.15
  56.8 0.0 copy-done.16
  56.8 0.0 copy-done.17
  56.8 1.4 %update.1 = (f32[3,3,2,32]{3,2,1,0:T(2,128)}, f32[3,3,2,32]{3,2,1,0:T(2,128)}, f32[3,3,2,32]{3,2,1,0:T(2,128)}, f32[3,3,32,64]{3,2,1,0:T(8,128)}, f32[3,3,32,64]...) custom-call(s32[1]{0:T(128)S(6)} %copy.42.refs_0_, ...), custom_call_target="tpu_custom_call" | custom-call | tf_op jit(solution)/shard_map/update/pallas_call | solution.py:918
  (14 shorter events, 0.0 us)
Async XLA Ops:
  1.3 55.4 %copy-start = (f32[3,3,32,64]{3,2,1,0:T(8,128)S(1)}, f32[3,3,32,64]{3,2,1,0:T(8,128)}, u32[]{:S(2)}) copy-start(f32[3,3,32,64]{3,2,1,0:T(8,128)} %refs_5_.3) | copy-start | bytes 221188
  1.3 55.4 %copy-start.1 = (f32[3,3,64,32]{2,3,1,0:T(8,128)S(1)}, f32[3,3,64,32]{2,3,1,0:T(8,128)}, u32[]{:S(2)}) copy-start(f32[3,3,64,32]{2,3,1,0:T(8,128)} %param.34) | copy-start | bytes 221188
  1.3 55.4 %copy-start.2 = (f32[3,3,32,64]{3,2,1,0:T(8,128)S(1)}, f32[3,3,32,64]{3,2,1,0:T(8,128)}, u32[]{:S(2)}) copy-start(f32[3,3,32,64]{3,2,1,0:T(8,128)} %refs_6_.1) | copy-start | bytes 221188
  1.3 55.4 %copy-start.3 = (f32[3,3,32,64]{3,2,1,0:T(8,128)S(1)}, f32[3,3,32,64]{3,2,1,0:T(8,128)}, u32[]{:S(2)}) copy-start(f32[3,3,32,64]{3,2,1,0:T(8,128)} %refs_7_.1) | copy-start | bytes 221188
  1.4 55.4 %copy-start.4 = (f32[3,3,64,32]{2,3,1,0:T(8,128)S(1)}, f32[3,3,64,32]{2,3,1,0:T(8,128)}, u32[]{:S(2)}) copy-start(f32[3,3,64,32]{2,3,1,0:T(8,128)} %param.35) | copy-start | bytes 221188
  1.4 55.4 %copy-start.5 = (f32[3,3,64,32]{2,3,1,0:T(8,128)S(1)}, f32[3,3,64,32]{2,3,1,0:T(8,128)}, u32[]{:S(2)}) copy-start(f32[3,3,64,32]{2,3,1,0:T(8,128)} %param.36) | copy-start | bytes 221188
  1.4 55.4 %copy-start.6 = (f32[64,32]{0,1:T(8,128)S(1)}, f32[64,32]{0,1:T(8,128)}, u32[]{:S(2)}) copy-start(f32[64,32]{0,1:T(8,128)} %param.37) | copy-start | bytes 24580
  1.4 55.4 %copy-start.7 = (f32[3,3,2,32]{3,2,1,0:T(2,128)S(1)}, f32[3,3,2,32]{3,2,1,0:T(2,128)}, u32[]{:S(2)}) copy-start(f32[3,3,2,32]{3,2,1,0:T(2,128)} %refs_2_.3) | copy-start | bytes 6916
  1.4 55.4 %copy-start.8 = (f32[64,32]{0,1:T(8,128)S(1)}, f32[64,32]{0,1:T(8,128)}, u32[]{:S(2)}) copy-start(f32[64,32]{0,1:T(8,128)} %param.38) | copy-start | bytes 24580
  1.4 55.4 %copy-start.9 = (f32[64,32]{0,1:T(8,128)S(1)}, f32[64,32]{0,1:T(8,128)}, u32[]{:S(2)}) copy-start(f32[64,32]{0,1:T(8,128)} %param.39) | copy-start | bytes 24580
  1.4 55.4 %copy-start.10 = (f32[3,3,2,32]{3,2,1,0:T(2,128)S(1)}, f32[3,3,2,32]{3,2,1,0:T(2,128)}, u32[]{:S(2)}) copy-start(f32[3,3,2,32]{3,2,1,0:T(2,128)} %refs_3_.3) | copy-start | bytes 6916
  1.4 55.4 %copy-start.11 = (f32[3,3,2,32]{3,2,1,0:T(2,128)S(1)}, f32[3,3,2,32]{3,2,1,0:T(2,128)}, u32[]{:S(2)}) copy-start(f32[3,3,2,32]{3,2,1,0:T(2,128)} %refs_4_.3) | copy-start | bytes 6916
  1.4 55.4 %copy-start.12 = (f32[32,3]{0,1:T(4,128)S(1)}, f32[32,3]{0,1:T(4,128)}, u32[]{:S(2)}) copy-start(f32[32,3]{0,1:T(4,128)} %param.40) | copy-start | bytes 1156
  1.4 55.4 %copy-start.13 = (f32[163]{0:T(256)S(1)}, f32[163]{0:T(256)}, u32[]{:S(2)}) copy-start(f32[163]{0:T(256)} %refs_17_.1) | copy-start | bytes 1960
  1.5 55.4 %copy-start.14 = (f32[32,3]{0,1:T(4,128)S(1)}, f32[32,3]{0,1:T(4,128)}, u32[]{:S(2)}) copy-start(f32[32,3]{0,1:T(4,128)} %param.41) | copy-start | bytes 1156
  1.5 55.4 %copy-start.15 = (f32[32,3]{0,1:T(4,128)S(1)}, f32[32,3]{0,1:T(4,128)}, u32[]{:S(2)}) copy-start(f32[32,3]{0,1:T(4,128)} %param.42) | copy-start | bytes 1156
  1.5 55.4 %copy-start.16 = (f32[163]{0:T(256)S(1)}, f32[163]{0:T(256)}, u32[]{:S(2)}) copy-start(f32[163]{0:T(256)} %refs_18_.1) | copy-start | bytes 1960
  1.5 55.4 %copy-start.17 = (f32[163]{0:T(256)S(1)}, f32[163]{0:T(256)}, u32[]{:S(2)}) copy-start(f32[163]{0:T(256)} %refs_19_.1) | copy-start | bytes 1960

commit v9 on v8

--- a/solution.py
+++ b/solution.py
@@ -347,7 +347,7 @@
     style_sum, sg_sum, go_sum, g2_sum,
     pay_a, got_a, own_a, met_a, full_a, pay_b, got_b, own_b, met_b, full_b,
     pay_c, got_c, own_c, met_c,
-    load_sems, halo_send, halo_recv, s1_send, s1_recv, s2_send, s2_recv, rim_send, rim_recv,
+    load_sems, halo_send, halo_recv, flow_send, flow_recv, s1_send, s1_recv, s2_send, s2_recv, rim_send, rim_recv,
     *sems,
 ):
     pre_ref = gc_ref
@@ -368,13 +368,14 @@
     ones_ref[...] = jnp.ones_like(ones_ref)
     arrived()
     last = x_ref.shape[2] - HALO
-    finish_halo = swap_edges(
-        tiles,
-        [
-            (ref.at[:, :, pl.ds(0, HALO), :], ref.at[:, :, pl.ds(last, HALO), :], lo, hi)
-            for ref, lo, hi in ((x_hbm, x_lo, x_hi), (t_hbm, t_lo, t_hi))
-        ],
-        halo_send, halo_recv,
+    finish_halo, finish_targets = (
+        swap_edges(
+            tiles, [(ref.at[:, :, pl.ds(0, HALO), :], ref.at[:, :, pl.ds(last, HALO), :], lo, hi)], send, recv
+        )
+        for ref, lo, hi, send, recv in (
+            (x_hbm, x_lo, x_hi, halo_send, halo_recv),
+            (t_hbm, t_lo, t_hi, flow_send, flow_recv),
+        )
     )
     for load in loads[0:4]:
         load.wait()
@@ -495,6 +496,7 @@
     outside = (fine < 0) | (fine >= height)
     known = (part < 2) | ((part == 2) & jnp.logical_not(outside))
     perm_t = jnp.where((ci == (ri % 2) * t_rows + source) & known, 1.0, 0.0).astype(bf16)
+    finish_targets()
     even, odd = both_columns(target_rows)
     put_lanes(t_out, 0, dot(perm_t, jnp.concatenate([even, odd], axis=0).astype(bf16)))
     later_tables(k2_ref, k3_ref, kh_ref, bias_ref, w3_ref, wd3_ref, wd2_ref, wh_ref, wht_ref, b3_ref, bh_ref)
@@ -714,7 +716,7 @@
         g2_sum[...] += sums
         d2_ref[...] += d2
 
-    repeat_rows(rows - 2, 7, masked, 2)
+    repeat_rows(rows - 2, 14, masked, 2)
     finish_rims()
     up = jnp.where(edge[0] < 0, rim_up[...].astype(f32), 0.0)
     dn = jnp.where(edge[1] > rows, rim_dn[...].astype(f32), 0.0)
@@ -902,7 +904,7 @@
         + block_bufs(parts[0])
         + block_bufs(parts[1])
         + [buf((small, 128), f32), buf((tiles, small, 128), f32), buf((small, 128), f32), buf((images_count, small, 128), f32)]
-        + [DMA((9,)), DMA((4,)), DMA((4,)), DMA((tiles,)), DMA((tiles,)), DMA((tiles,)), DMA((tiles,)), DMA((2,)), DMA((2,))]
+        + [DMA((9,)), DMA((2,)), DMA((2,)), DMA((2,)), DMA((2,)), DMA((tiles,)), DMA((tiles,)), DMA((tiles,)), DMA((tiles,)), DMA((2,)), DMA((2,))]
         + block_sems * 2
         + [DMA((tiles,)), DMA((tiles,)), DMA((images_count,)), DMA((images_count,))],
         compiler_params=pltpu.CompilerParams(collective_id=1, has_side_effects=True, vmem_limit_bytes=60 * 2**20),

time: 58.6 us -> 57.3 us (0.978)
  Pallas kernels: 56.6 us -> 55.3 us
    pallas_call x1, Pallas kernels: 55.2 us -> 53.9 us  [on_device(): pl.pallas_call(lambda *refs: step_kernel(tiles, images_count, grad_scale,...]
where the time goes in v9:
time: 57.3 us; the launch traced here: 57.1 us
  Pallas kernels  55.3 us (97%)
  between operations  1.78 us (3%)
    pallas_call x1, Pallas kernels, on_device(): pl.pallas_call(lambda *refs: step_kernel(tiles, images_count, grad_scale,...  53.9 us
    pallas_call x1, Pallas kernels, on_device(): pl.pallas_call(lambda *refs: update_kernel(float(pixel_count), parts[0] *...  1.39 us

profile of v9, /device:TPU:0, one launch (start us, length us, event | category | flops | bytes accessed | tf_op | source)
XLA Modules:
  0.0 57.1 jit_solution(7167137900976477310)
XLA Ops:
  1.3 0.0 copy-start
  1.3 0.0 copy-start.1
  1.3 0.0 copy-start.2
  1.3 0.0 copy-start.3
  1.4 0.0 copy-start.4
  1.4 0.0 copy-start.5
  1.4 0.0 copy-start.6
  1.4 0.0 copy-start.7
  1.4 0.0 copy-start.8
  1.4 0.0 copy-start.9
  1.4 0.0 copy-start.10
  1.4 0.0 copy-start.11
  1.4 0.0 copy-start.12
  1.4 0.0 copy-start.13
  1.5 0.0 copy-start.14
  1.5 0.0 copy-start.15
  1.5 0.0 copy-start.16
  1.5 0.0 copy-start.17
  1.5 53.9 %step.1.refs_1_ = f32[392,128]{1,0:T(8,128)S(1)} custom-call(s32[2]{0:T(128)} %refs_0_.2, bf16[2,2,32,1024]{3,2,1,0:T(8,128)(2,1)} %refs_1_.1, s32[2,2,32,1024]{3,2,1,0:T(8,128)} %refs_2_.2, s32[2,32,1024]{2,1,0:T(8,128)} %refs_3_.2, f32[3,3,2,32]{3,2,1,0:T(2,128)} %refs_2_.3, f32[3,3,32,64]{3,2,1,0:T(8,128)} %refs_5_.3, f32[3,3,32,64]{3,2,1,0:T(8,128)} %bitcast.18, ...), custom_call_target="tpu_custom_call" | custom-call | tf_op jit(solution)/shard_map/step/pallas_call | solution.py:882
  55.4 0.0 copy-done
  55.4 0.0 copy-done.1
  55.4 0.0 copy-done.2
  55.4 0.0 copy-done.3
  55.6 1.4 %update.1 = (f32[3,3,2,32]{3,2,1,0:T(2,128)}, f32[3,3,2,32]{3,2,1,0:T(2,128)}, f32[3,3,2,32]{3,2,1,0:T(2,128)}, f32[3,3,32,64]{3,2,1,0:T(8,128)}, f32[3,3,32,64]...) custom-call(s32[1]{0:T(128)S(6)} %copy.42.refs_0_, ...), custom_call_target="tpu_custom_call" | custom-call | tf_op jit(solution)/shard_map/update/pallas_call | solution.py:920
  (14 shorter events, 0.0 us)
Async XLA Ops:
  1.3 54.1 %copy-start = (f32[3,3,32,64]{3,2,1,0:T(8,128)S(1)}, f32[3,3,32,64]{3,2,1,0:T(8,128)}, u32[]{:S(2)}) copy-start(f32[3,3,32,64]{3,2,1,0:T(8,128)} %refs_5_.3) | copy-start | bytes 221188
  1.3 54.1 %copy-start.1 = (f32[3,3,64,32]{2,3,1,0:T(8,128)S(1)}, f32[3,3,64,32]{2,3,1,0:T(8,128)}, u32[]{:S(2)}) copy-start(f32[3,3,64,32]{2,3,1,0:T(8,128)} %param.34) | copy-start | bytes 221188
  1.3 54.1 %copy-start.2 = (f32[3,3,32,64]{3,2,1,0:T(8,128)S(1)}, f32[3,3,32,64]{3,2,1,0:T(8,128)}, u32[]{:S(2)}) copy-start(f32[3,3,32,64]{3,2,1,0:T(8,128)} %refs_6_.1) | copy-start | bytes 221188
  1.3 54.1 %copy-start.3 = (f32[3,3,32,64]{3,2,1,0:T(8,128)S(1)}, f32[3,3,32,64]{3,2,1,0:T(8,128)}, u32[]{:S(2)}) copy-start(f32[3,3,32,64]{3,2,1,0:T(8,128)} %refs_7_.1) | copy-start | bytes 221188
  1.4 54.1 %copy-start.4 = (f32[3,3,64,32]{2,3,1,0:T(8,128)S(1)}, f32[3,3,64,32]{2,3,1,0:T(8,128)}, u32[]{:S(2)}) copy-start(f32[3,3,64,32]{2,3,1,0:T(8,128)} %param.35) | copy-start | bytes 221188
  1.4 54.1 %copy-start.5 = (f32[3,3,64,32]{2,3,1,0:T(8,128)S(1)}, f32[3,3,64,32]{2,3,1,0:T(8,128)}, u32[]{:S(2)}) copy-start(f32[3,3,64,32]{2,3,1,0:T(8,128)} %param.36) | copy-start | bytes 221188
  1.4 54.1 %copy-start.6 = (f32[64,32]{0,1:T(8,128)S(1)}, f32[64,32]{0,1:T(8,128)}, u32[]{:S(2)}) copy-start(f32[64,32]{0,1:T(8,128)} %param.37) | copy-start | bytes 24580
  1.4 54.1 %copy-start.7 = (f32[3,3,2,32]{3,2,1,0:T(2,128)S(1)}, f32[3,3,2,32]{3,2,1,0:T(2,128)}, u32[]{:S(2)}) copy-start(f32[3,3,2,32]{3,2,1,0:T(2,128)} %refs_2_.3) | copy-start | bytes 6916
  1.4 54.1 %copy-start.8 = (f32[64,32]{0,1:T(8,128)S(1)}, f32[64,32]{0,1:T(8,128)}, u32[]{:S(2)}) copy-start(f32[64,32]{0,1:T(8,128)} %param.38) | copy-start | bytes 24580
  1.4 54.1 %copy-start.9 = (f32[64,32]{0,1:T(8,128)S(1)}, f32[64,32]{0,1:T(8,128)}, u32[]{:S(2)}) copy-start(f32[64,32]{0,1:T(8,128)} %param.39) | copy-start | bytes 24580
  1.4 54.1 %copy-start.10 = (f32[3,3,2,32]{3,2,1,0:T(2,128)S(1)}, f32[3,3,2,32]{3,2,1,0:T(2,128)}, u32[]{:S(2)}) copy-start(f32[3,3,2,32]{3,2,1,0:T(2,128)} %refs_3_.3) | copy-start | bytes 6916
  1.4 54.1 %copy-start.11 = (f32[3,3,2,32]{3,2,1,0:T(2,128)S(1)}, f32[3,3,2,32]{3,2,1,0:T(2,128)}, u32[]{:S(2)}) copy-start(f32[3,3,2,32]{3,2,1,0:T(2,128)} %refs_4_.3) | copy-start | bytes 6916
  1.4 54.1 %copy-start.12 = (f32[32,3]{0,1:T(4,128)S(1)}, f32[32,3]{0,1:T(4,128)}, u32[]{:S(2)}) copy-start(f32[32,3]{0,1:T(4,128)} %param.40) | copy-start | bytes 1156
  1.4 54.1 %copy-start.13 = (f32[163]{0:T(256)S(1)}, f32[163]{0:T(256)}, u32[]{:S(2)}) copy-start(f32[163]{0:T(256)} %refs_17_.1) | copy-start | bytes 1960
  1.5 54.1 %copy-start.14 = (f32[32,3]{0,1:T(4,128)S(1)}, f32[32,3]{0,1:T(4,128)}, u32[]{:S(2)}) copy-start(f32[32,3]{0,1:T(4,128)} %param.41) | copy-start | bytes 1156
  1.5 54.1 %copy-start.15 = (f32[32,3]{0,1:T(4,128)S(1)}, f32[32,3]{0,1:T(4,128)}, u32[]{:S(2)}) copy-start(f32[32,3]{0,1:T(4,128)} %param.42) | copy-start | bytes 1156
  1.5 54.1 %copy-start.16 = (f32[163]{0:T(256)S(1)}, f32[163]{0:T(256)}, u32[]{:S(2)}) copy-start(f32[163]{0:T(256)} %refs_18_.1) | copy-start | bytes 1960
  1.5 54.1 %copy-start.17 = (f32[163]{0:T(256)S(1)}, f32[163]{0:T(256)}, u32[]{:S(2)}) copy-start(f32[163]{0:T(256)} %refs_19_.1) | copy-start | bytes 1960
